TPU v7x, 128 devices: a whole 4x4x4 slice. The times are simulated.
128 devices in a mesh: aux: 8 (over y, core), virt: 16 (over z, x).
Axes of the slice: x: 4, y: 4, z: 4, core: 2. Of those that a mesh axis runs over, the one named last changes fastest.
Arguments:
- integrals: float32 [1024, 6, 2560], P('virt', None, 'aux'), may hold values from -1.25 to 1.25
- metric_root: float32 [2560, 2560], P(None, 'aux'), may hold values from -0.125 to 0.125
- occ_energy: float32 [256], replicated, may hold values from -1.5 to -0.3
- virt_energy: float32 [1024], replicated, may hold values from 0.2 to 3
- batch_index: int32 [6], replicated, may hold values from 0 to 255, as said below
- virt_order: int32 [1024], replicated, may hold values from 0 to 1023, each once
Outputs:
- density: float32 [1024, 6, 2560], P('virt', None, 'aux')
Inputs may be any that keep to these rules, and one draw needn't show every extreme that they name: `batch_index`: 6 distinct occupied orbital numbers, among them 0 and 255. `virt_order`: each number appears once.
All inputs are finite; a program needn't handle non-finite values.
Results may differ from a plain program's by a relative error of at most 0.000057.
Values sent between devices are 32-bit elements; how exact they have to be, the bound alone decides.
No kernel may reach another device: no remote copies, remote signals or barrier semaphores. Data moves between devices by JAX's collectives and lax.ppermute only.
A program may use at most 128 MiB of HBM per device.

v0:
```python
import jax
import jax.numpy as jnp
import numpy as np
from jax import lax
from jax.experimental import pallas as pl
from jax.experimental.pallas import tpu as pltpu
from jax.sharding import PartitionSpec as P


F32 = jnp.float32
BF16 = jnp.bfloat16
OCC = 6
VL = 64
QL = 320
QH = 1280
QT = QH // 128


def plane(dz, dx):
    return [(z * 4 + x, (z + dz) % 4 * 4 + (x + dx) % 4) for z in range(4) for x in range(4)]


def column(place, swap):
    return [(y * 2 + c, place(y) * 2 + (c ^ swap)) for y in range(4) for c in range(2)]


XP, XM, X2 = plane(0, 1), plane(0, -1), plane(0, 2)
ZP, ZM, Z2 = plane(1, 0), plane(-1, 0), plane(2, 0)
YA = column(lambda y: y ^ 1, 0)
YB = column(lambda y: 3 - y, 0)
CORE = column(lambda y: y, 1)


def split(value):
    high = value.astype(BF16)
    return high, (value - high.astype(F32)).astype(BF16)


def product(left, right, dims):
    left_high, left_low = left
    right_high, right_low = right

    def one(a, b):
        return lax.dot_general(a, b, (dims, ((), ())), preferred_element_type=F32)

    return one(left_high, right_low) + one(left_low, right_high) + one(left_high, right_high)


def half_turn(value):
    return pltpu.roll(value, 64, 1)


def lanes(rows):
    return lax.broadcasted_iota(jnp.int32, (rows, 128), 1) < 64


def fitted_kernel(places, integrals, metric, sent, kept, right, full):
    core = places[0]
    for y in range(4):
        start = pl.multiple_of(640 * y + 384 * core, 128)
        right[:, 256 * y : 256 * y + 256] = metric[:, pl.ds(start, 256)]
    low = lanes(QL)
    for p in range(2):
        first = metric[:, 1280 * p + 256 : 1280 * p + 384]
        second = metric[:, 1280 * p + 896 : 1280 * p + 1024]
        even = jnp.where(low, first, half_turn(second))
        odd = jnp.where(low, half_turn(first), second)
        right[:, 1024 + 128 * p : 1152 + 128 * p] = jnp.where(core == 0, even, odd)
    left = integrals[...].reshape(OCC * VL, QL)
    value = product(split(left), split(right[...]), ((1,), (0,)))
    full[...] = value.reshape(OCC, 4, 2, 8, QH)
    y_a, y_b, y_far, y_own = places[1], places[2], places[3], places[4]
    for target, half, slot, y in (
        (sent, 0, 0, y_a), (sent, 0, 1, y_far), (sent, 1, 0, y_b), (sent, 1, 1, y_far),
        (kept, 0, 0, y_own), (kept, 0, 1, y_b), (kept, 1, 0, y_own), (kept, 1, 1, y_a),
    ):
        for i in range(OCC):
            for q in range(QT):
                target[half, slot, i, q] = full[i, y, half, :, 128 * q : 128 * q + 128]


def fitted_part(places, integrals, metric):
    piece = jax.ShapeDtypeStruct((2, 2, OCC, QT, 8, 128), F32)
    return pl.pallas_call(
        fitted_kernel,
        out_shape=(piece, piece),
        in_specs=[
            pl.BlockSpec(memory_space=pltpu.SMEM),
            pl.BlockSpec(memory_space=pltpu.VMEM),
            pl.BlockSpec(memory_space=pltpu.VMEM),
        ],
        out_specs=(pl.BlockSpec(memory_space=pltpu.VMEM),) * 2,
        scratch_shapes=[pltpu.VMEM((QL, QH), F32), pltpu.VMEM((OCC, 4, 2, 8, QH), F32)],
        compiler_params=settings(20),
        cost_estimate=cost(FLOPS // 3),
    )(places, integrals, metric)


def store_split(high, low, row, q, first, second):
    value = jnp.concatenate([first, second], axis=0)
    upper, lower = split(value)
    high[row : row + 16, 128 * q : 128 * q + 128] = upper
    low[row : row + 16, 128 * q : 128 * q + 128] = lower


VMEM_SPEC = pl.BlockSpec(memory_space=pltpu.VMEM)
SMEM_SPEC = pl.BlockSpec(memory_space=pltpu.SMEM)
PARTS = (jax.ShapeDtypeStruct((OCC * VL, QH), BF16),) * 2
FLOPS = 2 * 3 * (OCC * VL) ** 2 * QH


def settings(mebibytes):
    return pltpu.CompilerParams(vmem_limit_bytes=mebibytes * 2**20)


def cost(flops):
    return pl.CostEstimate(flops=flops, bytes_accessed=4 * 2**20, transcendentals=0)


def rows_kernel(own, near_a, near_b, far_0, far_1, high, low):
    for i in range(OCC):
        for k, ref in enumerate((own, near_a, near_b, None)):
            for q in range(QT):
                first, second = (far_0[i, q], far_1[i, q]) if ref is None else (ref[0, i, q], ref[1, i, q])
                store_split(high, low, (i * 4 + k) * 16, q, first, second)


def rows_part(*rows):
    return pl.pallas_call(
        rows_kernel,
        out_shape=PARTS,
        in_specs=[VMEM_SPEC] * 5,
        out_specs=(VMEM_SPEC,) * 2,
        compiler_params=settings(12),
        cost_estimate=cost(FLOPS // 4),
        name="rows",
    )(*rows)


def pair_kernel(left_high, left_low, *refs):
    cols = refs[:4]
    result, high, low = refs[4:]
    for i in range(OCC):
        for k, ref in enumerate(cols):
            for q in range(QT):
                store_split(high, low, (i * 4 + k) * 16, q, ref[0, i, q], ref[1, i, q])
    left = left_high[...], left_low[...]
    result[...] = product(left, (high[...], low[...]), ((1,), (1,)))


def pair_part(left, cols):
    return pl.pallas_call(
        pair_kernel,
        out_shape=(jax.ShapeDtypeStruct((OCC * VL, OCC * VL), F32), *PARTS),
        in_specs=[VMEM_SPEC] * 6,
        out_specs=(VMEM_SPEC,) * 3,
        compiler_params=settings(16),
        cost_estimate=cost(FLOPS),
    )(*left, *cols)


def amplitudes(pair, row_term, col_term):
    low = lanes(VL)
    pieces = []
    for i in range(OCC):
        at = 128 * (i // 2)
        swapped = []
        for t in range(OCC // 2):
            first = pair[2 * t * VL : 2 * t * VL + VL, at : at + 128]
            second = pair[(2 * t + 1) * VL : (2 * t + 2) * VL, at : at + 128]
            if i % 2 == 0:
                second = half_turn(second)
            else:
                first = half_turn(first)
            swapped.append(jnp.where(low, first, second))
        direct = pair[VL * i : VL * i + VL, :]
        levels = row_term[VL * i : VL * i + VL, :] + col_term
        pieces.append((2.0 * direct - jnp.concatenate(swapped, axis=1)) / levels)
    return jnp.concatenate(pieces, axis=0)


def density_term(own, other, row_term, col_term, high, low):
    amplitude = amplitudes(own[...] + other[...], row_term[...], col_term[...])
    return product(split(amplitude), (high[...], low[...]), ((1,), (0,)))


def density_first_kernel(*refs):
    refs[-1][...] = density_term(*refs[:-1])


def density_next_kernel(*refs):
    refs[-1][...] = refs[-2][...] + density_term(*refs[:-2])


def density_part(inputs, before):
    args = inputs if before is None else (*inputs, before)
    return pl.pallas_call(
        density_first_kernel if before is None else density_next_kernel,
        out_shape=jax.ShapeDtypeStruct((OCC * VL, QH), F32),
        in_specs=[VMEM_SPEC] * len(args),
        out_specs=VMEM_SPEC,
        compiler_params=settings(16),
        cost_estimate=cost(FLOPS),
    )(*args)


def density_last_kernel(places, *refs):
    before, sent_0, sent_1, kept_0, kept_1, whole = refs[6:]
    term = before[...] + density_term(*refs[:6])
    order = (places[4], places[1], places[2], places[3])
    for q in range(QT):
        for i in range(OCC):
            for k in range(4):
                row = (i * 4 + k) * 16
                whole[q, i, order[k]] = term[row : row + 16, 128 * q : 128 * q + 128]
    low = lanes(32)
    for target, start, slots in (
        (sent_0, 0, (1, 3)), (sent_1, 3, (2, 3)), (kept_0, 0, (0, 2)), (kept_1, 3, (0, 1)),
    ):
        for slot, k in enumerate(slots):
            y = order[k]
            for i in range(3):
                for q in range(2):
                    row = (q * 3 + i) * VL
                    target[slot, row : row + VL, :] = whole[2 * y + q, start + i].reshape(VL, 128)
                rest = whole[8 + y // 2, start + i].reshape(VL, 128)
                rest = jnp.where(y % 2 == 1, half_turn(rest), rest)
                row = 6 * VL + 32 * i
                target[slot, row : row + 32, :] = jnp.where(low, rest[:32], half_turn(rest[32:]))


def density_last(places, inputs, before):
    piece = jax.ShapeDtypeStruct((2, 480, 128), F32)
    return pl.pallas_call(
        density_last_kernel,
        out_shape=(piece,) * 4,
        in_specs=[SMEM_SPEC] + [VMEM_SPEC] * 7,
        out_specs=(VMEM_SPEC,) * 4,
        scratch_shapes=[pltpu.VMEM((QT, OCC, 4, 16, 128), F32)],
        compiler_params=settings(18),
        cost_estimate=cost(FLOPS),
    )(places, *inputs, before)


def unpack_kernel(places, kept_0, near_0, last_0, kept_1, near_1, last_1, result):
    low = lanes(VL)
    for half, refs in enumerate(((kept_0, near_0, last_0), (kept_1, near_1, last_1))):
        kept, near, last = refs
        total = kept[0] + near[0] + last[...]
        for i in range(3):
            first = total[i * VL : i * VL + VL]
            second = total[(3 + i) * VL : (4 + i) * VL]
            packed = total[6 * VL + 32 * i : 6 * VL + 32 * i + 32]
            rest = jnp.concatenate([packed, half_turn(packed)], axis=0)
            first_turned, second_turned = half_turn(first), half_turn(second)
            zero = places[0] == 0
            at = half * 3 + i
            result[at, :, 0:128] = jnp.where(zero, first, jnp.where(low, rest, first_turned))
            result[at, :, 128:256] = jnp.where(zero, second, jnp.where(low, first_turned, second_turned))
            result[at, :, 256:320] = jnp.where(zero, rest, second_turned)[:, :64]


def unpack(places, kept_0, near_0, last_0, kept_1, near_1, last_1):
    slot = pl.BlockSpec((1, 480, 128), lambda g: (0, 0, 0))
    whole = pl.BlockSpec((480, 128), lambda g: (0, 0))
    return pl.pallas_call(
        unpack_kernel,
        out_shape=jax.ShapeDtypeStruct((OCC, VL, QL), F32),
        in_specs=[pl.BlockSpec(memory_space=pltpu.SMEM), slot, slot, whole, slot, slot, whole],
        out_specs=pl.BlockSpec((OCC, VL, QL), lambda g: (0, 0, 0)),
        grid=(1,),
        compiler_params=settings(10),
        name="unpack",
    )(places, kept_0, near_0, last_0, kept_1, near_1, last_1)


def pick(table, places):
    at = jnp.arange(table.shape[0], dtype=jnp.int32)
    return jnp.sum(jnp.where(places[:, None] == at[None, :], table[None, :], 0), axis=1)


def on_virt(value, pairs):
    return lax.ppermute(value, "virt", pairs)


def on_aux(value, pairs):
    return lax.ppermute(value, "aux", pairs)


def stacked(first, second):
    return jnp.stack([first, second])


SPOTS = (
    (0, 0, 0), (0, -1, 0), (0, 1, 0), (0, 2, 0), (0, 0, 1), (-1, 0, 1), (1, 0, 1), (2, 0, 1),
    (-1, 0, 0), (-1, -1, 0), (1, 0, 0), (1, -1, 0), (0, -1, 1), (-1, -1, 1), (0, 1, 1), (-1, 1, 1),
    (-1, 1, 0), (-1, 2, 0), (1, 1, 0), (1, 2, 0), (1, -1, 1), (2, -1, 1), (1, 1, 1), (2, 1, 1),
    (2, 0, 0), (2, -1, 0), (2, 1, 0), (2, 2, 0), (0, 2, 1), (-1, 2, 1), (1, 2, 1), (2, 2, 1),
)


def spread(values):
    return jnp.asarray(np.repeat(np.asarray(values, np.int32), 8))


def energy_terms(y, z, x, near, occ_energy, virt_energy, batch_index, virt_order):
    eight = jnp.asarray(np.tile(np.arange(8, dtype=np.int32), 40))
    zeros = [0] * 8
    step_z = spread(zeros + [s[0] for s in SPOTS])
    step_x = spread(zeros + [s[1] for s in SPOTS])
    half = spread([0, 1] * 4 + [s[2] for s in SPOTS])
    turn = spread([0, 0, 1, 1, 2, 2, 3, 3] + [0] * 32)
    chip = jnp.where(turn == 0, y, jnp.where(turn == 1, near[0], jnp.where(turn == 2, near[1], near[2])))
    spots = (((z + step_z) & 3) * 4 + ((x + step_x) & 3)) * VL + chip * 16 + half * 8 + eight
    levels = pick(virt_energy, pick(virt_order, spots))
    terms = pick(occ_energy, batch_index)[:, None] - levels[None, :]
    row_term = terms[:, :64].reshape(OCC * VL, 1)
    return row_term, [terms[:, 64 * k : 64 * k + 64].reshape(1, OCC * VL) for k in range(1, 5)]


def shards(integrals, metric_root, occ_energy, virt_energy, batch_index, virt_order):
    aux_place = lax.axis_index("aux").astype(jnp.int32)
    virt_place = lax.axis_index("virt").astype(jnp.int32)
    y, core = aux_place // 2, aux_place % 2
    z, x = virt_place // 4, virt_place % 4
    near = [y ^ 1, 3 - y, (y + 2) % 4, y]
    places = jnp.stack([core, *near])
    partner_places = jnp.stack([1 - core, *near])

    values = integrals.transpose(1, 0, 2)
    metric = metric_root.T
    out_sent, out_kept = fitted_part(partner_places, values, metric)
    in_sent = on_aux(out_sent, CORE)
    in_kept = on_aux(out_kept, CORE)
    own_sent, own_kept = fitted_part(places, values, metric)
    sent_0, sent_1 = own_sent[0] + in_sent[0], own_sent[1] + in_sent[1]
    kept_0, kept_1 = own_kept[0] + in_kept[0], own_kept[1] + in_kept[1]
    near_0 = on_aux(sent_0, YA)
    near_1 = on_aux(sent_1, YB)
    row_term, col_terms = energy_terms(y, z, x, near, occ_energy, virt_energy, batch_index, virt_order)
    near_0, near_1, row_term, col_terms = lax.optimization_barrier((near_0, near_1, row_term, col_terms))
    last_0 = on_aux(kept_0[1] + near_0[1], YB)
    last_1 = on_aux(kept_1[1] + near_1[1], YA)
    half_0 = kept_0[0] + near_0[0] + last_0
    half_1 = kept_1[0] + near_1[0] + last_1

    a_m = on_virt(half_0, XP)
    a_p = on_virt(half_0, XM)
    b_m = on_virt(half_1, ZP)
    b_p = on_virt(half_1, ZM)
    own = stacked(half_0, half_1)
    row_a = on_aux(own, YA)
    row_b = on_aux(own, YB)
    a_2 = on_virt(half_0, X2)
    b_2 = on_virt(half_1, Z2)
    far_0 = on_aux(row_a[0], YB)
    far_1 = on_aux(row_b[1], YA)

    u_a, u_b = stacked(half_0, a_m), stacked(half_1, b_m)
    ua_m, ua_p = on_virt(u_a, ZP), on_virt(u_a, ZM)
    ub_m, ub_p = on_virt(u_b, XP), on_virt(u_b, XM)
    w_a, w_b = stacked(a_p, a_2), stacked(b_p, b_2)
    wa_m, wa_p = on_virt(w_a, ZP), on_virt(w_a, ZM)
    wb_m, wb_p = on_virt(w_b, XP), on_virt(w_b, XM)
    ua_2, ub_2 = on_virt(ua_m, ZP), on_virt(ub_m, XP)
    wa_2, wb_2 = on_virt(wa_p, ZM), on_virt(wb_p, XM)

    left = rows_part(own, row_a, row_b, far_0, far_1)
    chunks = (
        (u_a, w_a, u_b, w_b), (ua_m, ua_p, ub_m, ub_p), (wa_m, wa_p, wb_m, wb_p), (ua_2, wa_2, ub_2, wb_2),
    )
    total = None
    for k, cols in enumerate(chunks):
        pair, high, low = pair_part(left, cols)
        other = on_aux(pair, CORE)
        inputs = (pair, other, row_term, col_terms[k], high, low)
        if k < 3:
            total = density_part(inputs, total)
    out_0, out_1, stay_0, stay_1 = density_last(places, inputs, total)
    near_0 = on_aux(out_0, YA)
    near_1 = on_aux(out_1, YB)
    last_0 = on_aux(stay_0[1] + near_0[1], YB)
    last_1 = on_aux(stay_1[1] + near_1[1], YA)
    result = unpack(places, stay_0, near_0, last_0, stay_1, near_1, last_1)
    return result.transpose(1, 0, 2)


def solution(mesh):
    return jax.shard_map(
        shards,
        mesh=mesh,
        in_specs=(P("virt", None, "aux"), P(None, "aux"), P(), P(), P(), P()),
        out_specs=P("virt", None, "aux"),
        check_vma=False,
    )
```

profile of v0, /device:TPU:0, one launch (start us, length us, event | category | flops | bytes accessed | tf_op | source)
XLA Modules:
  0.0 152.8 jit_solution(13526471214134844009)
XLA Ops:
  0.1 1.9 %copy-done = f32[2560,320]{0,1:T(8,128)S(1)} copy-done((f32[2560,320]{0,1:T(8,128)S(1)}, f32[2560,320]{0,1:T(8,128)}, u32[]{:S(2)}) %copy-start) | copy-done | bytes 3276824
  2.0 1.1 copy-done.2
  3.1 3.7 %shard_map.110 = (f32[2,2,6,10,8,128]{5,4,3,2,1,0:T(8,128)}, f32[2,2,6,10,8,128]{5,4,3,2,1,0:T(8,128)}) custom-call(s32[5]{0:T(128)S(1)} %stack.76.places, f32[6,64,320]{2,1,0:T(8,128)S(1)} %bitcast.71, f32[320,2560]{1,0:T(8,128)S(1)} %bitcast.69), custom_call_target="tpu_custom_call" | custom-call | flops 377487360 | bytes 4194304 | tf_op jit(solution)/shard_map/pallas_call | solution.py:84
  7.9 1.1 copy-done.3
  8.9 2.5 %shard_map.109 = (f32[2,2,6,10,8,128]{5,4,3,2,1,0:T(8,128)S(1)}, f32[2,2,6,10,8,128]{5,4,3,2,1,0:T(8,128)S(1)}) custom-call(s32[5]{0:T(128)S(1)} %stack.74.places, f32[6,64,320]{2,1,0:T(8,128)S(1)} %bitcast.72, f32[320,2560]{1,0:T(8,128)S(1)} %bitcast.70), custom_call_target="tpu_custom_call" | custom-call | flops 377487360 | bytes 4194304 | tf_op jit(solution)/shard_map/pallas_call | solution.py:84
  12.0 1.3 fusion
  13.3 1.8 %collective-permute-start.2 = (f32[2,6,10,8,128]{4,3,2,1,0:T(8,128)S(1)}, f32[2,6,10,8,128]{4,3,2,1,0:T(8,128)S(1)}, u32[]{:S(2)}, u32[]{:S(2)}) collective-permute-start(f32[2,6,10,8,128]{4,3,2,1,0:T(8,128)S(1)} %get-tuple-element.66), channel_id=1, source_target_pairs={{0,32},{16,48},{32,0},{48,16},{64,96},{80,112},{96,64},{112,80},{1... | collective-permute-start | bytes 1474568 | tf_op jit(solution)/shard_map/ppermute | solution.py:287
  15.1 2.2 %collective-permute-start.3 = (f32[2,6,10,8,128]{4,3,2,1,0:T(8,128)S(1)}, f32[2,6,10,8,128]{4,3,2,1,0:T(8,128)S(1)}, u32[]{:S(2)}, u32[]{:S(2)}) collective-permute-start(f32[2,6,10,8,128]{4,3,2,1,0:T(8,128)S(1)} %get-tuple-element.65), channel_id=1, source_target_pairs={{0,96},{16,112},{32,64},{48,80},{64,32},{80,48},{96,0},{112,16},{1... | collective-permute-start | bytes 1474568 | tf_op jit(solution)/shard_map/ppermute | solution.py:287
  17.7 1.6 %slice_add_fusion = (f32[1,2,6,10,8,128]{5,4,3,2,1,0:T(8,128)S(1)}, f32[1,2,6,10,8,128]{5,4,3,2,1,0:T(8,128)S(1)}) fusion(f32[2,2,6,10,8,128]{5,4,3,2,1,0:T(8,128)} %collective-permute-done, f32[2,2,6,10,8,128]{5,4,3,2,1,0:T(8,128)} %copy-done.14), kind=kLoop, calls=%fused_computation.6 | loop fusion | flops 245760 | bytes 2949120 | tf_op jit(solution)/shard_map/add | solution.py:337
  19.3 7.2 %collective-permute-done.2 = f32[2,6,10,8,128]{4,3,2,1,0:T(8,128)S(1)} collective-permute-done((f32[2,6,10,8,128]{4,3,2,1,0:T(8,128)S(1)}, f32[2,6,10,8,128]{4,3,2,1,0:T(8,128)S(1)}, u32[]{:S(2)}, u32[]{:S(2)}) %collective-permute-start.2) | collective-permute-done | bytes 491552 | tf_op jit(solution)/shard_map/ppermute | solution.py:287
  26.5 2.6 %collective-permute-done.3 = f32[2,6,10,8,128]{4,3,2,1,0:T(8,128)S(1)} collective-permute-done((f32[2,6,10,8,128]{4,3,2,1,0:T(8,128)S(1)}, f32[2,6,10,8,128]{4,3,2,1,0:T(8,128)S(1)}, u32[]{:S(2)}, u32[]{:S(2)}) %collective-permute-start.3) | collective-permute-done | bytes 491552 | tf_op jit(solution)/shard_map/ppermute | solution.py:287
  29.1 2.3 %collective-permute-start.4 = (f32[6,10,8,128]{3,2,1,0:T(8,128)S(1)}, f32[6,10,8,128]{3,2,1,0:T(8,128)S(1)}, u32[]{:S(2)}, u32[]{:S(2)}) collective-permute-start(f32[6,10,8,128]{3,2,1,0:T(8,128)S(1)} %fusion.10), channel_id=1, source_target_pairs={{0,96},{16,112},{32,64},{48,80},{64,32},{80,48},{96,0},{112,16},{1... | collective-permute-start | bytes 737288 | tf_op jit(solution)/shard_map/ppermute | solution.py:287
  31.5 5.6 %collective-permute-done.4 = f32[6,10,8,128]{3,2,1,0:T(8,128)S(1)} collective-permute-done((f32[6,10,8,128]{3,2,1,0:T(8,128)S(1)}, f32[6,10,8,128]{3,2,1,0:T(8,128)S(1)}, u32[]{:S(2)}, u32[]{:S(2)}) %collective-permute-start.4) | collective-permute-done | bytes 245792 | tf_op jit(solution)/shard_map/ppermute | solution.py:287
  37.2 1.6 %collective-permute-start.10 = (f32[6,10,8,128]{3,2,1,0:T(8,128)S(1)}, f32[6,10,8,128]{3,2,1,0:T(8,128)S(1)}, u32[]{:S(2)}, u32[]{:S(2)}) collective-permute-start(f32[6,10,8,128]{3,2,1,0:T(8,128)S(1)} %fusion.13), channel_id=1, source_target_pairs={{0,1},{1,2},{2,3},{3,0},{4,5},{5,6},{6,7},{7,4},{8,9},{9,10},{10,1... | collective-permute-start | bytes 737288 | tf_op jit(solution)/shard_map/ppermute | solution.py:283
  38.8 2.0 %collective-permute-start.17 = (f32[6,10,8,128]{3,2,1,0:T(8,128)S(1)}, f32[6,10,8,128]{3,2,1,0:T(8,128)S(1)}, u32[]{:S(2)}, u32[]{:S(2)}) collective-permute-start(f32[6,10,8,128]{3,2,1,0:T(8,128)S(1)} %fusion.8), channel_id=1, source_target_pairs={{0,4},{1,5},{2,6},{3,7},{4,8},{5,9},{6,10},{7,11},{8,12},{9,13},{1... | collective-permute-start | bytes 737288 | tf_op jit(solution)/shard_map/ppermute | solution.py:283
  40.8 2.2 %collective-permute-start.20 = (f32[6,10,8,128]{3,2,1,0:T(8,128)S(1)}, f32[6,10,8,128]{3,2,1,0:T(8,128)S(1)}, u32[]{:S(2)}, u32[]{:S(2)}) collective-permute-start(f32[6,10,8,128]{3,2,1,0:T(8,128)S(1)} %fusion.8), channel_id=1, source_target_pairs={{0,12},{1,13},{2,14},{3,15},{4,0},{5,1},{6,2},{7,3},{8,4},{9,5},{1... | collective-permute-start | bytes 737288 | tf_op jit(solution)/shard_map/ppermute | solution.py:283
  43.0 1.8 %collective-permute-start.21 = (f32[6,10,8,128]{3,2,1,0:T(8,128)S(1)}, f32[6,10,8,128]{3,2,1,0:T(8,128)S(1)}, u32[]{:S(2)}, u32[]{:S(2)}) collective-permute-start(f32[6,10,8,128]{3,2,1,0:T(8,128)S(1)} %fusion.8), channel_id=1, source_target_pairs={{0,8},{1,9},{2,10},{3,11},{4,12},{5,13},{6,14},{7,15},{8,0},{9,1},... | collective-permute-start | bytes 737288 | tf_op jit(solution)/shard_map/ppermute | solution.py:283
  44.8 2.0 %collective-permute-start.13 = (f32[6,10,8,128]{3,2,1,0:T(8,128)S(1)}, f32[6,10,8,128]{3,2,1,0:T(8,128)S(1)}, u32[]{:S(2)}, u32[]{:S(2)}) collective-permute-start(f32[6,10,8,128]{3,2,1,0:T(8,128)S(1)} %fusion.13), channel_id=1, source_target_pairs={{0,3},{1,0},{2,1},{3,2},{4,7},{5,4},{6,5},{7,6},{8,11},{9,8},{10,9... | collective-permute-start | bytes 737288 | tf_op jit(solution)/shard_map/ppermute | solution.py:283
  46.7 2.8 %collective-permute-done.17 = f32[6,10,8,128]{3,2,1,0:T(8,128)S(1)} collective-permute-done((f32[6,10,8,128]{3,2,1,0:T(8,128)S(1)}, f32[6,10,8,128]{3,2,1,0:T(8,128)S(1)}, u32[]{:S(2)}, u32[]{:S(2)}) %collective-permute-start.17) | collective-permute-done | bytes 245792 | tf_op jit(solution)/shard_map/ppermute | solution.py:283
  49.7 2.3 %collective-permute-start.7 = (f32[2,6,10,8,128]{4,3,2,1,0:T(8,128)S(1)}, f32[2,6,10,8,128]{4,3,2,1,0:T(8,128)S(1)}, u32[]{:S(2)}, u32[]{:S(2)}) collective-permute-start(f32[2,6,10,8,128]{4,3,2,1,0:T(8,128)S(1)} %get-tuple-element.68.own), channel_id=1, source_target_pairs={{0,96},{16,112},{32,64},{48,80},{64,32},{80,48},{96,0},{112,16},{1... | collective-permute-start | bytes 1474568 | tf_op jit(solution)/shard_map/ppermute | solution.py:287
  52.0 1.3 collective-permute-start.11
  53.2 1.3 collective-permute-done.21
  54.6 1.5 collective-permute-start.18
  56.1 1.9 %collective-permute-start.14 = (f32[6,10,8,128]{3,2,1,0:T(8,128)S(1)}, f32[6,10,8,128]{3,2,1,0:T(8,128)S(1)}, u32[]{:S(2)}, u32[]{:S(2)}) collective-permute-start(f32[6,10,8,128]{3,2,1,0:T(8,128)S(1)} %fusion.13), channel_id=1, source_target_pairs={{0,2},{1,3},{2,0},{3,1},{4,6},{5,7},{6,4},{7,5},{8,10},{9,11},{10,... | collective-permute-start | bytes 737288 | tf_op jit(solution)/shard_map/ppermute | solution.py:283
  58.0 11.9 %collective-permute-done.14 = f32[6,10,8,128]{3,2,1,0:T(8,128)S(1)} collective-permute-done((f32[6,10,8,128]{3,2,1,0:T(8,128)S(1)}, f32[6,10,8,128]{3,2,1,0:T(8,128)S(1)}, u32[]{:S(2)}, u32[]{:S(2)}) %collective-permute-start.14) | collective-permute-done | bytes 245792 | tf_op jit(solution)/shard_map/ppermute | solution.py:283
  69.9 1.2 collective-permute-start.28
  71.2 2.2 %collective-permute-start.22 = (f32[2,6,10,8,128]{4,3,2,1,0:T(8,128)S(1)}, f32[2,6,10,8,128]{4,3,2,1,0:T(8,128)S(1)}, u32[]{:S(2)}, u32[]{:S(2)}) collective-permute-start(f32[2,6,10,8,128]{4,3,2,1,0:T(8,128)S(1)} %pad_maximum_fusion.4.refs_3_), channel_id=1, source_target_pairs={{0,3},{1,0},{2,1},{3,2},{4,7},{5,4},{6,5},{7,6},{8,11},{9,8},{10,9... | collective-permute-start | bytes 1474568 | tf_op jit(solution)/shard_map/ppermute | solution.py:283
  73.4 1.0 collective-permute-start.15
  74.5 7.4 %collective-permute-done.28.refs_1_ = f32[2,6,10,8,128]{4,3,2,1,0:T(8,128)S(1)} collective-permute-done((f32[2,6,10,8,128]{4,3,2,1,0:T(8,128)S(1)}, f32[2,6,10,8,128]{4,3,2,1,0:T(8,128)S(1)}, u32[]{:S(2)}, u32[]{:S(2)}) %collective-permute-start.28) | collective-permute-done | bytes 491552 | tf_op jit(solution)/shard_map/ppermute | solution.py:283
  81.9 2.2 %collective-permute-start.8 = (f32[6,10,8,128]{3,2,1,0:T(8,128)S(1)}, f32[6,10,8,128]{3,2,1,0:T(8,128)S(1)}, u32[]{:S(2)}, u32[]{:S(2)}) collective-permute-start(f32[6,10,8,128]{3,2,1,0:T(8,128)S(1)} %slice_bitcast_fusion.1), channel_id=1, source_target_pairs={{0,96},{16,112},{32,64},{48,80},{64,32},{80,48},{96,0},{112,16},{1... | collective-permute-start | bytes 737288 | tf_op jit(solution)/shard_map/ppermute | solution.py:287
  84.2 8.6 %collective-permute-done.22.refs_3_ = f32[2,6,10,8,128]{4,3,2,1,0:T(8,128)S(1)} collective-permute-done((f32[2,6,10,8,128]{4,3,2,1,0:T(8,128)S(1)}, f32[2,6,10,8,128]{4,3,2,1,0:T(8,128)S(1)}, u32[]{:S(2)}, u32[]{:S(2)}) %collective-permute-start.22) | collective-permute-done | bytes 491552 | tf_op jit(solution)/shard_map/ppermute | solution.py:283
  93.8 2.3 %collective-permute-start.16 = (f32[2,6,10,8,128]{4,3,2,1,0:T(8,128)S(1)}, f32[2,6,10,8,128]{4,3,2,1,0:T(8,128)S(1)}, u32[]{:S(2)}, u32[]{:S(2)}) collective-permute-start(f32[2,6,10,8,128]{4,3,2,1,0:T(8,128)S(1)} %collective-permute-done.15.refs_1_), channel_id=1, source_target_pairs={{0,12},{1,13},{2,14},{3,15},{4,0},{5,1},{6,2},{7,3},{8,4},{9,5},{1... | collective-permute-start | bytes 1474568 | tf_op jit(solution)/shard_map/ppermute | solution.py:283
  96.1 2.0 %collective-permute-start.19 = (f32[2,6,10,8,128]{4,3,2,1,0:T(8,128)S(1)}, f32[2,6,10,8,128]{4,3,2,1,0:T(8,128)S(1)}, u32[]{:S(2)}, u32[]{:S(2)}) collective-permute-start(f32[2,6,10,8,128]{4,3,2,1,0:T(8,128)S(1)} %collective-permute-done.18.refs_2_), channel_id=1, source_target_pairs={{0,1},{1,2},{2,3},{3,0},{4,5},{5,6},{6,7},{7,4},{8,9},{9,10},{10,1... | collective-permute-start | bytes 1474568 | tf_op jit(solution)/shard_map/ppermute | solution.py:283
  98.4 2.6 %shard_map.114 = (f32[384,384]{1,0:T(8,128)}, bf16[384,1280]{1,0:T(8,128)(2,1)S(1)}, bf16[384,1280]{1,0:T(8,128)(2,1)S(1)}) custom-call(bf16[384,1280]{1,0:T(8,128)(2,1)S(1)} %get-tuple-element.40.left_high, bf16[384,1280]{1,0:T(8,128)(2,1)S(1)} %get-tuple-element.41.left_low, f32[2,6,10,8,128]{4,3,2,1,0:T(8,128)S(1)} %get-tuple-element.69.refs_0_, ...), custom_call_target="tpu_custom_call" | custom-call | flops 1132462080 | bytes 4194304 | tf_op jit(solution)/shard_map/pallas_call | solution.py:152
  102.8 2.6 %shard_map.113 = (f32[384,384]{1,0:T(8,128)}, bf16[384,1280]{1,0:T(8,128)(2,1)S(1)}, bf16[384,1280]{1,0:T(8,128)(2,1)S(1)}) custom-call(bf16[384,1280]{1,0:T(8,128)(2,1)S(1)} %get-tuple-element.40.left_high, bf16[384,1280]{1,0:T(8,128)(2,1)S(1)} %get-tuple-element.41.left_low, f32[2,6,10,8,128]{4,3,2,1,0:T(8,128)S(1)} %collective-permute-done.11.refs_0_, ...), custom_call_target="tpu_custom_call" | custom-call | flops 1132462080 | bytes 4194304 | tf_op jit(solution)/shard_map/pallas_call | solution.py:152
  107.9 2.6 %shard_map.112 = (f32[384,384]{1,0:T(8,128)}, bf16[384,1280]{1,0:T(8,128)(2,1)S(1)}, bf16[384,1280]{1,0:T(8,128)(2,1)S(1)}) custom-call(bf16[384,1280]{1,0:T(8,128)(2,1)S(1)} %get-tuple-element.40.left_high, bf16[384,1280]{1,0:T(8,128)(2,1)S(1)} %get-tuple-element.41.left_low, f32[2,6,10,8,128]{4,3,2,1,0:T(8,128)S(1)} %collective-permute-done.25.refs_0_, ...), custom_call_target="tpu_custom_call" | custom-call | flops 1132462080 | bytes 4194304 | tf_op jit(solution)/shard_map/pallas_call | solution.py:152
  110.5 2.6 %shard_map.111 = (f32[384,384]{1,0:T(8,128)}, bf16[384,1280]{1,0:T(8,128)(2,1)S(1)}, bf16[384,1280]{1,0:T(8,128)(2,1)S(1)}) custom-call(bf16[384,1280]{1,0:T(8,128)(2,1)S(1)} %get-tuple-element.40.left_high, bf16[384,1280]{1,0:T(8,128)(2,1)S(1)} %get-tuple-element.41.left_low, f32[2,6,10,8,128]{4,3,2,1,0:T(8,128)S(1)} %collective-permute-done.12.refs_0_, ...), custom_call_target="tpu_custom_call" | custom-call | flops 1132462080 | bytes 4194304 | tf_op jit(solution)/shard_map/pallas_call | solution.py:152
  113.8 1.2 copy-done.5
  115.0 3.2 %shard_map.115.refs_6_ = f32[384,1280]{1,0:T(8,128)S(1)} custom-call(f32[384,384]{1,0:T(8,128)} %get-tuple-element.55.refs_0_, f32[384,384]{1,0:T(8,128)} %collective-permute-done.31.refs_1_, f32[384,1]{1,0:T(8,128)S(1)} %copy.19.refs_2_, f32[1,384]{1,0:T(1,128)S(1)} %reshape.38.refs_3_, bf16[384,1280]{1,0:T(8,128)(2,1)S(1)} %get-tuple-element.57.refs_4_, ...), custom_call_target="tpu_custom_call" | custom-call | flops 1132462080 | bytes 4194304 | tf_op jit(solution)/shard_map/pallas_call | solution.py:197
  118.3 3.2 %shard_map.116.refs_6_ = f32[384,1280]{1,0:T(8,128)S(1)} custom-call(f32[384,384]{1,0:T(8,128)} %get-tuple-element.51.refs_0_, f32[384,384]{1,0:T(8,128)} %collective-permute-done.30.refs_1_, f32[384,1]{1,0:T(8,128)S(1)} %copy.19.refs_2_, f32[1,384]{1,0:T(1,128)S(1)} %reshape.39.refs_3_, bf16[384,1280]{1,0:T(8,128)(2,1)S(1)} %copy-done.7, ...), custom_call_target="tpu_custom_call" | custom-call | flops 1132462080 | bytes 4194304 | tf_op jit(solution)/shard_map/pallas_call | solution.py:197
  121.6 3.1 %shard_map.117.refs_6_ = f32[384,1280]{1,0:T(8,128)S(1)} custom-call(f32[384,384]{1,0:T(8,128)} %get-tuple-element.47.refs_0_, f32[384,384]{1,0:T(8,128)} %collective-permute-done.27.refs_1_, f32[384,1]{1,0:T(8,128)S(1)} %copy.19.refs_2_, f32[1,384]{1,0:T(1,128)S(1)} %reshape.40.refs_3_, bf16[384,1280]{1,0:T(8,128)(2,1)S(1)} %copy-done.11, ...), custom_call_target="tpu_custom_call" | custom-call | flops 1132462080 | bytes 4194304 | tf_op jit(solution)/shard_map/pallas_call | solution.py:197
  124.7 3.6 %shard_map.118 = (f32[2,480,128]{2,1,0:T(8,128)S(1)}, f32[2,480,128]{2,1,0:T(8,128)S(1)}, f32[2,480,128]{2,1,0:T(8,128)S(1)}, f32[2,480,128]{2,1,0:T(8,128)S(1)}) custom-call(s32[5]{0:T(128)S(1)} %stack.74.places, f32[384,384]{1,0:T(8,128)} %get-tuple-element.42.refs_0_, f32[384,384]{1,0:T(8,128)} %collective-permute-done.24.refs_1_, ...), custom_call_target="tpu_custom_call" | custom-call | flops 1132462080 | bytes 4194304 | tf_op jit(solution)/shard_map/pallas_call | solution.py:234
  128.3 1.6 %collective-permute-start.34 = (f32[2,480,128]{2,1,0:T(8,128)S(1)}, f32[2,480,128]{2,1,0:T(8,128)S(1)}, u32[]{:S(2)}, u32[]{:S(2)}) collective-permute-start(f32[2,480,128]{2,1,0:T(8,128)S(1)} %get-tuple-element.62), channel_id=1, source_target_pairs={{0,96},{16,112},{32,64},{48,80},{64,32},{80,48},{96,0},{112,16},{1... | collective-permute-start | bytes 1474568 | tf_op jit(solution)/shard_map/ppermute | solution.py:287
  129.9 12.8 %collective-permute-done.34.near_1 = f32[2,480,128]{2,1,0:T(8,128)S(1)} collective-permute-done((f32[2,480,128]{2,1,0:T(8,128)S(1)}, f32[2,480,128]{2,1,0:T(8,128)S(1)}, u32[]{:S(2)}, u32[]{:S(2)}) %collective-permute-start.34) | collective-permute-done | bytes 491552 | tf_op jit(solution)/shard_map/ppermute | solution.py:287
  142.9 1.7 %collective-permute-start.33 = (f32[480,128]{1,0:T(8,128)S(1)}, f32[480,128]{1,0:T(8,128)S(1)}, u32[]{:S(2)}, u32[]{:S(2)}) collective-permute-start(f32[480,128]{1,0:T(8,128)S(1)} %fusion.3), channel_id=1, source_target_pairs={{0,96},{16,112},{32,64},{48,80},{64,32},{80,48},{96,0},{112,16},{1... | collective-permute-start | bytes 737288 | tf_op jit(solution)/shard_map/ppermute | solution.py:287
  144.6 5.3 %collective-permute-done.35.last_1 = f32[480,128]{1,0:T(8,128)S(1)} collective-permute-done((f32[480,128]{1,0:T(8,128)S(1)}, f32[480,128]{1,0:T(8,128)S(1)}, u32[]{:S(2)}, u32[]{:S(2)}) %collective-permute-start.35) | collective-permute-done | bytes 245792 | tf_op jit(solution)/shard_map/ppermute | solution.py:287
  149.9 1.3 collective-permute-done.33.last_0
  151.2 1.6 %unpack.1 = f32[6,64,320]{2,1,0:T(8,128)} custom-call(s32[5]{0:T(128)S(1)} %stack.74.places, f32[2,480,128]{2,1,0:T(8,128)S(1)} %get-tuple-element.59.kept_0, f32[2,480,128]{2,1,0:T(8,128)S(1)} %collective-permute-done.32.near_0, f32[480,128]{1,0:T(8,128)S(1)} %collective-permute-done.33.last_0, f32[2,480,128]{2,1,0:T(8,128)S(1)} %get-tuple-element.61.kept_1, ...), custom_call_target="tpu_custom_call" | custom-call | tf_op jit(solution)/shard_map/unpack/pallas_call | solution.py:266
  (113 shorter events, 9.0 us)
Async XLA Ops:
  3.1 4.4 %copy-start.17 = (s32[320]{0:T(512)S(1)}, s32[320]{0:T(512)}, u32[]{:S(2)}) copy-start(s32[320]{0:T(512)} %constant.83.clone) | copy-start | bytes 3844
  3.1 4.4 %copy-start.18 = (s32[320]{0:T(512)S(1)}, s32[320]{0:T(512)}, u32[]{:S(2)}) copy-start(s32[320]{0:T(512)} %constant.84.clone) | copy-start | bytes 3844
  3.1 4.4 %copy-start.19 = (s32[320]{0:T(512)S(1)}, s32[320]{0:T(512)}, u32[]{:S(2)}) copy-start(s32[320]{0:T(512)} %constant.91) | copy-start | bytes 3844
  3.1 4.4 %copy-start.21 = (pred[320]{0:T(512)(128)(4,1)S(1)}, pred[320]{0:T(512)(128)(4,1)}, u32[]{:S(2)}) copy-start(pred[320]{0:T(512)(128)(4,1)} %constant.87) | copy-start | bytes 964
  3.1 4.4 %copy-start.22 = (pred[320]{0:T(512)(128)(4,1)S(1)}, pred[320]{0:T(512)(128)(4,1)}, u32[]{:S(2)}) copy-start(pred[320]{0:T(512)(128)(4,1)} %constant.88) | copy-start | bytes 964
  3.1 4.4 %copy-start.23 = (pred[320]{0:T(512)(128)(4,1)S(1)}, pred[320]{0:T(512)(128)(4,1)}, u32[]{:S(2)}) copy-start(pred[320]{0:T(512)(128)(4,1)} %constant.89) | copy-start | bytes 964
  3.1 4.4 %copy-start.15 = (s32[1024]{0:T(1024)S(1)}, s32[1024]{0:T(1024)}, u32[]{:S(2)}) copy-start(s32[1024]{0:T(1024)} %param.16) | copy-start | bytes 12292
  3.1 4.7 %copy-start.1 = (f32[2560,320]{0,1:T(8,128)S(1)}, f32[2560,320]{0,1:T(8,128)}, u32[]{:S(2)}) copy-start(f32[2560,320]{0,1:T(8,128)} %param.12) | copy-start | bytes 9830404
  6.9 5.1 %collective-permute-start.1 = (f32[2,2,6,10,8,128]{5,4,3,2,1,0:T(8,128)}, f32[2,2,6,10,8,128]{5,4,3,2,1,0:T(8,128)}, u32[]{:S(2)}, u32[]{:S(2)}) collective-permute-start(f32[2,2,6,10,8,128]{5,4,3,2,1,0:T(8,128)} %get-tuple-element.37), channel_id=1, source_target_pairs={{0,16},{16,0},{32,48},{48,32},{64,80},{80,64},{96,112},{112,96},{1... | collective-permute-start | bytes 2949128 | tf_op jit(solution)/shard_map/ppermute | solution.py:287
  6.9 10.8 %collective-permute-start = (f32[2,2,6,10,8,128]{5,4,3,2,1,0:T(8,128)}, f32[2,2,6,10,8,128]{5,4,3,2,1,0:T(8,128)}, u32[]{:S(2)}, u32[]{:S(2)}) collective-permute-start(f32[2,2,6,10,8,128]{5,4,3,2,1,0:T(8,128)} %get-tuple-element.35), channel_id=1, source_target_pairs={{0,16},{16,0},{32,48},{48,32},{64,80},{80,64},{96,112},{112,96},{1... | collective-permute-start | bytes 2949128 | tf_op jit(solution)/shard_map/ppermute | solution.py:287
  13.3 13.2 %collective-permute-start.2 = (f32[2,6,10,8,128]{4,3,2,1,0:T(8,128)S(1)}, f32[2,6,10,8,128]{4,3,2,1,0:T(8,128)S(1)}, u32[]{:S(2)}, u32[]{:S(2)}) collective-permute-start(f32[2,6,10,8,128]{4,3,2,1,0:T(8,128)S(1)} %get-tuple-element.66), channel_id=1, source_target_pairs={{0,32},{16,48},{32,0},{48,16},{64,96},{80,112},{96,64},{112,80},{1... | collective-permute-start | bytes 1474568 | tf_op jit(solution)/shard_map/ppermute | solution.py:287
  15.1 14.1 %collective-permute-start.3 = (f32[2,6,10,8,128]{4,3,2,1,0:T(8,128)S(1)}, f32[2,6,10,8,128]{4,3,2,1,0:T(8,128)S(1)}, u32[]{:S(2)}, u32[]{:S(2)}) collective-permute-start(f32[2,6,10,8,128]{4,3,2,1,0:T(8,128)S(1)} %get-tuple-element.65), channel_id=1, source_target_pairs={{0,96},{16,112},{32,64},{48,80},{64,32},{80,48},{96,0},{112,16},{1... | collective-permute-start | bytes 1474568 | tf_op jit(solution)/shard_map/ppermute | solution.py:287
  29.1 8.0 %collective-permute-start.4 = (f32[6,10,8,128]{3,2,1,0:T(8,128)S(1)}, f32[6,10,8,128]{3,2,1,0:T(8,128)S(1)}, u32[]{:S(2)}, u32[]{:S(2)}) collective-permute-start(f32[6,10,8,128]{3,2,1,0:T(8,128)S(1)} %fusion.10), channel_id=1, source_target_pairs={{0,96},{16,112},{32,64},{48,80},{64,32},{80,48},{96,0},{112,16},{1... | collective-permute-start | bytes 737288 | tf_op jit(solution)/shard_map/ppermute | solution.py:287
  31.4 7.3 %collective-permute-start.5 = (f32[6,10,8,128]{3,2,1,0:T(8,128)S(1)}, f32[6,10,8,128]{3,2,1,0:T(8,128)S(1)}, u32[]{:S(2)}, u32[]{:S(2)}) collective-permute-start(f32[6,10,8,128]{3,2,1,0:T(8,128)S(1)} %fusion.5), channel_id=1, source_target_pairs={{0,32},{16,48},{32,0},{48,16},{64,96},{80,112},{96,64},{112,80},{1... | collective-permute-start | bytes 737288 | tf_op jit(solution)/shard_map/ppermute | solution.py:287
  37.2 9.5 %collective-permute-start.10 = (f32[6,10,8,128]{3,2,1,0:T(8,128)S(1)}, f32[6,10,8,128]{3,2,1,0:T(8,128)S(1)}, u32[]{:S(2)}, u32[]{:S(2)}) collective-permute-start(f32[6,10,8,128]{3,2,1,0:T(8,128)S(1)} %fusion.13), channel_id=1, source_target_pairs={{0,1},{1,2},{2,3},{3,0},{4,5},{5,6},{6,7},{7,4},{8,9},{9,10},{10,1... | collective-permute-start | bytes 737288 | tf_op jit(solution)/shard_map/ppermute | solution.py:283
  38.8 10.7 %collective-permute-start.17 = (f32[6,10,8,128]{3,2,1,0:T(8,128)S(1)}, f32[6,10,8,128]{3,2,1,0:T(8,128)S(1)}, u32[]{:S(2)}, u32[]{:S(2)}) collective-permute-start(f32[6,10,8,128]{3,2,1,0:T(8,128)S(1)} %fusion.8), channel_id=1, source_target_pairs={{0,4},{1,5},{2,6},{3,7},{4,8},{5,9},{6,10},{7,11},{8,12},{9,13},{1... | collective-permute-start | bytes 737288 | tf_op jit(solution)/shard_map/ppermute | solution.py:283
  40.8 11.2 %collective-permute-start.20 = (f32[6,10,8,128]{3,2,1,0:T(8,128)S(1)}, f32[6,10,8,128]{3,2,1,0:T(8,128)S(1)}, u32[]{:S(2)}, u32[]{:S(2)}) collective-permute-start(f32[6,10,8,128]{3,2,1,0:T(8,128)S(1)} %fusion.8), channel_id=1, source_target_pairs={{0,12},{1,13},{2,14},{3,15},{4,0},{5,1},{6,2},{7,3},{8,4},{9,5},{1... | collective-permute-start | bytes 737288 | tf_op jit(solution)/shard_map/ppermute | solution.py:283
  43.0 11.6 %collective-permute-start.21 = (f32[6,10,8,128]{3,2,1,0:T(8,128)S(1)}, f32[6,10,8,128]{3,2,1,0:T(8,128)S(1)}, u32[]{:S(2)}, u32[]{:S(2)}) collective-permute-start(f32[6,10,8,128]{3,2,1,0:T(8,128)S(1)} %fusion.8), channel_id=1, source_target_pairs={{0,8},{1,9},{2,10},{3,11},{4,12},{5,13},{6,14},{7,15},{8,0},{9,1},... | collective-permute-start | bytes 737288 | tf_op jit(solution)/shard_map/ppermute | solution.py:283
  44.8 11.3 %collective-permute-start.13 = (f32[6,10,8,128]{3,2,1,0:T(8,128)S(1)}, f32[6,10,8,128]{3,2,1,0:T(8,128)S(1)}, u32[]{:S(2)}, u32[]{:S(2)}) collective-permute-start(f32[6,10,8,128]{3,2,1,0:T(8,128)S(1)} %fusion.13), channel_id=1, source_target_pairs={{0,3},{1,0},{2,1},{3,2},{4,7},{5,4},{6,5},{7,6},{8,11},{9,8},{10,9... | collective-permute-start | bytes 737288 | tf_op jit(solution)/shard_map/ppermute | solution.py:283
  49.6 21.5 %collective-permute-start.6 = (f32[2,6,10,8,128]{4,3,2,1,0:T(8,128)S(1)}, f32[2,6,10,8,128]{4,3,2,1,0:T(8,128)S(1)}, u32[]{:S(2)}, u32[]{:S(2)}) collective-permute-start(f32[2,6,10,8,128]{4,3,2,1,0:T(8,128)S(1)} %get-tuple-element.68.own), channel_id=1, source_target_pairs={{0,32},{16,48},{32,0},{48,16},{64,96},{80,112},{96,64},{112,80},{1... | collective-permute-start | bytes 1474568 | tf_op jit(solution)/shard_map/ppermute | solution.py:287
  49.7 21.5 %collective-permute-start.7 = (f32[2,6,10,8,128]{4,3,2,1,0:T(8,128)S(1)}, f32[2,6,10,8,128]{4,3,2,1,0:T(8,128)S(1)}, u32[]{:S(2)}, u32[]{:S(2)}) collective-permute-start(f32[2,6,10,8,128]{4,3,2,1,0:T(8,128)S(1)} %get-tuple-element.68.own), channel_id=1, source_target_pairs={{0,96},{16,112},{32,64},{48,80},{64,32},{80,48},{96,0},{112,16},{1... | collective-permute-start | bytes 1474568 | tf_op jit(solution)/shard_map/ppermute | solution.py:287
  52.0 21.5 %collective-permute-start.11 = (f32[2,6,10,8,128]{4,3,2,1,0:T(8,128)S(1)}, f32[2,6,10,8,128]{4,3,2,1,0:T(8,128)S(1)}, u32[]{:S(2)}, u32[]{:S(2)}) collective-permute-start(f32[2,6,10,8,128]{4,3,2,1,0:T(8,128)S(1)} %get-tuple-element.69.refs_0_), channel_id=1, source_target_pairs={{0,4},{1,5},{2,6},{3,7},{4,8},{5,9},{6,10},{7,11},{8,12},{9,13},{1... | collective-permute-start | bytes 1474568 | tf_op jit(solution)/shard_map/ppermute | solution.py:283
  54.6 18.9 %collective-permute-start.18 = (f32[2,6,10,8,128]{4,3,2,1,0:T(8,128)S(1)}, f32[2,6,10,8,128]{4,3,2,1,0:T(8,128)S(1)}, u32[]{:S(2)}, u32[]{:S(2)}) collective-permute-start(f32[2,6,10,8,128]{4,3,2,1,0:T(8,128)S(1)} %get-tuple-element.67.refs_2_), channel_id=1, source_target_pairs={{0,1},{1,2},{2,3},{3,0},{4,5},{5,6},{6,7},{7,4},{8,9},{9,10},{10,1... | collective-permute-start | bytes 1474568 | tf_op jit(solution)/shard_map/ppermute | solution.py:283
  56.1 13.9 %collective-permute-start.14 = (f32[6,10,8,128]{3,2,1,0:T(8,128)S(1)}, f32[6,10,8,128]{3,2,1,0:T(8,128)S(1)}, u32[]{:S(2)}, u32[]{:S(2)}) collective-permute-start(f32[6,10,8,128]{3,2,1,0:T(8,128)S(1)} %fusion.13), channel_id=1, source_target_pairs={{0,2},{1,3},{2,0},{3,1},{4,6},{5,7},{6,4},{7,5},{8,10},{9,11},{10,... | collective-permute-start | bytes 737288 | tf_op jit(solution)/shard_map/ppermute | solution.py:283
  69.9 12.0 %collective-permute-start.28 = (f32[2,6,10,8,128]{4,3,2,1,0:T(8,128)S(1)}, f32[2,6,10,8,128]{4,3,2,1,0:T(8,128)S(1)}, u32[]{:S(2)}, u32[]{:S(2)}) collective-permute-start(f32[2,6,10,8,128]{4,3,2,1,0:T(8,128)S(1)} %get-tuple-element.69.refs_0_), channel_id=1, source_target_pairs={{0,12},{1,13},{2,14},{3,15},{4,0},{5,1},{6,2},{7,3},{8,4},{9,5},{1... | collective-permute-start | bytes 1474568 | tf_op jit(solution)/shard_map/ppermute | solution.py:283
  71.1 13.0 %collective-permute-start.29 = (f32[2,6,10,8,128]{4,3,2,1,0:T(8,128)S(1)}, f32[2,6,10,8,128]{4,3,2,1,0:T(8,128)S(1)}, u32[]{:S(2)}, u32[]{:S(2)}) collective-permute-start(f32[2,6,10,8,128]{4,3,2,1,0:T(8,128)S(1)} %get-tuple-element.67.refs_2_), channel_id=1, source_target_pairs={{0,3},{1,0},{2,1},{3,2},{4,7},{5,4},{6,5},{7,6},{8,11},{9,8},{10,9... | collective-permute-start | bytes 1474568 | tf_op jit(solution)/shard_map/ppermute | solution.py:283
  71.2 21.6 %collective-permute-start.22 = (f32[2,6,10,8,128]{4,3,2,1,0:T(8,128)S(1)}, f32[2,6,10,8,128]{4,3,2,1,0:T(8,128)S(1)}, u32[]{:S(2)}, u32[]{:S(2)}) collective-permute-start(f32[2,6,10,8,128]{4,3,2,1,0:T(8,128)S(1)} %pad_maximum_fusion.4.refs_3_), channel_id=1, source_target_pairs={{0,3},{1,0},{2,1},{3,2},{4,7},{5,4},{6,5},{7,6},{8,11},{9,8},{10,9... | collective-permute-start | bytes 1474568 | tf_op jit(solution)/shard_map/ppermute | solution.py:283
  73.4 20.4 %collective-permute-start.26 = (f32[2,6,10,8,128]{4,3,2,1,0:T(8,128)S(1)}, f32[2,6,10,8,128]{4,3,2,1,0:T(8,128)S(1)}, u32[]{:S(2)}, u32[]{:S(2)}) collective-permute-start(f32[2,6,10,8,128]{4,3,2,1,0:T(8,128)S(1)} %pad_maximum_fusion.4.refs_3_), channel_id=1, source_target_pairs={{0,1},{1,2},{2,3},{3,0},{4,5},{5,6},{6,7},{7,4},{8,9},{9,10},{10,1... | collective-permute-start | bytes 1474568 | tf_op jit(solution)/shard_map/ppermute | solution.py:283
  73.4 20.4 %collective-permute-start.15 = (f32[2,6,10,8,128]{4,3,2,1,0:T(8,128)S(1)}, f32[2,6,10,8,128]{4,3,2,1,0:T(8,128)S(1)}, u32[]{:S(2)}, u32[]{:S(2)}) collective-permute-start(f32[2,6,10,8,128]{4,3,2,1,0:T(8,128)S(1)} %pad_maximum_fusion.2.refs_1_), channel_id=1, source_target_pairs={{0,12},{1,13},{2,14},{3,15},{4,0},{5,1},{6,2},{7,3},{8,4},{9,5},{1... | collective-permute-start | bytes 1474568 | tf_op jit(solution)/shard_map/ppermute | solution.py:283
  81.9 14.2 %collective-permute-start.8 = (f32[6,10,8,128]{3,2,1,0:T(8,128)S(1)}, f32[6,10,8,128]{3,2,1,0:T(8,128)S(1)}, u32[]{:S(2)}, u32[]{:S(2)}) collective-permute-start(f32[6,10,8,128]{3,2,1,0:T(8,128)S(1)} %slice_bitcast_fusion.1), channel_id=1, source_target_pairs={{0,96},{16,112},{32,64},{48,80},{64,32},{80,48},{96,0},{112,16},{1... | collective-permute-start | bytes 737288 | tf_op jit(solution)/shard_map/ppermute | solution.py:287
  84.2 11.9 %collective-permute-start.9 = (f32[6,10,8,128]{3,2,1,0:T(8,128)S(1)}, f32[6,10,8,128]{3,2,1,0:T(8,128)S(1)}, u32[]{:S(2)}, u32[]{:S(2)}) collective-permute-start(f32[6,10,8,128]{3,2,1,0:T(8,128)S(1)} %slice_bitcast_fusion), channel_id=1, source_target_pairs={{0,32},{16,48},{32,0},{48,16},{64,96},{80,112},{96,64},{112,80},{1... | collective-permute-start | bytes 737288 | tf_op jit(solution)/shard_map/ppermute | solution.py:287
  92.8 10.0 %collective-permute-start.25 = (f32[2,6,10,8,128]{4,3,2,1,0:T(8,128)S(1)}, f32[2,6,10,8,128]{4,3,2,1,0:T(8,128)S(1)}, u32[]{:S(2)}, u32[]{:S(2)}) collective-permute-start(f32[2,6,10,8,128]{4,3,2,1,0:T(8,128)S(1)} %pad_maximum_fusion.2.refs_1_), channel_id=1, source_target_pairs={{0,4},{1,5},{2,6},{3,7},{4,8},{5,9},{6,10},{7,11},{8,12},{9,13},{1... | collective-permute-start | bytes 1474568 | tf_op jit(solution)/shard_map/ppermute | solution.py:283
  93.8 13.6 %collective-permute-start.23 = (f32[2,6,10,8,128]{4,3,2,1,0:T(8,128)S(1)}, f32[2,6,10,8,128]{4,3,2,1,0:T(8,128)S(1)}, u32[]{:S(2)}, u32[]{:S(2)}) collective-permute-start(f32[2,6,10,8,128]{4,3,2,1,0:T(8,128)S(1)} %collective-permute-done.22.refs_3_), channel_id=1, source_target_pairs={{0,3},{1,0},{2,1},{3,2},{4,7},{5,4},{6,5},{7,6},{8,11},{9,8},{10,9... | collective-permute-start | bytes 1474568 | tf_op jit(solution)/shard_map/ppermute | solution.py:283
  93.8 16.7 %collective-permute-start.16 = (f32[2,6,10,8,128]{4,3,2,1,0:T(8,128)S(1)}, f32[2,6,10,8,128]{4,3,2,1,0:T(8,128)S(1)}, u32[]{:S(2)}, u32[]{:S(2)}) collective-permute-start(f32[2,6,10,8,128]{4,3,2,1,0:T(8,128)S(1)} %collective-permute-done.15.refs_1_), channel_id=1, source_target_pairs={{0,12},{1,13},{2,14},{3,15},{4,0},{5,1},{6,2},{7,3},{8,4},{9,5},{1... | collective-permute-start | bytes 1474568 | tf_op jit(solution)/shard_map/ppermute | solution.py:283
  96.1 14.4 %collective-permute-start.12 = (f32[2,6,10,8,128]{4,3,2,1,0:T(8,128)S(1)}, f32[2,6,10,8,128]{4,3,2,1,0:T(8,128)S(1)}, u32[]{:S(2)}, u32[]{:S(2)}) collective-permute-start(f32[2,6,10,8,128]{4,3,2,1,0:T(8,128)S(1)} %collective-permute-done.11.refs_0_), channel_id=1, source_target_pairs={{0,4},{1,5},{2,6},{3,7},{4,8},{5,9},{6,10},{7,11},{8,12},{9,13},{1... | collective-permute-start | bytes 1474568 | tf_op jit(solution)/shard_map/ppermute | solution.py:283
  96.1 14.4 %collective-permute-start.19 = (f32[2,6,10,8,128]{4,3,2,1,0:T(8,128)S(1)}, f32[2,6,10,8,128]{4,3,2,1,0:T(8,128)S(1)}, u32[]{:S(2)}, u32[]{:S(2)}) collective-permute-start(f32[2,6,10,8,128]{4,3,2,1,0:T(8,128)S(1)} %collective-permute-done.18.refs_2_), channel_id=1, source_target_pairs={{0,1},{1,2},{2,3},{3,0},{4,5},{5,6},{6,7},{7,4},{8,9},{9,10},{10,1... | collective-permute-start | bytes 1474568 | tf_op jit(solution)/shard_map/ppermute | solution.py:283
  102.8 11.0 %collective-permute-start.31 = (f32[384,384]{1,0:T(8,128)}, f32[384,384]{1,0:T(8,128)}, u32[]{:S(2)}, u32[]{:S(2)}) collective-permute-start(f32[384,384]{1,0:T(8,128)} %get-tuple-element.55.refs_0_), channel_id=1, source_target_pairs={{0,16},{16,0},{32,48},{48,32},{64,80},{80,64},{96,112},{112,96},{1... | collective-permute-start | bytes 1769480 | tf_op jit(solution)/shard_map/ppermute | solution.py:287
  107.4 10.9 %collective-permute-start.30 = (f32[384,384]{1,0:T(8,128)}, f32[384,384]{1,0:T(8,128)}, u32[]{:S(2)}, u32[]{:S(2)}) collective-permute-start(f32[384,384]{1,0:T(8,128)} %get-tuple-element.51.refs_0_), channel_id=1, source_target_pairs={{0,16},{16,0},{32,48},{48,32},{64,80},{80,64},{96,112},{112,96},{1... | collective-permute-start | bytes 1769480 | tf_op jit(solution)/shard_map/ppermute | solution.py:287
  110.5 11.0 %collective-permute-start.27 = (f32[384,384]{1,0:T(8,128)}, f32[384,384]{1,0:T(8,128)}, u32[]{:S(2)}, u32[]{:S(2)}) collective-permute-start(f32[384,384]{1,0:T(8,128)} %get-tuple-element.47.refs_0_), channel_id=1, source_target_pairs={{0,16},{16,0},{32,48},{48,32},{64,80},{80,64},{96,112},{112,96},{1... | collective-permute-start | bytes 1769480 | tf_op jit(solution)/shard_map/ppermute | solution.py:287
  113.2 11.5 %collective-permute-start.24 = (f32[384,384]{1,0:T(8,128)}, f32[384,384]{1,0:T(8,128)}, u32[]{:S(2)}, u32[]{:S(2)}) collective-permute-start(f32[384,384]{1,0:T(8,128)} %get-tuple-element.42.refs_0_), channel_id=1, source_target_pairs={{0,16},{16,0},{32,48},{48,32},{64,80},{80,64},{96,112},{112,96},{1... | collective-permute-start | bytes 1769480 | tf_op jit(solution)/shard_map/ppermute | solution.py:287
  115.0 3.2 %copy-start.7 = (bf16[384,1280]{1,0:T(8,128)(2,1)S(1)}, bf16[384,1280]{1,0:T(8,128)(2,1)}, u32[]{:S(2)}) copy-start(bf16[384,1280]{1,0:T(8,128)(2,1)} %copy-done.6) | copy-start | bytes 2949124
  115.0 3.2 %copy-start.9 = (bf16[384,1280]{1,0:T(8,128)(2,1)S(1)}, bf16[384,1280]{1,0:T(8,128)(2,1)}, u32[]{:S(2)}) copy-start(bf16[384,1280]{1,0:T(8,128)(2,1)} %copy-done.8) | copy-start | bytes 2949124
  118.3 3.3 %copy-start.11 = (bf16[384,1280]{1,0:T(8,128)(2,1)S(1)}, bf16[384,1280]{1,0:T(8,128)(2,1)}, u32[]{:S(2)}) copy-start(bf16[384,1280]{1,0:T(8,128)(2,1)} %copy-done.10) | copy-start | bytes 2949124
  118.3 3.3 %copy-start.13 = (bf16[384,1280]{1,0:T(8,128)(2,1)S(1)}, bf16[384,1280]{1,0:T(8,128)(2,1)}, u32[]{:S(2)}) copy-start(bf16[384,1280]{1,0:T(8,128)(2,1)} %copy-done.12) | copy-start | bytes 2949124
  128.3 14.4 %collective-permute-start.34 = (f32[2,480,128]{2,1,0:T(8,128)S(1)}, f32[2,480,128]{2,1,0:T(8,128)S(1)}, u32[]{:S(2)}, u32[]{:S(2)}) collective-permute-start(f32[2,480,128]{2,1,0:T(8,128)S(1)} %get-tuple-element.62), channel_id=1, source_target_pairs={{0,96},{16,112},{32,64},{48,80},{64,32},{80,48},{96,0},{112,16},{1... | collective-permute-start | bytes 1474568 | tf_op jit(solution)/shard_map/ppermute | solution.py:287
  129.9 13.0 %collective-permute-start.32 = (f32[2,480,128]{2,1,0:T(8,128)S(1)}, f32[2,480,128]{2,1,0:T(8,128)S(1)}, u32[]{:S(2)}, u32[]{:S(2)}) collective-permute-start(f32[2,480,128]{2,1,0:T(8,128)S(1)} %get-tuple-element.60), channel_id=1, source_target_pairs={{0,32},{16,48},{32,0},{48,16},{64,96},{80,112},{96,64},{112,80},{1... | collective-permute-start | bytes 1474568 | tf_op jit(solution)/shard_map/ppermute | solution.py:287
  142.8 7.1 %collective-permute-start.35 = (f32[480,128]{1,0:T(8,128)S(1)}, f32[480,128]{1,0:T(8,128)S(1)}, u32[]{:S(2)}, u32[]{:S(2)}) collective-permute-start(f32[480,128]{1,0:T(8,128)S(1)} %fusion.2), channel_id=1, source_target_pairs={{0,32},{16,48},{32,0},{48,16},{64,96},{80,112},{96,64},{112,80},{1... | collective-permute-start | bytes 737288 | tf_op jit(solution)/shard_map/ppermute | solution.py:287
  142.9 8.3 %collective-permute-start.33 = (f32[480,128]{1,0:T(8,128)S(1)}, f32[480,128]{1,0:T(8,128)S(1)}, u32[]{:S(2)}, u32[]{:S(2)}) collective-permute-start(f32[480,128]{1,0:T(8,128)S(1)} %fusion.3), channel_id=1, source_target_pairs={{0,96},{16,112},{32,64},{48,80},{64,32},{80,48},{96,0},{112,16},{1... | collective-permute-start | bytes 737288 | tf_op jit(solution)/shard_map/ppermute | solution.py:287
  (13 other events, 23.0 us)
where the time goes:
time: 153 us
  waiting for transfers between devices  67.8 us (44%)
  starting transfers between devices  39.7 us (26%)
  Pallas kernels  31.7 us (21%)
  local copies, waits for them, and re-layouts  9 us (6%)
  other arithmetic  4.12 us (3%)
    ppermute x18, waiting for transfers between devices, on_aux(): return lax.ppermute(value, 'aux', pairs)  34.9 us
    ppermute x18, waiting for transfers between devices, on_virt(): return lax.ppermute(value, 'virt', pairs)  32.9 us
    ppermute x18, starting transfers between devices, on_virt(): return lax.ppermute(value, 'virt', pairs)  24 us
    ppermute x18, starting transfers between devices, on_aux(): return lax.ppermute(value, 'aux', pairs)  15.7 us
    pallas_call x4, Pallas kernels, pair_part(): pl.pallas_call(pair_kernel, out_shape=(jax.ShapeDtypeStruct((OCC * VL, OC...  10.5 us
    pallas_call x3, Pallas kernels, density_part(): pl.pallas_call(density_first_kernel if before is None else density_next_k...  9.53 us
    unnamed x50, local copies, waits for them, and re-layouts  8.21 us
    pallas_call x2, Pallas kernels, fitted_part(): pl.pallas_call(fitted_kernel, out_shape=(piece, piece), in_specs=[pl.Bloc...  6.19 us
  transfers between devices with their start and end apart: 36, of which 12 were waited for; matrix products, arithmetic and copies ran while one was open for 3% of the time, Pallas kernels for 15%

commit v1 on v0

v1 whole, which is shorter than its diff:
```python
import jax
import jax.numpy as jnp
from jax import lax
from jax.experimental import pallas as pl
from jax.experimental.pallas import tpu as pltpu
from jax.sharding import PartitionSpec as P


F32 = jnp.float32
BF16 = jnp.bfloat16
OCC = 6
VL = 64
QL = 320
QH = 1280
QT = QH // 128


def plane(step_z, step_x):
    return [(z * 4 + x, (z ^ step_z) * 4 + (x ^ step_x)) for z in range(4) for x in range(4)]


def column(place, swap):
    return [(y * 2 + c, place(y) * 2 + (c ^ swap)) for y in range(4) for c in range(2)]


XA, XB = plane(0, 1), plane(0, 3)
ZA, ZB = plane(1, 0), plane(3, 0)
YA = column(lambda y: y ^ 1, 0)
YB = column(lambda y: y ^ 3, 0)
Y2 = column(lambda y: y ^ 2, 0)
CORE = column(lambda y: y, 1)


def split(value):
    high = value.astype(BF16)
    return high, (value - high.astype(F32)).astype(BF16)


def product(left, right, dims):
    left_high, left_low = left
    right_high, right_low = right

    def one(a, b):
        return lax.dot_general(a, b, (dims, ((), ())), preferred_element_type=F32)

    return one(left_high, right_low) + one(left_low, right_high) + one(left_high, right_high)


def half_turn(value):
    return pltpu.roll(value, 64, 1)


def lanes(rows):
    return lax.broadcasted_iota(jnp.int32, (rows, 128), 1) < 64


VMEM_SPEC = pl.BlockSpec(memory_space=pltpu.VMEM)
SMEM_SPEC = pl.BlockSpec(memory_space=pltpu.SMEM)
HBM_SPEC = pl.BlockSpec(memory_space=pltpu.HBM)
PIECE = (OCC, QT, 8, 128)
PART = (OCC * VL, QH)
FLOPS = 2 * 3 * (OCC * VL) ** 2 * QH


def settings(mebibytes):
    return pltpu.CompilerParams(vmem_limit_bytes=mebibytes * 2**20)


def cost(flops):
    return pl.CostEstimate(flops=flops, bytes_accessed=4 * 2**20, transcendentals=0)


def near_memory(shape, kind=F32):
    return pltpu.VMEM(shape, kind)


def held(*values):
    return [pltpu.with_memory_space_constraint(v, pltpu.VMEM) for v in values]


def fitted_kernel(places, integrals, metric, sent, kept, left, right, full, arrivals):
    core = places[0]
    start = pl.multiple_of(256 * core, 128)
    copies = [pltpu.make_async_copy(integrals, left, arrivals.at[4])]
    for y in range(4):
        columns = metric.at[:, pl.ds(pl.multiple_of(640 * y + start, 128), 384)]
        copies.append(pltpu.make_async_copy(columns, right.at[y], arrivals.at[y]))
    for copy in copies:
        copy.start()
    copies[0].wait()
    rows = left[...].reshape(OCC * VL, QL)
    main_high, main_low = split(rows[:, :256])
    rest_high, rest_low = split(rows[:, 256:])
    rest = jnp.concatenate([rest_high, rest_low, rest_high], axis=1)
    side = pl.multiple_of(128 * core, 128)
    other = pl.multiple_of(256 - 256 * core, 128)
    low = lanes(QL)

    def put(columns, at):
        high, low_part = split(columns)
        value = product((main_high, main_low), (high[:256], low_part[:256]), ((1,), (0,)))
        ends = jnp.concatenate([low_part[256:], high[256:], high[256:]], axis=0)
        value = value + jnp.dot(rest, ends, preferred_element_type=F32)
        full[:, :, :, :, at : at + 256] = value.reshape(OCC, 4, 2, 8, 256)

    rests = []
    for y in range(4):
        copies[1 + y].wait()
        put(right[y, :, pl.ds(side, 256)], 256 * y)
        rests.append(right[y, :, pl.ds(other, 128)])
    packed = []
    for p in range(2):
        first, second = rests[2 * p], rests[2 * p + 1]
        even = jnp.where(low, first, half_turn(second))
        odd = jnp.where(low, half_turn(first), second)
        packed.append(jnp.where(core == 0, even, odd))
    put(jnp.concatenate(packed, axis=1), 1024)
    y_a, y_b, y_far, y_own = places[1], places[2], places[3], places[4]
    for target, half, slot, y in (
        (sent, 0, 0, y_a), (sent, 0, 1, y_far), (sent, 1, 0, y_b), (sent, 1, 1, y_far),
        (kept, 0, 0, y_own), (kept, 0, 1, y_b), (kept, 1, 0, y_own), (kept, 1, 1, y_a),
    ):
        for i in range(OCC):
            for q in range(QT):
                target[half, slot, i, q] = full[i, y, half, :, 128 * q : 128 * q + 128]


def fitted_part(places, integrals, metric):
    piece = near_memory((2, 2, *PIECE))
    return pl.pallas_call(
        fitted_kernel,
        out_shape=(piece, piece),
        in_specs=[SMEM_SPEC, HBM_SPEC, HBM_SPEC],
        out_specs=(VMEM_SPEC,) * 2,
        scratch_shapes=[
            pltpu.VMEM((OCC, VL, QL), F32),
            pltpu.VMEM((4, QL, 384), F32),
            pltpu.VMEM((OCC, 4, 2, 8, QH), F32),
            pltpu.SemaphoreType.DMA((5,)),
        ],
        compiler_params=settings(12),
        cost_estimate=cost(FLOPS // 3),
    )(places, integrals, metric)


def small_call(kernel, shapes, args):
    return pl.pallas_call(
        kernel,
        out_shape=tuple(near_memory(shape) for shape in shapes),
        in_specs=[VMEM_SPEC] * len(args),
        out_specs=(VMEM_SPEC,) * len(shapes),
        compiler_params=settings(4),
        cost_estimate=cost(FLOPS // 40),
    )(*held(*args))


def sent_kernel(own, other, near_0, near_1, far_0, far_1):
    for half, near, far in ((0, near_0, far_0), (1, near_1, far_1)):
        near[...] = own[half, 0] + other[half, 0]
        far[...] = own[half, 1] + other[half, 1]


def relay_kernel(half):
    def kernel(own, other, far, result):
        result[...] = own[half, 1] + other[half, 1] + far[...]

    return kernel


def shard_kernel(own, other, near_0, near_1, last_0, last_1, result):
    for half, near, last in ((0, near_0, last_0), (1, near_1, last_1)):
        result[half] = own[half, 0] + other[half, 0] + near[...] + last[...]


def line_kernel(half):
    def kernel(first, second, line):
        line[0], line[1] = first[half], second[half]

    return kernel


def join_kernel(half):
    def kernel(near, far, result):
        result[0], result[1] = near[half], far[...]

    return kernel


def pick_kernel(half):
    def kernel(value, result):
        result[...] = value[half]

    return kernel


def final_relay_kernel(kept, far, result):
    result[...] = kept[1] + far[...]


def store_split(high, low, row, q, first, second):
    value = jnp.concatenate([first, second], axis=0)
    upper, lower = split(value)
    high[row : row + 16, 128 * q : 128 * q + 128] = upper
    low[row : row + 16, 128 * q : 128 * q + 128] = lower


def rows_kernel(own, near_a, near_b, far, high, low):
    for i in range(OCC):
        for k, ref in enumerate((own, near_a, near_b, far)):
            for q in range(QT):
                store_split(high, low, (i * 4 + k) * 16, q, ref[0, i, q], ref[1, i, q])


def rows_part(*rows):
    return pl.pallas_call(
        rows_kernel,
        out_shape=(near_memory(PART, BF16),) * 2,
        in_specs=[VMEM_SPEC] * 4,
        out_specs=(VMEM_SPEC,) * 2,
        compiler_params=settings(4),
        cost_estimate=cost(FLOPS // 8),
        name="rows",
    )(*held(*rows))


def pair_kernel(left_high, left_low, *refs):
    cols = refs[:-3]
    result, high, low = refs[-3:]
    blocks = []
    for ref in cols:
        blocks += [(ref, ())] if len(ref.shape) == 4 else [(ref, (0,)), (ref, (1,))]
    count = len(blocks) // 2
    for i in range(OCC):
        for k in range(count):
            (one, at_one), (two, at_two) = blocks[2 * k], blocks[2 * k + 1]
            for q in range(QT):
                store_split(high, low, (i * count + k) * 16, q, one[(*at_one, i, q)], two[(*at_two, i, q)])
    left = left_high[...], left_low[...]
    result[...] = product(left, (high[...], low[...]), ((1,), (1,)))


def pair_part(left, cols):
    width = 48 * sum(1 if c.ndim == 4 else 2 for c in cols)
    part = near_memory((width, QH), BF16)
    return pl.pallas_call(
        pair_kernel,
        out_shape=(near_memory((OCC * VL, width)), part, part),
        in_specs=[VMEM_SPEC] * (2 + len(cols)),
        out_specs=(VMEM_SPEC,) * 3,
        compiler_params=settings(12),
        cost_estimate=cost(FLOPS),
    )(*held(*left, *cols))


def amplitudes(pair, row_term, col_term):
    low = lanes(VL)
    pieces = []
    for i in range(OCC):
        at = 128 * (i // 2)
        swapped = []
        if pair.shape[1] == 2 * OCC * VL:
            swapped = [pair[VL * j : VL * j + VL, 128 * i : 128 * i + 128] for j in range(OCC)]
        for t in range(0 if swapped else OCC // 2):
            first = pair[2 * t * VL : 2 * t * VL + VL, at : at + 128]
            second = pair[(2 * t + 1) * VL : (2 * t + 2) * VL, at : at + 128]
            if i % 2 == 0:
                second = half_turn(second)
            else:
                first = half_turn(first)
            swapped.append(jnp.where(low, first, second))
        direct = pair[VL * i : VL * i + VL, :]
        levels = row_term[VL * i : VL * i + VL, :] + col_term
        pieces.append((2.0 * direct - jnp.concatenate(swapped, axis=1)) / levels)
    return jnp.concatenate(pieces, axis=0)


def density_term(own, other, row_term, col_term, high, low):
    amplitude = amplitudes(own[...] + other[...], row_term[...], col_term[...])
    return product(split(amplitude), (high[...], low[...]), ((1,), (0,)))


def density_first_kernel(*refs):
    refs[-1][...] = density_term(*refs[:-1])


def density_next_kernel(*refs):
    refs[-1][...] = refs[-2][...] + density_term(*refs[:-2])


def density_part(inputs, before):
    args = inputs if before is None else (*inputs, before)
    return pl.pallas_call(
        density_first_kernel if before is None else density_next_kernel,
        out_shape=near_memory(PART),
        in_specs=[VMEM_SPEC] * len(args),
        out_specs=VMEM_SPEC,
        compiler_params=settings(10),
        cost_estimate=cost(FLOPS),
    )(*held(*args))


def density_last_kernel(places, *refs):
    before, near_0, near_1, far_0, far_1, kept_0, kept_1, whole = refs[6:]
    term = before[...] + density_term(*refs[:6])
    order = (places[4], places[1], places[2], places[3])
    for q in range(QT):
        for i in range(OCC):
            for k in range(4):
                row = (i * 4 + k) * 16
                whole[q, i, order[k]] = term[row : row + 16, 128 * q : 128 * q + 128]
    low = lanes(32)
    for target, start, k in (
        (far_0, 0, 3), (far_1, 3, 3), (near_0, 0, 1), (near_1, 3, 2),
        (kept_0.at[0], 0, 0), (kept_0.at[1], 0, 2), (kept_1.at[0], 3, 0), (kept_1.at[1], 3, 1),
    ):
        y = order[k]
        for i in range(3):
            for q in range(2):
                row = (q * 3 + i) * VL
                target[row : row + VL, :] = whole[2 * y + q, start + i].reshape(VL, 128)
            rest = whole[8 + (y >> 1), start + i].reshape(VL, 128)
            rest = jnp.where((y & 1) == 1, half_turn(rest), rest)
            row = 6 * VL + 32 * i
            target[row : row + 32, :] = jnp.where(low, rest[:32], half_turn(rest[32:]))


def density_last(places, inputs, before):
    piece, two = near_memory((480, 128)), near_memory((2, 480, 128))
    return pl.pallas_call(
        density_last_kernel,
        out_shape=(piece,) * 4 + (two,) * 2,
        in_specs=[SMEM_SPEC] + [VMEM_SPEC] * 7,
        out_specs=(VMEM_SPEC,) * 6,
        scratch_shapes=[pltpu.VMEM((QT, OCC, 4, 16, 128), F32)],
        compiler_params=settings(12),
        cost_estimate=cost(FLOPS),
    )(places, *held(*inputs, before))


def unpack_kernel(places, kept_0, near_0, last_0, kept_1, near_1, last_1, result):
    low = lanes(VL)
    for half, refs in enumerate(((kept_0, near_0, last_0), (kept_1, near_1, last_1))):
        kept, near, last = refs
        total = kept[0] + near[...] + last[...]
        for i in range(3):
            first = total[i * VL : i * VL + VL]
            second = total[(3 + i) * VL : (4 + i) * VL]
            packed = total[6 * VL + 32 * i : 6 * VL + 32 * i + 32]
            rest = jnp.concatenate([packed, half_turn(packed)], axis=0)
            first_turned, second_turned = half_turn(first), half_turn(second)
            zero = places[0] == 0
            at = half * 3 + i
            result[at, :, 0:128] = jnp.where(zero, first, jnp.where(low, rest, first_turned))
            result[at, :, 128:256] = jnp.where(zero, second, jnp.where(low, first_turned, second_turned))
            result[at, :, 256:320] = jnp.where(zero, rest, second_turned)[:, :64]


def unpack(places, *parts):
    return pl.pallas_call(
        unpack_kernel,
        out_shape=jax.ShapeDtypeStruct((OCC, VL, QL), F32),
        in_specs=[SMEM_SPEC] + [VMEM_SPEC] * 6,
        out_specs=VMEM_SPEC,
        compiler_params=settings(4),
        name="unpack",
    )(places, *held(*parts))


def on_virt(value, pairs):
    return lax.ppermute(value, "virt", pairs)


def on_aux(value, pairs):
    return lax.ppermute(value, "aux", pairs)


SPOTS = (
    (0, 1, 0), (0, 1, 1), (0, 3, 0), (0, 3, 1), (1, 0, 0), (1, 0, 1), (3, 0, 0), (3, 0, 1),
    (1, 1, 0), (1, 3, 0), (3, 1, 0), (3, 3, 0), (1, 1, 1), (3, 1, 1), (1, 3, 1), (3, 3, 1),
    (0, 0, 0), (0, 0, 1), (0, 2, 0), (2, 0, 1), (1, 2, 0), (3, 2, 0), (2, 1, 1), (2, 3, 1),
    (2, 1, 0), (2, 3, 0), (1, 2, 1), (3, 2, 1), (2, 0, 0), (2, 2, 0), (0, 2, 1), (2, 2, 1),
)


def terms_kernel(places, batch_index, occ_energy, virt_energy, virt_order, row_term, *col_terms):
    z, x = places[5], places[6]
    chips = (places[4], places[1], places[2], places[3])
    lane = lax.broadcasted_iota(jnp.int32, (8, 128), 1).astype(F32)
    step = lax.broadcasted_iota(jnp.int32, (8, 128), 0).astype(F32)
    order = virt_order[...].astype(F32)

    def pick(table, at):
        total = jnp.zeros((8, 128), F32)
        for r in range(8):
            total = total + jnp.where(at == lane + 128.0 * r, table[r : r + 1, :], 0.0)
        return jnp.sum(total, axis=1, keepdims=True)

    spots = [(z * 4 + x, chips[r], h) for r in range(4) for h in range(2)]
    spots += [((z ^ dz) * 4 + (x ^ dx), chips[0], h) for dz, dx, h in SPOTS]
    levels = []
    for place, chip, half in spots:
        first = (place * VL + chip * 16 + half * 8).astype(F32)
        levels.append(pick(virt_energy[...], pick(order, first + step)))
    occ = [occ_energy[batch_index[i]] for i in range(OCC)]
    rows = jnp.concatenate(levels[:8], axis=0)
    for i in range(OCC):
        row_term[VL * i : VL * i + VL, :] = occ[i] - rows
    low = lax.broadcasted_iota(jnp.int32, (1, 128), 1) < 64
    first, second, third = col_terms

    def along(values):
        both = jnp.concatenate(values, axis=0)
        flat = jnp.broadcast_to(both, (128, 128)).T[:8]
        return flat[:1], half_turn(flat)[:1]

    flat, turned = along(levels[16:32])
    for i in range(OCC):
        second[:, 128 * i : 128 * i + 128] = occ[i] - flat
    flat, turned = along(levels[8:16] + levels[32:40])
    for target, value in ((first, jnp.where(low, flat, turned)), (third, jnp.where(low, turned, flat))):
        for t in range(3):
            target[:, 128 * t : 128 * t + 128] = jnp.where(low, occ[2 * t], occ[2 * t + 1]) - value


def energy_terms(places, batch_index, occ_energy, virt_energy, virt_order):
    column = near_memory((1, OCC * VL))
    return pl.pallas_call(
        terms_kernel,
        out_shape=(near_memory((OCC * VL, 1)), column, near_memory((1, 2 * OCC * VL)), column),
        in_specs=[SMEM_SPEC] * 3 + [VMEM_SPEC] * 2,
        out_specs=(VMEM_SPEC,) * 4,
        compiler_params=settings(4),
        cost_estimate=cost(FLOPS // 4),
        name="terms",
    )(places, batch_index, occ_energy, virt_energy.reshape(8, 128), virt_order.reshape(8, 128))


def shards(integrals, metric_root, occ_energy, virt_energy, batch_index, virt_order):
    aux_place = lax.axis_index("aux").astype(jnp.int32)
    virt_place = lax.axis_index("virt").astype(jnp.int32)
    y, core = aux_place >> 1, aux_place & 1
    z, x = virt_place >> 2, virt_place & 3
    near = [y ^ 1, y ^ 3, y ^ 2, y, z, x]
    places = jnp.stack([core, *near])
    partner_places = jnp.stack([1 - core, *near])

    values = pltpu.with_memory_space_constraint(integrals.transpose(1, 0, 2), pltpu.HBM)
    metric = pltpu.with_memory_space_constraint(metric_root.T, pltpu.HBM)
    out_sent, out_kept = fitted_part(partner_places, values, metric)
    in_sent = on_aux(out_sent, CORE)
    in_kept = on_aux(out_kept, CORE)
    own_sent, own_kept = fitted_part(places, values, metric)
    near_0, near_1, far_0, far_1 = small_call(sent_kernel, (PIECE,) * 4, (own_sent, in_sent))
    far_0, far_1 = on_aux(far_0, YA), on_aux(far_1, YB)
    near_0, near_1 = on_aux(near_0, YA), on_aux(near_1, YB)
    row_term, *col_terms = energy_terms(places, batch_index, occ_energy, virt_energy, virt_order)
    (last_0,) = small_call(relay_kernel(0), (PIECE,), (own_kept, in_kept, far_0))
    last_0 = on_aux(last_0, YB)
    (last_1,) = small_call(relay_kernel(1), (PIECE,), (own_kept, in_kept, far_1))
    last_1 = on_aux(last_1, YA)
    last_1, row_term, col_terms = lax.optimization_barrier((last_1, row_term, col_terms))
    parts = (own_kept, in_kept, near_0, near_1, last_0, last_1)
    (own,) = small_call(shard_kernel, ((2, *PIECE),), parts)

    s_xa, s_xb = on_virt(own, XA), on_virt(own, XB)
    s_za, s_zb = on_virt(own, ZA), on_virt(own, ZB)
    row_a, row_b = on_aux(own, YA), on_aux(own, YB)
    (beyond_a,) = small_call(pick_kernel(0), (PIECE,), (s_xa,))
    (beyond_b,) = small_call(pick_kernel(1), (PIECE,), (s_za,))
    a_2, b_2 = on_virt(beyond_a, XB), on_virt(beyond_b, ZB)
    row_2 = on_aux(own, Y2)

    (line_a,) = small_call(line_kernel(0), ((2, *PIECE),), (s_xa, s_xb))
    pa_a, pa_b = on_virt(line_a, ZA), on_virt(line_a, ZB)
    (line_b,) = small_call(line_kernel(1), ((2, *PIECE),), (s_za, s_zb))
    pb_a, pb_b = on_virt(line_b, XA), on_virt(line_b, XB)
    qa_b, qa_a = on_virt(a_2, ZB), on_virt(a_2, ZA)
    qb_b, qb_a = on_virt(b_2, XB), on_virt(b_2, XA)
    pa_2, pb_2 = on_virt(pa_a, ZB), on_virt(pb_a, XB)
    (both_a,) = small_call(join_kernel(0), ((2, *PIECE),), (s_zb, qa_b))
    (both_b,) = small_call(join_kernel(1), ((2, *PIECE),), (s_xb, qb_b))
    f_a, f_b = on_virt(both_a, ZA), on_virt(both_b, XA)

    left = rows_part(own, row_a, row_b, row_2)
    chunks = (
        (s_xa, s_xb, s_za, s_zb),
        (pa_a, pa_b, pb_a, pb_b, own, a_2, b_2, qa_a, qa_b, qb_a, qb_b),
        (pa_2, pb_2, f_a, f_b),
    )
    total = None
    for k, cols in enumerate(chunks):
        pair, high, low = pair_part(left, cols)
        other = on_aux(pair, CORE)
        inputs = (pair, other, row_term, col_terms[k], high, low)
        if k < 2:
            total = density_part(inputs, total)
    near_0, near_1, far_0, far_1, kept_0, kept_1 = density_last(places, inputs, total)
    far_0, far_1 = on_aux(far_0, YA), on_aux(far_1, YB)
    near_0, near_1 = on_aux(near_0, YA), on_aux(near_1, YB)
    (last_0,) = small_call(final_relay_kernel, ((480, 128),), (kept_0, far_0))
    last_0 = on_aux(last_0, YB)
    (last_1,) = small_call(final_relay_kernel, ((480, 128),), (kept_1, far_1))
    last_1 = on_aux(last_1, YA)
    result = unpack(places, kept_0, near_0, last_0, kept_1, near_1, last_1)
    return result.transpose(1, 0, 2)


def solution(mesh):
    return jax.shard_map(
        shards,
        mesh=mesh,
        in_specs=(P("virt", None, "aux"), P(None, "aux"), P(), P(), P(), P()),
        out_specs=P("virt", None, "aux"),
        check_vma=False,
    )
```

time: 153 us -> 131 us (0.86)
  waiting for transfers between devices: 67.8 us -> 53.7 us
  starting transfers between devices: 39.7 us -> 50.1 us
  local copies, waits for them, and re-layouts: 9 us -> 0.18 us
  Pallas kernels: 31.7 us -> 26.6 us
  other arithmetic: 4.12 us -> 0 us
    unnamed x50 -> x8, local copies, waits for them, and re-layouts: 8.21 us -> 0.01 us
    ppermute x18, starting transfers between devices: 24 us -> 31.8 us  [on_virt(): return lax.ppermute(value, 'virt', pairs)]
    ppermute x18 -> x20, waiting for transfers between devices: 34.9 us -> 27.3 us  [on_aux(): return lax.ppermute(value, 'aux', pairs)]
    ppermute x18, waiting for transfers between devices: 32.9 us -> 26.4 us  [on_virt(): return lax.ppermute(value, 'virt', pairs)]
    pallas_call x3 -> x2, Pallas kernels: 9.53 us -> 4.61 us  [density_part(): pl.pallas_call(density_first_kernel if before is None else density_next_k...]
    add x9 -> x0, other arithmetic: 3.06 us -> none  [the longest x1 1.58 us: shards(): kept_0, kept_1 = (own_kept[0] + in_kept[0], own_kept[1] + in_kept[1])]
    ppermute x18 -> x20, starting transfers between devices: 15.7 us -> 18.3 us  [on_aux(): return lax.ppermute(value, 'aux', pairs)]
    pallas_call x8 -> x20, Pallas kernels: 20.6 us -> 20.4 us  [the longest x2 9.38 us: fitted_part(): pl.pallas_call(fitted_kernel, out_shape=(piece, piece), in_specs=[SMEM_SP...]
  transfers between devices with their start and end apart: 36 -> 38, of which waited for: 12 -> 18; matrix products, arithmetic and copies ran while one was open for 3% -> 0% of each run, Pallas kernels for 15% -> 13%
where the time goes in v1:
time: 131 us
  waiting for transfers between devices  53.7 us (41%)
  starting transfers between devices  50.1 us (38%)
  Pallas kernels  26.6 us (20%)
    ppermute x18, starting transfers between devices, on_virt(): return lax.ppermute(value, 'virt', pairs)  31.8 us
    ppermute x20, waiting for transfers between devices, on_aux(): return lax.ppermute(value, 'aux', pairs)  27.3 us
    ppermute x18, waiting for transfers between devices, on_virt(): return lax.ppermute(value, 'virt', pairs)  26.4 us
    ppermute x20, starting transfers between devices, on_aux(): return lax.ppermute(value, 'aux', pairs)  18.3 us
    pallas_call x2, Pallas kernels, fitted_part(): pl.pallas_call(fitted_kernel, out_shape=(piece, piece), in_specs=[SMEM_SP...  9.38 us
    pallas_call x3, Pallas kernels, pair_part(): pl.pallas_call(pair_kernel, out_shape=(near_memory((OCC * VL, width)), pa...  6.19 us
    pallas_call x2, Pallas kernels, density_part(): pl.pallas_call(density_first_kernel if before is None else density_next_k...  4.61 us
    pallas_call x1, Pallas kernels, density_last(): pl.pallas_call(density_last_kernel, out_shape=(piece,) * 4 + (two,) * 2,...  2.95 us
  transfers between devices with their start and end apart: 38, of which 18 were waited for; matrix products, arithmetic and copies ran while one was open for 0% of the time, Pallas kernels for 13%

profile of v1, /device:TPU:0, one launch (start us, length us, event | category | flops | bytes accessed | tf_op | source)
XLA Modules:
  0.0 130.9 jit_solution(3336212426501716839)
XLA Ops:
  0.1 5.2 %shard_map.65 = (f32[2,2,6,10,8,128]{5,4,3,2,1,0:T(8,128)}, f32[2,2,6,10,8,128]{5,4,3,2,1,0:T(8,128)S(1)}) custom-call(s32[7]{0:T(128)S(1)} %stack.45.places, f32[6,64,320]{2,1,0:T(8,128)} %bitcast.17, f32[320,2560]{1,0:T(8,128)} %bitcast.15), custom_call_target="tpu_custom_call" | custom-call | flops 377487360 | bytes 4194304 | tf_op jit(solution)/shard_map/pallas_call | solution.py:130
  6.0 4.2 %shard_map.64 = (f32[2,2,6,10,8,128]{5,4,3,2,1,0:T(8,128)S(1)}, f32[2,2,6,10,8,128]{5,4,3,2,1,0:T(8,128)S(1)}) custom-call(s32[7]{0:T(128)S(1)} %stack.43.places, f32[6,64,320]{2,1,0:T(8,128)} %bitcast.18, f32[320,2560]{1,0:T(8,128)} %bitcast.16), custom_call_target="tpu_custom_call" | custom-call | flops 377487360 | bytes 4194304 | tf_op jit(solution)/shard_map/pallas_call | solution.py:130
  10.3 3.2 %collective-permute-start.6 = (f32[6,10,8,128]{3,2,1,0:T(8,128)S(1)}, f32[6,10,8,128]{3,2,1,0:T(8,128)S(1)}, u32[]{:S(2)}, u32[]{:S(2)}) collective-permute-start(f32[6,10,8,128]{3,2,1,0:T(8,128)S(1)} %get-tuple-element.46), channel_id=1, source_target_pairs={{0,96},{16,112},{32,64},{48,80},{64,32},{80,48},{96,0},{112,16},{1... | collective-permute-start | bytes 737288 | tf_op jit(solution)/shard_map/ppermute | solution.py:374
  13.6 1.9 %collective-permute-start.2 = (f32[6,10,8,128]{3,2,1,0:T(8,128)S(1)}, f32[6,10,8,128]{3,2,1,0:T(8,128)S(1)}, u32[]{:S(2)}, u32[]{:S(2)}) collective-permute-start(f32[6,10,8,128]{3,2,1,0:T(8,128)S(1)} %get-tuple-element.43), channel_id=1, source_target_pairs={{0,32},{16,48},{32,0},{48,16},{64,96},{80,112},{96,64},{112,80},{1... | collective-permute-start | bytes 737288 | tf_op jit(solution)/shard_map/ppermute | solution.py:374
  15.6 4.8 %collective-permute-done.6.far = f32[6,10,8,128]{3,2,1,0:T(8,128)S(1)} collective-permute-done((f32[6,10,8,128]{3,2,1,0:T(8,128)S(1)}, f32[6,10,8,128]{3,2,1,0:T(8,128)S(1)}, u32[]{:S(2)}, u32[]{:S(2)}) %collective-permute-start.6) | collective-permute-done | bytes 245792 | tf_op jit(solution)/shard_map/ppermute | solution.py:374
  21.0 1.3 %collective-permute-done.4.far = f32[6,10,8,128]{3,2,1,0:T(8,128)S(1)} collective-permute-done((f32[6,10,8,128]{3,2,1,0:T(8,128)S(1)}, f32[6,10,8,128]{3,2,1,0:T(8,128)S(1)}, u32[]{:S(2)}, u32[]{:S(2)}) %collective-permute-start.4) | collective-permute-done | bytes 245792 | tf_op jit(solution)/shard_map/ppermute | solution.py:374
  22.4 1.5 %collective-permute-start.5 = (f32[6,10,8,128]{3,2,1,0:T(8,128)S(1)}, f32[6,10,8,128]{3,2,1,0:T(8,128)S(1)}, u32[]{:S(2)}, u32[]{:S(2)}) collective-permute-start(f32[6,10,8,128]{3,2,1,0:T(8,128)S(1)} %shard_map.67), channel_id=1, source_target_pairs={{0,96},{16,112},{32,64},{48,80},{64,32},{80,48},{96,0},{112,16},{1... | collective-permute-start | bytes 737288 | tf_op jit(solution)/shard_map/ppermute | solution.py:374
  23.8 1.1 terms.1
  24.9 6.8 %collective-permute-done.7.last_1 = f32[6,10,8,128]{3,2,1,0:T(8,128)S(1)} collective-permute-done((f32[6,10,8,128]{3,2,1,0:T(8,128)S(1)}, f32[6,10,8,128]{3,2,1,0:T(8,128)S(1)}, u32[]{:S(2)}, u32[]{:S(2)}) %collective-permute-start.7) | collective-permute-done | bytes 245792 | tf_op jit(solution)/shard_map/ppermute | solution.py:374
  31.8 1.6 %collective-permute-start.11 = (f32[2,6,10,8,128]{4,3,2,1,0:T(8,128)S(1)}, f32[2,6,10,8,128]{4,3,2,1,0:T(8,128)S(1)}, u32[]{:S(2)}, u32[]{:S(2)}) collective-permute-start(f32[2,6,10,8,128]{4,3,2,1,0:T(8,128)S(1)} %shard_map.69.own.refs_4_), channel_id=1, source_target_pairs={{0,1},{1,0},{2,3},{3,2},{4,5},{5,4},{6,7},{7,6},{8,9},{9,8},{10,11... | collective-permute-start | bytes 1474568 | tf_op jit(solution)/shard_map/ppermute | solution.py:370
  33.4 1.9 %collective-permute-start.15 = (f32[2,6,10,8,128]{4,3,2,1,0:T(8,128)S(1)}, f32[2,6,10,8,128]{4,3,2,1,0:T(8,128)S(1)}, u32[]{:S(2)}, u32[]{:S(2)}) collective-permute-start(f32[2,6,10,8,128]{4,3,2,1,0:T(8,128)S(1)} %shard_map.69.own.refs_4_), channel_id=1, source_target_pairs={{0,4},{1,5},{2,6},{3,7},{4,0},{5,1},{6,2},{7,3},{8,12},{9,13},{10,... | collective-permute-start | bytes 1474568 | tf_op jit(solution)/shard_map/ppermute | solution.py:370
  35.3 2.1 %collective-permute-start.12 = (f32[2,6,10,8,128]{4,3,2,1,0:T(8,128)S(1)}, f32[2,6,10,8,128]{4,3,2,1,0:T(8,128)S(1)}, u32[]{:S(2)}, u32[]{:S(2)}) collective-permute-start(f32[2,6,10,8,128]{4,3,2,1,0:T(8,128)S(1)} %shard_map.69.own.refs_4_), channel_id=1, source_target_pairs={{0,3},{1,2},{2,1},{3,0},{4,7},{5,6},{6,5},{7,4},{8,11},{9,10},{10,... | collective-permute-start | bytes 1474568 | tf_op jit(solution)/shard_map/ppermute | solution.py:370
  37.4 2.5 %collective-permute-start.16 = (f32[2,6,10,8,128]{4,3,2,1,0:T(8,128)S(1)}, f32[2,6,10,8,128]{4,3,2,1,0:T(8,128)S(1)}, u32[]{:S(2)}, u32[]{:S(2)}) collective-permute-start(f32[2,6,10,8,128]{4,3,2,1,0:T(8,128)S(1)} %shard_map.69.own.refs_4_), channel_id=1, source_target_pairs={{0,12},{1,13},{2,14},{3,15},{4,8},{5,9},{6,10},{7,11},{8,4},{9,5},... | collective-permute-start | bytes 1474568 | tf_op jit(solution)/shard_map/ppermute | solution.py:370
  39.9 0.6 collective-permute-start.10
  40.6 3.4 %collective-permute-done.11.first.value.refs_0_ = f32[2,6,10,8,128]{4,3,2,1,0:T(8,128)S(1)} collective-permute-done((f32[2,6,10,8,128]{4,3,2,1,0:T(8,128)S(1)}, f32[2,6,10,8,128]{4,3,2,1,0:T(8,128)S(1)}, u32[]{:S(2)}, u32[]{:S(2)}) %collective-permute-start.11) | collective-permute-done | bytes 491552 | tf_op jit(solution)/shard_map/ppermute | solution.py:370
  44.4 0.9 collective-permute-done.15.first.value.refs_2_
  45.4 1.8 %collective-permute-start.9 = (f32[2,6,10,8,128]{4,3,2,1,0:T(8,128)S(1)}, f32[2,6,10,8,128]{4,3,2,1,0:T(8,128)S(1)}, u32[]{:S(2)}, u32[]{:S(2)}) collective-permute-start(f32[2,6,10,8,128]{4,3,2,1,0:T(8,128)S(1)} %shard_map.69.own.refs_4_), channel_id=1, source_target_pairs={{0,96},{16,112},{32,64},{48,80},{64,32},{80,48},{96,0},{112,16},{1... | collective-permute-start | bytes 1474568 | tf_op jit(solution)/shard_map/ppermute | solution.py:374
  47.1 0.9 collective-permute-done.12.second.near.refs_1_
  48.0 2.1 %collective-permute-start.19 = (f32[6,10,8,128]{3,2,1,0:T(8,128)S(1)}, f32[6,10,8,128]{3,2,1,0:T(8,128)S(1)}, u32[]{:S(2)}, u32[]{:S(2)}) collective-permute-start(f32[6,10,8,128]{3,2,1,0:T(8,128)S(1)} %shard_map.72), channel_id=1, source_target_pairs={{0,3},{1,2},{2,1},{3,0},{4,7},{5,6},{6,5},{7,4},{8,11},{9,10},{10,... | collective-permute-start | bytes 737288 | tf_op jit(solution)/shard_map/ppermute | solution.py:370
  50.1 3.1 %collective-permute-start.22 = (f32[6,10,8,128]{3,2,1,0:T(8,128)S(1)}, f32[6,10,8,128]{3,2,1,0:T(8,128)S(1)}, u32[]{:S(2)}, u32[]{:S(2)}) collective-permute-start(f32[6,10,8,128]{3,2,1,0:T(8,128)S(1)} %shard_map.74), channel_id=1, source_target_pairs={{0,12},{1,13},{2,14},{3,15},{4,8},{5,9},{6,10},{7,11},{8,4},{9,5},... | collective-permute-start | bytes 737288 | tf_op jit(solution)/shard_map/ppermute | solution.py:370
  53.2 2.2 %collective-permute-done.19.refs_5_ = f32[6,10,8,128]{3,2,1,0:T(8,128)S(1)} collective-permute-done((f32[6,10,8,128]{3,2,1,0:T(8,128)S(1)}, f32[6,10,8,128]{3,2,1,0:T(8,128)S(1)}, u32[]{:S(2)}, u32[]{:S(2)}) %collective-permute-start.19) | collective-permute-done | bytes 245792 | tf_op jit(solution)/shard_map/ppermute | solution.py:370
  55.4 3.1 %collective-permute-start.20 = (f32[6,10,8,128]{3,2,1,0:T(8,128)S(1)}, f32[6,10,8,128]{3,2,1,0:T(8,128)S(1)}, u32[]{:S(2)}, u32[]{:S(2)}) collective-permute-start(f32[6,10,8,128]{3,2,1,0:T(8,128)S(1)} %collective-permute-done.19.refs_5_), channel_id=1, source_target_pairs={{0,12},{1,13},{2,14},{3,15},{4,8},{5,9},{6,10},{7,11},{8,4},{9,5},... | collective-permute-start | bytes 737288 | tf_op jit(solution)/shard_map/ppermute | solution.py:370
  58.8 1.9 %collective-permute-start.23 = (f32[6,10,8,128]{3,2,1,0:T(8,128)S(1)}, f32[6,10,8,128]{3,2,1,0:T(8,128)S(1)}, u32[]{:S(2)}, u32[]{:S(2)}) collective-permute-start(f32[6,10,8,128]{3,2,1,0:T(8,128)S(1)} %collective-permute-done.22.refs_6_), channel_id=1, source_target_pairs={{0,3},{1,2},{2,1},{3,0},{4,7},{5,6},{6,5},{7,4},{8,11},{9,10},{10,... | collective-permute-start | bytes 737288 | tf_op jit(solution)/shard_map/ppermute | solution.py:370
  60.8 1.3 collective-permute-done.8.near_a
  62.1 1.0 collective-permute-start.28
  63.0 1.1 collective-permute-start.27
  64.2 1.0 collective-permute-start.13
  65.2 1.0 collective-permute-done.23.far.refs_10_
  66.2 5.8 %collective-permute-start.26 = (f32[2,6,10,8,128]{4,3,2,1,0:T(8,128)S(1)}, f32[2,6,10,8,128]{4,3,2,1,0:T(8,128)S(1)}, u32[]{:S(2)}, u32[]{:S(2)}) collective-permute-start(f32[2,6,10,8,128]{4,3,2,1,0:T(8,128)S(1)} %shard_map.70), channel_id=1, source_target_pairs={{0,12},{1,13},{2,14},{3,15},{4,8},{5,9},{6,10},{7,11},{8,4},{9,5},... | collective-permute-start | bytes 1474568 | tf_op jit(solution)/shard_map/ppermute | solution.py:370
  72.5 8.2 %collective-permute-done.29.refs_9_ = f32[6,10,8,128]{3,2,1,0:T(8,128)S(1)} collective-permute-done((f32[6,10,8,128]{3,2,1,0:T(8,128)S(1)}, f32[6,10,8,128]{3,2,1,0:T(8,128)S(1)}, u32[]{:S(2)}, u32[]{:S(2)}) %collective-permute-start.29) | collective-permute-done | bytes 245792 | tf_op jit(solution)/shard_map/ppermute | solution.py:370
  81.0 2.6 %shard_map.77 = (f32[384,768]{1,0:T(8,128)S(1)}, bf16[768,1280]{1,0:T(8,128)(2,1)S(1)}, bf16[768,1280]{1,0:T(8,128)(2,1)S(1)}) custom-call(bf16[384,1280]{1,0:T(8,128)(2,1)S(1)} %get-tuple-element.52.left_high, bf16[384,1280]{1,0:T(8,128)(2,1)S(1)} %get-tuple-element.53.left_low, f32[2,6,10,8,128]{4,3,2,1,0:T(8,128)S(1)} %collective-permute-done.13.refs_0_, ...), custom_call_target="tpu_custom_call" | custom-call | flops 1132462080 | bytes 4194304 | tf_op jit(solution)/shard_map/pallas_call | solution.py:245
  83.9 4.0 %collective-permute-start.14 = (f32[2,6,10,8,128]{4,3,2,1,0:T(8,128)S(1)}, f32[2,6,10,8,128]{4,3,2,1,0:T(8,128)S(1)}, u32[]{:S(2)}, u32[]{:S(2)}) collective-permute-start(f32[2,6,10,8,128]{4,3,2,1,0:T(8,128)S(1)} %collective-permute-done.13.refs_0_), channel_id=1, source_target_pairs={{0,12},{1,13},{2,14},{3,15},{4,8},{5,9},{6,10},{7,11},{8,4},{9,5},... | collective-permute-start | bytes 1474568 | tf_op jit(solution)/shard_map/ppermute | solution.py:370
  87.9 1.8 %shard_map.78 = (f32[384,384]{1,0:T(8,128)S(1)}, bf16[384,1280]{1,0:T(8,128)(2,1)S(1)}, bf16[384,1280]{1,0:T(8,128)(2,1)S(1)}) custom-call(bf16[384,1280]{1,0:T(8,128)(2,1)S(1)} %get-tuple-element.52.left_high, bf16[384,1280]{1,0:T(8,128)(2,1)S(1)} %get-tuple-element.53.left_low, f32[2,6,10,8,128]{4,3,2,1,0:T(8,128)S(1)} %collective-permute-done.11.first.value.refs_0_, ...), custom_call_target="tpu_custom_call" | custom-call | flops 1132462080 | bytes 4194304 | tf_op jit(solution)/shard_map/pallas_call | solution.py:245
  89.9 7.5 %collective-permute-done.21.refs_2_ = f32[2,6,10,8,128]{4,3,2,1,0:T(8,128)S(1)} collective-permute-done((f32[2,6,10,8,128]{4,3,2,1,0:T(8,128)S(1)}, f32[2,6,10,8,128]{4,3,2,1,0:T(8,128)S(1)}, u32[]{:S(2)}, u32[]{:S(2)}) %collective-permute-start.21) | collective-permute-done | bytes 491552 | tf_op jit(solution)/shard_map/ppermute | solution.py:370
  97.4 1.3 collective-permute-done.18.refs_1_
  99.2 1.8 %shard_map.76 = (f32[384,384]{1,0:T(8,128)S(1)}, bf16[384,1280]{1,0:T(8,128)(2,1)S(1)}, bf16[384,1280]{1,0:T(8,128)(2,1)S(1)}) custom-call(bf16[384,1280]{1,0:T(8,128)(2,1)S(1)} %get-tuple-element.52.left_high, bf16[384,1280]{1,0:T(8,128)(2,1)S(1)} %get-tuple-element.53.left_low, f32[2,6,10,8,128]{4,3,2,1,0:T(8,128)S(1)} %collective-permute-done.14.refs_0_, ...), custom_call_target="tpu_custom_call" | custom-call | flops 1132462080 | bytes 4194304 | tf_op jit(solution)/shard_map/pallas_call | solution.py:245
  101.2 1.8 %shard_map.79.refs_6_ = f32[384,1280]{1,0:T(8,128)S(1)} custom-call(f32[384,384]{1,0:T(8,128)S(1)} %get-tuple-element.63.refs_0_, f32[384,384]{1,0:T(8,128)S(1)} %collective-permute-done.31.refs_1_, f32[384,1]{1,0:T(8,128)S(1)} %get-tuple-element.55.refs_2_, f32[1,384]{1,0:T(1,128)S(1)} %get-tuple-element.64.refs_3_, ...), custom_call_target="tpu_custom_call" | custom-call | flops 1132462080 | bytes 4194304 | tf_op jit(solution)/shard_map/pallas_call | solution.py:292
  103.0 2.8 %shard_map.80.refs_6_ = f32[384,1280]{1,0:T(8,128)S(1)} custom-call(f32[384,768]{1,0:T(8,128)S(1)} %get-tuple-element.59.refs_0_, f32[384,768]{1,0:T(8,128)S(1)} %collective-permute-done.30.refs_1_, f32[384,1]{1,0:T(8,128)S(1)} %get-tuple-element.55.refs_2_, f32[1,768]{1,0:T(1,128)S(1)} %get-tuple-element.60.refs_3_, ...), custom_call_target="tpu_custom_call" | custom-call | flops 1132462080 | bytes 4194304 | tf_op jit(solution)/shard_map/pallas_call | solution.py:292
  105.8 2.9 %shard_map.81 = (f32[480,128]{1,0:T(8,128)S(1)}, f32[480,128]{1,0:T(8,128)S(1)}, f32[480,128]{1,0:T(8,128)S(1)}, f32[480,128]{1,0:T(8,128)S(1)}, f32[2,480,128]{2,1,0:T(8,128)S(1)}, /*index=5*/f32[2,480,128]{2,1,0:T(8,128)S(1)}) custom-call(s32[7]{0:T(128)S(1)} %stack.43.places, f32[384,384]{1,0:T(8,128)S(1)} %get-tuple-element.54.refs_0_, ...), custom_call_target="tpu_custom_call" | custom-call | flops 1132462080 | bytes 4194304 | tf_op jit(solution)/shard_map/pallas_call | solution.py:329
  108.8 1.9 %collective-permute-start.36 = (f32[480,128]{1,0:T(8,128)S(1)}, f32[480,128]{1,0:T(8,128)S(1)}, u32[]{:S(2)}, u32[]{:S(2)}) collective-permute-start(f32[480,128]{1,0:T(8,128)S(1)} %get-tuple-element.72), channel_id=1, source_target_pairs={{0,96},{16,112},{32,64},{48,80},{64,32},{80,48},{96,0},{112,16},{1... | collective-permute-start | bytes 737288 | tf_op jit(solution)/shard_map/ppermute | solution.py:374
  110.7 0.8 collective-permute-start.33
  111.5 1.2 collective-permute-start.32
  112.7 1.4 %collective-permute-start.35 = (f32[480,128]{1,0:T(8,128)S(1)}, f32[480,128]{1,0:T(8,128)S(1)}, u32[]{:S(2)}, u32[]{:S(2)}) collective-permute-start(f32[480,128]{1,0:T(8,128)S(1)} %get-tuple-element.71), channel_id=1, source_target_pairs={{0,96},{16,112},{32,64},{48,80},{64,32},{80,48},{96,0},{112,16},{1... | collective-permute-start | bytes 737288 | tf_op jit(solution)/shard_map/ppermute | solution.py:374
  114.1 4.8 %collective-permute-done.36.far = f32[480,128]{1,0:T(8,128)S(1)} collective-permute-done((f32[480,128]{1,0:T(8,128)S(1)}, f32[480,128]{1,0:T(8,128)S(1)}, u32[]{:S(2)}, u32[]{:S(2)}) %collective-permute-start.36) | collective-permute-done | bytes 245792 | tf_op jit(solution)/shard_map/ppermute | solution.py:374
  119.6 1.6 %collective-permute-start.34 = (f32[480,128]{1,0:T(8,128)S(1)}, f32[480,128]{1,0:T(8,128)S(1)}, u32[]{:S(2)}, u32[]{:S(2)}) collective-permute-start(f32[480,128]{1,0:T(8,128)S(1)} %shard_map.82), channel_id=1, source_target_pairs={{0,96},{16,112},{32,64},{48,80},{64,32},{80,48},{96,0},{112,16},{1... | collective-permute-start | bytes 737288 | tf_op jit(solution)/shard_map/ppermute | solution.py:374
  121.1 3.6 %collective-permute-done.32.near_0 = f32[480,128]{1,0:T(8,128)S(1)} collective-permute-done((f32[480,128]{1,0:T(8,128)S(1)}, f32[480,128]{1,0:T(8,128)S(1)}, u32[]{:S(2)}, u32[]{:S(2)}) %collective-permute-start.32) | collective-permute-done | bytes 245792 | tf_op jit(solution)/shard_map/ppermute | solution.py:374
  124.8 4.5 %collective-permute-done.37.last_1 = f32[480,128]{1,0:T(8,128)S(1)} collective-permute-done((f32[480,128]{1,0:T(8,128)S(1)}, f32[480,128]{1,0:T(8,128)S(1)}, u32[]{:S(2)}, u32[]{:S(2)}) %collective-permute-start.37) | collective-permute-done | bytes 245792 | tf_op jit(solution)/shard_map/ppermute | solution.py:374
  129.3 1.6 %unpack.1 = f32[6,64,320]{2,1,0:T(8,128)} custom-call(s32[7]{0:T(128)S(1)} %stack.43.places, f32[2,480,128]{2,1,0:T(8,128)S(1)} %get-tuple-element.67.kept.kept_0, f32[480,128]{1,0:T(8,128)S(1)} %collective-permute-done.32.near_0, f32[480,128]{1,0:T(8,128)S(1)} %collective-permute-done.34.last_0, f32[2,480,128]{2,1,0:T(8,128)S(1)} %get-tuple-element.70.kept.kept_1, ...), custom_call_target="tpu_custom_call" | custom-call | tf_op jit(solution)/shard_map/unpack/pallas_call | solution.py:359
  (61 shorter events, 5.3 us)
Async XLA Ops:
  5.3 4.9 %collective-permute-start.1 = (f32[2,2,6,10,8,128]{5,4,3,2,1,0:T(8,128)}, f32[2,2,6,10,8,128]{5,4,3,2,1,0:T(8,128)S(1)}, u32[]{:S(2)}, u32[]{:S(2)}) collective-permute-start(f32[2,2,6,10,8,128]{5,4,3,2,1,0:T(8,128)} %get-tuple-element.42), channel_id=1, source_target_pairs={{0,16},{16,0},{32,48},{48,32},{64,80},{80,64},{96,112},{112,96},{1... | collective-permute-start | bytes 2949128 | tf_op jit(solution)/shard_map/ppermute | solution.py:374
  5.4 10.2 %collective-permute-start = (f32[2,2,6,10,8,128]{5,4,3,2,1,0:T(8,128)S(1)}, f32[2,2,6,10,8,128]{5,4,3,2,1,0:T(8,128)S(1)}, u32[]{:S(2)}, u32[]{:S(2)}) collective-permute-start(f32[2,2,6,10,8,128]{5,4,3,2,1,0:T(8,128)S(1)} %get-tuple-element.40), channel_id=1, source_target_pairs={{0,16},{16,0},{32,48},{48,32},{64,80},{80,64},{96,112},{112,96},{1... | collective-permute-start | bytes 2949128 | tf_op jit(solution)/shard_map/ppermute | solution.py:374
  10.3 10.1 %collective-permute-start.6 = (f32[6,10,8,128]{3,2,1,0:T(8,128)S(1)}, f32[6,10,8,128]{3,2,1,0:T(8,128)S(1)}, u32[]{:S(2)}, u32[]{:S(2)}) collective-permute-start(f32[6,10,8,128]{3,2,1,0:T(8,128)S(1)} %get-tuple-element.46), channel_id=1, source_target_pairs={{0,96},{16,112},{32,64},{48,80},{64,32},{80,48},{96,0},{112,16},{1... | collective-permute-start | bytes 737288 | tf_op jit(solution)/shard_map/ppermute | solution.py:374
  13.5 8.8 %collective-permute-start.4 = (f32[6,10,8,128]{3,2,1,0:T(8,128)S(1)}, f32[6,10,8,128]{3,2,1,0:T(8,128)S(1)}, u32[]{:S(2)}, u32[]{:S(2)}) collective-permute-start(f32[6,10,8,128]{3,2,1,0:T(8,128)S(1)} %get-tuple-element.45), channel_id=1, source_target_pairs={{0,32},{16,48},{32,0},{48,16},{64,96},{80,112},{96,64},{112,80},{1... | collective-permute-start | bytes 737288 | tf_op jit(solution)/shard_map/ppermute | solution.py:374
  13.6 18.1 %collective-permute-start.2 = (f32[6,10,8,128]{3,2,1,0:T(8,128)S(1)}, f32[6,10,8,128]{3,2,1,0:T(8,128)S(1)}, u32[]{:S(2)}, u32[]{:S(2)}) collective-permute-start(f32[6,10,8,128]{3,2,1,0:T(8,128)S(1)} %get-tuple-element.43), channel_id=1, source_target_pairs={{0,32},{16,48},{32,0},{48,16},{64,96},{80,112},{96,64},{112,80},{1... | collective-permute-start | bytes 737288 | tf_op jit(solution)/shard_map/ppermute | solution.py:374
  15.5 16.2 %collective-permute-start.3 = (f32[6,10,8,128]{3,2,1,0:T(8,128)S(1)}, f32[6,10,8,128]{3,2,1,0:T(8,128)S(1)}, u32[]{:S(2)}, u32[]{:S(2)}) collective-permute-start(f32[6,10,8,128]{3,2,1,0:T(8,128)S(1)} %get-tuple-element.44), channel_id=1, source_target_pairs={{0,96},{16,112},{32,64},{48,80},{64,32},{80,48},{96,0},{112,16},{1... | collective-permute-start | bytes 737288 | tf_op jit(solution)/shard_map/ppermute | solution.py:374
  20.4 3.4 %copy-start = (f32[1024]{0:T(1024)S(1)}, f32[1024]{0:T(1024)}, u32[]{:S(2)}) copy-start(f32[1024]{0:T(1024)} %param.9) | copy-start | bytes 12292
  20.4 3.4 %copy-start.1 = (s32[1024]{0:T(1024)S(1)}, s32[1024]{0:T(1024)}, u32[]{:S(2)}) copy-start(s32[1024]{0:T(1024)} %param.11) | copy-start | bytes 12292
  20.4 3.4 %copy-start.2 = (f32[256]{0:T(256)S(1)}, f32[256]{0:T(256)}, u32[]{:S(2)}) copy-start(f32[256]{0:T(256)} %occ_energy.1) | copy-start | bytes 3076
  20.4 3.4 %copy-start.3 = (s32[6]{0:T(128)S(1)}, s32[6]{0:T(128)}, u32[]{:S(2)}) copy-start(s32[6]{0:T(128)} %batch_index.1) | copy-start | bytes 76
  20.5 11.2 %collective-permute-start.7 = (f32[6,10,8,128]{3,2,1,0:T(8,128)S(1)}, f32[6,10,8,128]{3,2,1,0:T(8,128)S(1)}, u32[]{:S(2)}, u32[]{:S(2)}) collective-permute-start(f32[6,10,8,128]{3,2,1,0:T(8,128)S(1)} %shard_map.68), channel_id=1, source_target_pairs={{0,32},{16,48},{32,0},{48,16},{64,96},{80,112},{96,64},{112,80},{1... | collective-permute-start | bytes 737288 | tf_op jit(solution)/shard_map/ppermute | solution.py:374
  22.4 9.4 %collective-permute-start.5 = (f32[6,10,8,128]{3,2,1,0:T(8,128)S(1)}, f32[6,10,8,128]{3,2,1,0:T(8,128)S(1)}, u32[]{:S(2)}, u32[]{:S(2)}) collective-permute-start(f32[6,10,8,128]{3,2,1,0:T(8,128)S(1)} %shard_map.67), channel_id=1, source_target_pairs={{0,96},{16,112},{32,64},{48,80},{64,32},{80,48},{96,0},{112,16},{1... | collective-permute-start | bytes 737288 | tf_op jit(solution)/shard_map/ppermute | solution.py:374
  31.8 12.2 %collective-permute-start.11 = (f32[2,6,10,8,128]{4,3,2,1,0:T(8,128)S(1)}, f32[2,6,10,8,128]{4,3,2,1,0:T(8,128)S(1)}, u32[]{:S(2)}, u32[]{:S(2)}) collective-permute-start(f32[2,6,10,8,128]{4,3,2,1,0:T(8,128)S(1)} %shard_map.69.own.refs_4_), channel_id=1, source_target_pairs={{0,1},{1,0},{2,3},{3,2},{4,5},{5,4},{6,7},{7,6},{8,9},{9,8},{10,11... | collective-permute-start | bytes 1474568 | tf_op jit(solution)/shard_map/ppermute | solution.py:370
  33.4 12.0 %collective-permute-start.15 = (f32[2,6,10,8,128]{4,3,2,1,0:T(8,128)S(1)}, f32[2,6,10,8,128]{4,3,2,1,0:T(8,128)S(1)}, u32[]{:S(2)}, u32[]{:S(2)}) collective-permute-start(f32[2,6,10,8,128]{4,3,2,1,0:T(8,128)S(1)} %shard_map.69.own.refs_4_), channel_id=1, source_target_pairs={{0,4},{1,5},{2,6},{3,7},{4,0},{5,1},{6,2},{7,3},{8,12},{9,13},{10,... | collective-permute-start | bytes 1474568 | tf_op jit(solution)/shard_map/ppermute | solution.py:370
  35.3 12.7 %collective-permute-start.12 = (f32[2,6,10,8,128]{4,3,2,1,0:T(8,128)S(1)}, f32[2,6,10,8,128]{4,3,2,1,0:T(8,128)S(1)}, u32[]{:S(2)}, u32[]{:S(2)}) collective-permute-start(f32[2,6,10,8,128]{4,3,2,1,0:T(8,128)S(1)} %shard_map.69.own.refs_4_), channel_id=1, source_target_pairs={{0,3},{1,2},{2,1},{3,0},{4,7},{5,6},{6,5},{7,4},{8,11},{9,10},{10,... | collective-permute-start | bytes 1474568 | tf_op jit(solution)/shard_map/ppermute | solution.py:370
  37.4 12.7 %collective-permute-start.16 = (f32[2,6,10,8,128]{4,3,2,1,0:T(8,128)S(1)}, f32[2,6,10,8,128]{4,3,2,1,0:T(8,128)S(1)}, u32[]{:S(2)}, u32[]{:S(2)}) collective-permute-start(f32[2,6,10,8,128]{4,3,2,1,0:T(8,128)S(1)} %shard_map.69.own.refs_4_), channel_id=1, source_target_pairs={{0,12},{1,13},{2,14},{3,15},{4,8},{5,9},{6,10},{7,11},{8,4},{9,5},... | collective-permute-start | bytes 1474568 | tf_op jit(solution)/shard_map/ppermute | solution.py:370
  39.9 20.8 %collective-permute-start.10 = (f32[2,6,10,8,128]{4,3,2,1,0:T(8,128)S(1)}, f32[2,6,10,8,128]{4,3,2,1,0:T(8,128)S(1)}, u32[]{:S(2)}, u32[]{:S(2)}) collective-permute-start(f32[2,6,10,8,128]{4,3,2,1,0:T(8,128)S(1)} %shard_map.69.own.refs_4_), channel_id=1, source_target_pairs={{0,64},{16,80},{32,96},{48,112},{64,0},{80,16},{96,32},{112,48},{1... | collective-permute-start | bytes 1474568 | tf_op jit(solution)/shard_map/ppermute | solution.py:374
  44.0 18.1 %collective-permute-start.8 = (f32[2,6,10,8,128]{4,3,2,1,0:T(8,128)S(1)}, f32[2,6,10,8,128]{4,3,2,1,0:T(8,128)S(1)}, u32[]{:S(2)}, u32[]{:S(2)}) collective-permute-start(f32[2,6,10,8,128]{4,3,2,1,0:T(8,128)S(1)} %shard_map.69.own.refs_4_), channel_id=1, source_target_pairs={{0,32},{16,48},{32,0},{48,16},{64,96},{80,112},{96,64},{112,80},{1... | collective-permute-start | bytes 1474568 | tf_op jit(solution)/shard_map/ppermute | solution.py:374
  45.4 17.7 %collective-permute-start.9 = (f32[2,6,10,8,128]{4,3,2,1,0:T(8,128)S(1)}, f32[2,6,10,8,128]{4,3,2,1,0:T(8,128)S(1)}, u32[]{:S(2)}, u32[]{:S(2)}) collective-permute-start(f32[2,6,10,8,128]{4,3,2,1,0:T(8,128)S(1)} %shard_map.69.own.refs_4_), channel_id=1, source_target_pairs={{0,96},{16,112},{32,64},{48,80},{64,32},{80,48},{96,0},{112,16},{1... | collective-permute-start | bytes 1474568 | tf_op jit(solution)/shard_map/ppermute | solution.py:374
  48.0 7.4 %collective-permute-start.19 = (f32[6,10,8,128]{3,2,1,0:T(8,128)S(1)}, f32[6,10,8,128]{3,2,1,0:T(8,128)S(1)}, u32[]{:S(2)}, u32[]{:S(2)}) collective-permute-start(f32[6,10,8,128]{3,2,1,0:T(8,128)S(1)} %shard_map.72), channel_id=1, source_target_pairs={{0,3},{1,2},{2,1},{3,0},{4,7},{5,6},{6,5},{7,4},{8,11},{9,10},{10,... | collective-permute-start | bytes 737288 | tf_op jit(solution)/shard_map/ppermute | solution.py:370
  50.1 8.6 %collective-permute-start.22 = (f32[6,10,8,128]{3,2,1,0:T(8,128)S(1)}, f32[6,10,8,128]{3,2,1,0:T(8,128)S(1)}, u32[]{:S(2)}, u32[]{:S(2)}) collective-permute-start(f32[6,10,8,128]{3,2,1,0:T(8,128)S(1)} %shard_map.74), channel_id=1, source_target_pairs={{0,12},{1,13},{2,14},{3,15},{4,8},{5,9},{6,10},{7,11},{8,4},{9,5},... | collective-permute-start | bytes 737288 | tf_op jit(solution)/shard_map/ppermute | solution.py:370
  55.4 8.7 %collective-permute-start.20 = (f32[6,10,8,128]{3,2,1,0:T(8,128)S(1)}, f32[6,10,8,128]{3,2,1,0:T(8,128)S(1)}, u32[]{:S(2)}, u32[]{:S(2)}) collective-permute-start(f32[6,10,8,128]{3,2,1,0:T(8,128)S(1)} %collective-permute-done.19.refs_5_), channel_id=1, source_target_pairs={{0,12},{1,13},{2,14},{3,15},{4,8},{5,9},{6,10},{7,11},{8,4},{9,5},... | collective-permute-start | bytes 737288 | tf_op jit(solution)/shard_map/ppermute | solution.py:370
  58.8 7.4 %collective-permute-start.23 = (f32[6,10,8,128]{3,2,1,0:T(8,128)S(1)}, f32[6,10,8,128]{3,2,1,0:T(8,128)S(1)}, u32[]{:S(2)}, u32[]{:S(2)}) collective-permute-start(f32[6,10,8,128]{3,2,1,0:T(8,128)S(1)} %collective-permute-done.22.refs_6_), channel_id=1, source_target_pairs={{0,3},{1,2},{2,1},{3,0},{4,7},{5,6},{6,5},{7,4},{8,11},{9,10},{10,... | collective-permute-start | bytes 737288 | tf_op jit(solution)/shard_map/ppermute | solution.py:370
  60.7 20.3 %collective-permute-start.17 = (f32[2,6,10,8,128]{4,3,2,1,0:T(8,128)S(1)}, f32[2,6,10,8,128]{4,3,2,1,0:T(8,128)S(1)}, u32[]{:S(2)}, u32[]{:S(2)}) collective-permute-start(f32[2,6,10,8,128]{4,3,2,1,0:T(8,128)S(1)} %shard_map.71), channel_id=1, source_target_pairs={{0,1},{1,0},{2,3},{3,2},{4,5},{5,4},{6,7},{7,6},{8,9},{9,8},{10,11... | collective-permute-start | bytes 1474568 | tf_op jit(solution)/shard_map/ppermute | solution.py:370
  62.1 9.9 %collective-permute-start.28 = (f32[6,10,8,128]{3,2,1,0:T(8,128)S(1)}, f32[6,10,8,128]{3,2,1,0:T(8,128)S(1)}, u32[]{:S(2)}, u32[]{:S(2)}) collective-permute-start(f32[6,10,8,128]{3,2,1,0:T(8,128)S(1)} %collective-permute-done.19.refs_5_), channel_id=1, source_target_pairs={{0,4},{1,5},{2,6},{3,7},{4,0},{5,1},{6,2},{7,3},{8,12},{9,13},{10,... | collective-permute-start | bytes 737288 | tf_op jit(solution)/shard_map/ppermute | solution.py:370
  63.0 17.9 %collective-permute-start.27 = (f32[2,6,10,8,128]{4,3,2,1,0:T(8,128)S(1)}, f32[2,6,10,8,128]{4,3,2,1,0:T(8,128)S(1)}, u32[]{:S(2)}, u32[]{:S(2)}) collective-permute-start(f32[2,6,10,8,128]{4,3,2,1,0:T(8,128)S(1)} %shard_map.71), channel_id=1, source_target_pairs={{0,3},{1,2},{2,1},{3,0},{4,7},{5,6},{6,5},{7,4},{8,11},{9,10},{10,... | collective-permute-start | bytes 1474568 | tf_op jit(solution)/shard_map/ppermute | solution.py:370
  64.2 16.8 %collective-permute-start.13 = (f32[2,6,10,8,128]{4,3,2,1,0:T(8,128)S(1)}, f32[2,6,10,8,128]{4,3,2,1,0:T(8,128)S(1)}, u32[]{:S(2)}, u32[]{:S(2)}) collective-permute-start(f32[2,6,10,8,128]{4,3,2,1,0:T(8,128)S(1)} %shard_map.70), channel_id=1, source_target_pairs={{0,4},{1,5},{2,6},{3,7},{4,0},{5,1},{6,2},{7,3},{8,12},{9,13},{10,... | collective-permute-start | bytes 1474568 | tf_op jit(solution)/shard_map/ppermute | solution.py:370
  66.2 14.8 %collective-permute-start.26 = (f32[2,6,10,8,128]{4,3,2,1,0:T(8,128)S(1)}, f32[2,6,10,8,128]{4,3,2,1,0:T(8,128)S(1)}, u32[]{:S(2)}, u32[]{:S(2)}) collective-permute-start(f32[2,6,10,8,128]{4,3,2,1,0:T(8,128)S(1)} %shard_map.70), channel_id=1, source_target_pairs={{0,12},{1,13},{2,14},{3,15},{4,8},{5,9},{6,10},{7,11},{8,4},{9,5},... | collective-permute-start | bytes 1474568 | tf_op jit(solution)/shard_map/ppermute | solution.py:370
  71.9 8.8 %collective-permute-start.29 = (f32[6,10,8,128]{3,2,1,0:T(8,128)S(1)}, f32[6,10,8,128]{3,2,1,0:T(8,128)S(1)}, u32[]{:S(2)}, u32[]{:S(2)}) collective-permute-start(f32[6,10,8,128]{3,2,1,0:T(8,128)S(1)} %collective-permute-done.22.refs_6_), channel_id=1, source_target_pairs={{0,1},{1,0},{2,3},{3,2},{4,5},{5,4},{6,7},{7,6},{8,9},{9,8},{10,11... | collective-permute-start | bytes 737288 | tf_op jit(solution)/shard_map/ppermute | solution.py:370
  80.8 9.0 %collective-permute-start.24 = (f32[2,6,10,8,128]{4,3,2,1,0:T(8,128)S(1)}, f32[2,6,10,8,128]{4,3,2,1,0:T(8,128)S(1)}, u32[]{:S(2)}, u32[]{:S(2)}) collective-permute-start(f32[2,6,10,8,128]{4,3,2,1,0:T(8,128)S(1)} %shard_map.75), channel_id=1, source_target_pairs={{0,1},{1,0},{2,3},{3,2},{4,5},{5,4},{6,7},{7,6},{8,9},{9,8},{10,11... | collective-permute-start | bytes 1474568 | tf_op jit(solution)/shard_map/ppermute | solution.py:370
  83.5 19.5 %collective-permute-start.30 = (f32[384,768]{1,0:T(8,128)S(1)}, f32[384,768]{1,0:T(8,128)S(1)}, u32[]{:S(2)}, u32[]{:S(2)}) collective-permute-start(f32[384,768]{1,0:T(8,128)S(1)} %get-tuple-element.59.refs_0_), channel_id=1, source_target_pairs={{0,16},{16,0},{32,48},{48,32},{64,80},{80,64},{96,112},{112,96},{1... | collective-permute-start | bytes 3538952 | tf_op jit(solution)/shard_map/ppermute | solution.py:374
  83.7 13.7 %collective-permute-start.21 = (f32[2,6,10,8,128]{4,3,2,1,0:T(8,128)S(1)}, f32[2,6,10,8,128]{4,3,2,1,0:T(8,128)S(1)}, u32[]{:S(2)}, u32[]{:S(2)}) collective-permute-start(f32[2,6,10,8,128]{4,3,2,1,0:T(8,128)S(1)} %shard_map.73), channel_id=1, source_target_pairs={{0,4},{1,5},{2,6},{3,7},{4,0},{5,1},{6,2},{7,3},{8,12},{9,13},{10,... | collective-permute-start | bytes 1474568 | tf_op jit(solution)/shard_map/ppermute | solution.py:370
  83.9 14.8 %collective-permute-start.18 = (f32[2,6,10,8,128]{4,3,2,1,0:T(8,128)S(1)}, f32[2,6,10,8,128]{4,3,2,1,0:T(8,128)S(1)}, u32[]{:S(2)}, u32[]{:S(2)}) collective-permute-start(f32[2,6,10,8,128]{4,3,2,1,0:T(8,128)S(1)} %collective-permute-done.17.refs_2_), channel_id=1, source_target_pairs={{0,3},{1,2},{2,1},{3,0},{4,7},{5,6},{6,5},{7,4},{8,11},{9,10},{10,... | collective-permute-start | bytes 1474568 | tf_op jit(solution)/shard_map/ppermute | solution.py:370
  83.9 15.3 %collective-permute-start.14 = (f32[2,6,10,8,128]{4,3,2,1,0:T(8,128)S(1)}, f32[2,6,10,8,128]{4,3,2,1,0:T(8,128)S(1)}, u32[]{:S(2)}, u32[]{:S(2)}) collective-permute-start(f32[2,6,10,8,128]{4,3,2,1,0:T(8,128)S(1)} %collective-permute-done.13.refs_0_), channel_id=1, source_target_pairs={{0,12},{1,13},{2,14},{3,15},{4,8},{5,9},{6,10},{7,11},{8,4},{9,5},... | collective-permute-start | bytes 1474568 | tf_op jit(solution)/shard_map/ppermute | solution.py:370
  89.8 11.4 %collective-permute-start.31 = (f32[384,384]{1,0:T(8,128)S(1)}, f32[384,384]{1,0:T(8,128)S(1)}, u32[]{:S(2)}, u32[]{:S(2)}) collective-permute-start(f32[384,384]{1,0:T(8,128)S(1)} %get-tuple-element.63.refs_0_), channel_id=1, source_target_pairs={{0,16},{16,0},{32,48},{48,32},{64,80},{80,64},{96,112},{112,96},{1... | collective-permute-start | bytes 1769480 | tf_op jit(solution)/shard_map/ppermute | solution.py:374
  101.1 4.7 %collective-permute-start.25 = (f32[384,384]{1,0:T(8,128)S(1)}, f32[384,384]{1,0:T(8,128)S(1)}, u32[]{:S(2)}, u32[]{:S(2)}) collective-permute-start(f32[384,384]{1,0:T(8,128)S(1)} %get-tuple-element.54.refs_0_), channel_id=1, source_target_pairs={{0,16},{16,0},{32,48},{48,32},{64,80},{80,64},{96,112},{112,96},{1... | collective-permute-start | bytes 1769480 | tf_op jit(solution)/shard_map/ppermute | solution.py:374
  108.8 10.1 %collective-permute-start.36 = (f32[480,128]{1,0:T(8,128)S(1)}, f32[480,128]{1,0:T(8,128)S(1)}, u32[]{:S(2)}, u32[]{:S(2)}) collective-permute-start(f32[480,128]{1,0:T(8,128)S(1)} %get-tuple-element.72), channel_id=1, source_target_pairs={{0,96},{16,112},{32,64},{48,80},{64,32},{80,48},{96,0},{112,16},{1... | collective-permute-start | bytes 737288 | tf_op jit(solution)/shard_map/ppermute | solution.py:374
  110.7 8.8 %collective-permute-start.33 = (f32[480,128]{1,0:T(8,128)S(1)}, f32[480,128]{1,0:T(8,128)S(1)}, u32[]{:S(2)}, u32[]{:S(2)}) collective-permute-start(f32[480,128]{1,0:T(8,128)S(1)} %get-tuple-element.69), channel_id=1, source_target_pairs={{0,32},{16,48},{32,0},{48,16},{64,96},{80,112},{96,64},{112,80},{1... | collective-permute-start | bytes 737288 | tf_op jit(solution)/shard_map/ppermute | solution.py:374
  111.5 13.3 %collective-permute-start.32 = (f32[480,128]{1,0:T(8,128)S(1)}, f32[480,128]{1,0:T(8,128)S(1)}, u32[]{:S(2)}, u32[]{:S(2)}) collective-permute-start(f32[480,128]{1,0:T(8,128)S(1)} %get-tuple-element.68), channel_id=1, source_target_pairs={{0,32},{16,48},{32,0},{48,16},{64,96},{80,112},{96,64},{112,80},{1... | collective-permute-start | bytes 737288 | tf_op jit(solution)/shard_map/ppermute | solution.py:374
  112.7 12.1 %collective-permute-start.35 = (f32[480,128]{1,0:T(8,128)S(1)}, f32[480,128]{1,0:T(8,128)S(1)}, u32[]{:S(2)}, u32[]{:S(2)}) collective-permute-start(f32[480,128]{1,0:T(8,128)S(1)} %get-tuple-element.71), channel_id=1, source_target_pairs={{0,96},{16,112},{32,64},{48,80},{64,32},{80,48},{96,0},{112,16},{1... | collective-permute-start | bytes 737288 | tf_op jit(solution)/shard_map/ppermute | solution.py:374
  118.9 10.4 %collective-permute-start.37 = (f32[480,128]{1,0:T(8,128)S(1)}, f32[480,128]{1,0:T(8,128)S(1)}, u32[]{:S(2)}, u32[]{:S(2)}) collective-permute-start(f32[480,128]{1,0:T(8,128)S(1)} %shard_map.83), channel_id=1, source_target_pairs={{0,32},{16,48},{32,0},{48,16},{64,96},{80,112},{96,64},{112,80},{1... | collective-permute-start | bytes 737288 | tf_op jit(solution)/shard_map/ppermute | solution.py:374
  119.6 9.7 %collective-permute-start.34 = (f32[480,128]{1,0:T(8,128)S(1)}, f32[480,128]{1,0:T(8,128)S(1)}, u32[]{:S(2)}, u32[]{:S(2)}) collective-permute-start(f32[480,128]{1,0:T(8,128)S(1)} %shard_map.82), channel_id=1, source_target_pairs={{0,96},{16,112},{32,64},{48,80},{64,32},{80,48},{96,0},{112,16},{1... | collective-permute-start | bytes 737288 | tf_op jit(solution)/shard_map/ppermute | solution.py:374

commit v2 on v1

--- a/solution.py
+++ b/solution.py
@@ -70,6 +70,12 @@
     return pl.CostEstimate(flops=flops, bytes_accessed=4 * 2**20, transcendentals=0)
 
 
+def chip_column():
+    place = lax.axis_index("aux").astype(jnp.int32)
+    y = place >> 1
+    return place & 1, (y ^ 1, y ^ 3, y ^ 2, y)
+
+
 def near_memory(shape, kind=F32):
     return pltpu.VMEM(shape, kind)
 
@@ -78,20 +84,15 @@
     return [pltpu.with_memory_space_constraint(v, pltpu.VMEM) for v in values]
 
 
-def fitted_kernel(places, integrals, metric, sent, kept, left, right, full, arrivals):
-    core = places[0]
-    start = pl.multiple_of(256 * core, 128)
-    copies = [pltpu.make_async_copy(integrals, left, arrivals.at[4])]
-    for y in range(4):
-        columns = metric.at[:, pl.ds(pl.multiple_of(640 * y + start, 128), 384)]
-        copies.append(pltpu.make_async_copy(columns, right.at[y], arrivals.at[y]))
-    for copy in copies:
-        copy.start()
-    copies[0].wait()
+def fitted_rows(left):
     rows = left[...].reshape(OCC * VL, QL)
     main_high, main_low = split(rows[:, :256])
     rest_high, rest_low = split(rows[:, 256:])
-    rest = jnp.concatenate([rest_high, rest_low, rest_high], axis=1)
+    return main_high, main_low, jnp.concatenate([rest_high, rest_low, rest_high], axis=1)
+
+
+def fitted_products(core, ys, rows, right, ready, sent, kept, full):
+    main_high, main_low, rest = rows
     side = pl.multiple_of(128 * core, 128)
     other = pl.multiple_of(256 - 256 * core, 128)
     low = lanes(QL)
@@ -105,7 +106,7 @@
 
     rests = []
     for y in range(4):
-        copies[1 + y].wait()
+        ready(y)
         put(right[y, :, pl.ds(side, 256)], 256 * y)
         rests.append(right[y, :, pl.ds(other, 128)])
     packed = []
@@ -115,7 +116,7 @@
         odd = jnp.where(low, half_turn(first), second)
         packed.append(jnp.where(core == 0, even, odd))
     put(jnp.concatenate(packed, axis=1), 1024)
-    y_a, y_b, y_far, y_own = places[1], places[2], places[3], places[4]
+    y_a, y_b, y_far, y_own = ys
     for target, half, slot, y in (
         (sent, 0, 0, y_a), (sent, 0, 1, y_far), (sent, 1, 0, y_b), (sent, 1, 1, y_far),
         (kept, 0, 0, y_own), (kept, 0, 1, y_b), (kept, 1, 0, y_own), (kept, 1, 1, y_a),
@@ -125,22 +126,58 @@
                 target[half, slot, i, q] = full[i, y, half, :, 128 * q : 128 * q + 128]
 
 
-def fitted_part(places, integrals, metric):
+def partner_kernel(integrals, metric, sent, kept, left, own_right, right, full, arrivals):
+    core, ys = chip_column()
+    copies = [pltpu.make_async_copy(integrals, left, arrivals.at[8])]
+    for k, (which, target) in enumerate(((1 - core, right), (core, own_right))):
+        start = pl.multiple_of(256 * which, 128)
+        for y in range(4):
+            columns = metric.at[:, pl.ds(pl.multiple_of(640 * y + start, 128), 384)]
+            copies.append(pltpu.make_async_copy(columns, target.at[y], arrivals.at[4 * k + y]))
+    for copy in copies:
+        copy.start()
+    copies[0].wait()
+    rows = fitted_rows(left)
+    fitted_products(1 - core, ys, rows, right, lambda y: copies[1 + y].wait(), sent, kept, full)
+    for copy in copies[5:]:
+        copy.wait()
+
+
+def self_kernel(left, right, sent, kept, full):
+    core, ys = chip_column()
+    fitted_products(core, ys, fitted_rows(left), right, lambda y: None, sent, kept, full)
+
+
+COLUMNS = (4, QL, 384)
+
+
+def fitted_parts(integrals, metric, between):
     piece = near_memory((2, 2, *PIECE))
-    return pl.pallas_call(
-        fitted_kernel,
+    common = dict(compiler_params=settings(12), cost_estimate=cost(FLOPS // 3))
+    sent, kept, left, right = pl.pallas_call(
+        partner_kernel,
+        out_shape=(piece, piece, near_memory((OCC, VL, QL)), near_memory(COLUMNS)),
+        in_specs=[HBM_SPEC, HBM_SPEC],
+        out_specs=(VMEM_SPEC,) * 4,
+        scratch_shapes=[
+            pltpu.VMEM(COLUMNS, F32),
+            pltpu.VMEM((OCC, 4, 2, 8, QH), F32),
+            pltpu.SemaphoreType.DMA((9,)),
+        ],
+        name="fitted_for_partner",
+        **common,
+    )(integrals, metric)
+    received = between(sent, kept)
+    own = pl.pallas_call(
+        self_kernel,
         out_shape=(piece, piece),
-        in_specs=[SMEM_SPEC, HBM_SPEC, HBM_SPEC],
+        in_specs=[VMEM_SPEC] * 2,
         out_specs=(VMEM_SPEC,) * 2,
-        scratch_shapes=[
-            pltpu.VMEM((OCC, VL, QL), F32),
-            pltpu.VMEM((4, QL, 384), F32),
-            pltpu.VMEM((OCC, 4, 2, 8, QH), F32),
-            pltpu.SemaphoreType.DMA((5,)),
-        ],
-        compiler_params=settings(12),
-        cost_estimate=cost(FLOPS // 3),
-    )(places, integrals, metric)
+        scratch_shapes=[pltpu.VMEM((OCC, 4, 2, 8, QH), F32)],
+        name="fitted_for_self",
+        **common,
+    )(*held(left, right))
+    return received, own
 
 
 def small_call(kernel, shapes, args):
@@ -299,10 +336,11 @@
     )(*held(*args))
 
 
-def density_last_kernel(places, *refs):
+def density_last_kernel(*refs):
     before, near_0, near_1, far_0, far_1, kept_0, kept_1, whole = refs[6:]
     term = before[...] + density_term(*refs[:6])
-    order = (places[4], places[1], places[2], places[3])
+    _, (y_a, y_b, y_far, y_own) = chip_column()
+    order = (y_own, y_a, y_b, y_far)
     for q in range(QT):
         for i in range(OCC):
             for k in range(4):
@@ -324,21 +362,22 @@
             target[row : row + 32, :] = jnp.where(low, rest[:32], half_turn(rest[32:]))
 
 
-def density_last(places, inputs, before):
+def density_last(inputs, before):
     piece, two = near_memory((480, 128)), near_memory((2, 480, 128))
     return pl.pallas_call(
         density_last_kernel,
         out_shape=(piece,) * 4 + (two,) * 2,
-        in_specs=[SMEM_SPEC] + [VMEM_SPEC] * 7,
+        in_specs=[VMEM_SPEC] * 7,
         out_specs=(VMEM_SPEC,) * 6,
         scratch_shapes=[pltpu.VMEM((QT, OCC, 4, 16, 128), F32)],
         compiler_params=settings(12),
         cost_estimate=cost(FLOPS),
-    )(places, *held(*inputs, before))
-
-
-def unpack_kernel(places, kept_0, near_0, last_0, kept_1, near_1, last_1, result):
+    )(*held(*inputs, before))
+
+
+def unpack_kernel(kept_0, near_0, last_0, kept_1, near_1, last_1, result):
     low = lanes(VL)
+    zero = chip_column()[0] == 0
     for half, refs in enumerate(((kept_0, near_0, last_0), (kept_1, near_1, last_1))):
         kept, near, last = refs
         total = kept[0] + near[...] + last[...]
@@ -348,22 +387,21 @@
             packed = total[6 * VL + 32 * i : 6 * VL + 32 * i + 32]
             rest = jnp.concatenate([packed, half_turn(packed)], axis=0)
             first_turned, second_turned = half_turn(first), half_turn(second)
-            zero = places[0] == 0
             at = half * 3 + i
             result[at, :, 0:128] = jnp.where(zero, first, jnp.where(low, rest, first_turned))
             result[at, :, 128:256] = jnp.where(zero, second, jnp.where(low, first_turned, second_turned))
             result[at, :, 256:320] = jnp.where(zero, rest, second_turned)[:, :64]
 
 
-def unpack(places, *parts):
+def unpack(*parts):
     return pl.pallas_call(
         unpack_kernel,
         out_shape=jax.ShapeDtypeStruct((OCC, VL, QL), F32),
-        in_specs=[SMEM_SPEC] + [VMEM_SPEC] * 6,
+        in_specs=[VMEM_SPEC] * 6,
         out_specs=VMEM_SPEC,
         compiler_params=settings(4),
         name="unpack",
-    )(places, *held(*parts))
+    )(*held(*parts))
 
 
 def on_virt(value, pairs):
@@ -376,15 +414,17 @@
 
 SPOTS = (
     (0, 1, 0), (0, 1, 1), (0, 3, 0), (0, 3, 1), (1, 0, 0), (1, 0, 1), (3, 0, 0), (3, 0, 1),
+    (0, 0, 0), (0, 0, 1), (0, 2, 0), (2, 0, 1), (1, 2, 0), (3, 2, 0), (2, 1, 1), (2, 3, 1),
     (1, 1, 0), (1, 3, 0), (3, 1, 0), (3, 3, 0), (1, 1, 1), (3, 1, 1), (1, 3, 1), (3, 3, 1),
-    (0, 0, 0), (0, 0, 1), (0, 2, 0), (2, 0, 1), (1, 2, 0), (3, 2, 0), (2, 1, 1), (2, 3, 1),
     (2, 1, 0), (2, 3, 0), (1, 2, 1), (3, 2, 1), (2, 0, 0), (2, 2, 0), (0, 2, 1), (2, 2, 1),
 )
 
 
-def terms_kernel(places, batch_index, occ_energy, virt_energy, virt_order, row_term, *col_terms):
-    z, x = places[5], places[6]
-    chips = (places[4], places[1], places[2], places[3])
+def terms_kernel(batch_index, occ_energy, virt_energy, virt_order, row_term, *col_terms):
+    place = lax.axis_index("virt").astype(jnp.int32)
+    z, x = place >> 2, place & 3
+    _, (y_a, y_b, y_far, y_own) = chip_column()
+    chips = (y_own, y_a, y_b, y_far)
     lane = lax.broadcasted_iota(jnp.int32, (8, 128), 1).astype(F32)
     step = lax.broadcasted_iota(jnp.int32, (8, 128), 0).astype(F32)
     order = virt_order[...].astype(F32)
@@ -406,54 +446,41 @@
     for i in range(OCC):
         row_term[VL * i : VL * i + VL, :] = occ[i] - rows
     low = lax.broadcasted_iota(jnp.int32, (1, 128), 1) < 64
-    first, second, third = col_terms
-
-    def along(values):
-        both = jnp.concatenate(values, axis=0)
+    for k in range(2):
+        both = jnp.concatenate(levels[8 + 16 * k : 24 + 16 * k], axis=0)
         flat = jnp.broadcast_to(both, (128, 128)).T[:8]
-        return flat[:1], half_turn(flat)[:1]
-
-    flat, turned = along(levels[16:32])
-    for i in range(OCC):
-        second[:, 128 * i : 128 * i + 128] = occ[i] - flat
-    flat, turned = along(levels[8:16] + levels[32:40])
-    for target, value in ((first, jnp.where(low, flat, turned)), (third, jnp.where(low, turned, flat))):
-        for t in range(3):
-            target[:, 128 * t : 128 * t + 128] = jnp.where(low, occ[2 * t], occ[2 * t + 1]) - value
-
-
-def energy_terms(places, batch_index, occ_energy, virt_energy, virt_order):
+        flat, turned = flat[:1], half_turn(flat)[:1]
+        for side, value in ((0, jnp.where(low, flat, turned)), (1, jnp.where(low, turned, flat))):
+            for t in range(3):
+                col_terms[2 * k + side][:, 128 * t : 128 * t + 128] = jnp.where(low, occ[2 * t], occ[2 * t + 1]) - value
+
+
+def energy_terms(batch_index, occ_energy, virt_energy, virt_order):
     column = near_memory((1, OCC * VL))
     return pl.pallas_call(
         terms_kernel,
-        out_shape=(near_memory((OCC * VL, 1)), column, near_memory((1, 2 * OCC * VL)), column),
-        in_specs=[SMEM_SPEC] * 3 + [VMEM_SPEC] * 2,
-        out_specs=(VMEM_SPEC,) * 4,
+        out_shape=(near_memory((OCC * VL, 1)), *(column,) * 4),
+        in_specs=[SMEM_SPEC] * 2 + [VMEM_SPEC] * 2,
+        out_specs=(VMEM_SPEC,) * 5,
         compiler_params=settings(4),
         cost_estimate=cost(FLOPS // 4),
         name="terms",
-    )(places, batch_index, occ_energy, virt_energy.reshape(8, 128), virt_order.reshape(8, 128))
+    )(batch_index, occ_energy, virt_energy.reshape(8, 128), virt_order.reshape(8, 128))
 
 
 def shards(integrals, metric_root, occ_energy, virt_energy, batch_index, virt_order):
-    aux_place = lax.axis_index("aux").astype(jnp.int32)
-    virt_place = lax.axis_index("virt").astype(jnp.int32)
-    y, core = aux_place >> 1, aux_place & 1
-    z, x = virt_place >> 2, virt_place & 3
-    near = [y ^ 1, y ^ 3, y ^ 2, y, z, x]
-    places = jnp.stack([core, *near])
-    partner_places = jnp.stack([1 - core, *near])
-
     values = pltpu.with_memory_space_constraint(integrals.transpose(1, 0, 2), pltpu.HBM)
     metric = pltpu.with_memory_space_constraint(metric_root.T, pltpu.HBM)
-    out_sent, out_kept = fitted_part(partner_places, values, metric)
-    in_sent = on_aux(out_sent, CORE)
-    in_kept = on_aux(out_kept, CORE)
-    own_sent, own_kept = fitted_part(places, values, metric)
+
+    def swap(sent, kept):
+        return on_aux(sent, CORE), on_aux(kept, CORE)
+
+    (in_sent, in_kept), (own_sent, own_kept) = fitted_parts(values, metric, swap)
+
     near_0, near_1, far_0, far_1 = small_call(sent_kernel, (PIECE,) * 4, (own_sent, in_sent))
     far_0, far_1 = on_aux(far_0, YA), on_aux(far_1, YB)
     near_0, near_1 = on_aux(near_0, YA), on_aux(near_1, YB)
-    row_term, *col_terms = energy_terms(places, batch_index, occ_energy, virt_energy, virt_order)
+    row_term, *col_terms = energy_terms(batch_index, occ_energy, virt_energy, virt_order)
     (last_0,) = small_call(relay_kernel(0), (PIECE,), (own_kept, in_kept, far_0))
     last_0 = on_aux(last_0, YB)
     (last_1,) = small_call(relay_kernel(1), (PIECE,), (own_kept, in_kept, far_1))
@@ -484,7 +511,8 @@
     left = rows_part(own, row_a, row_b, row_2)
     chunks = (
         (s_xa, s_xb, s_za, s_zb),
-        (pa_a, pa_b, pb_a, pb_b, own, a_2, b_2, qa_a, qa_b, qb_a, qb_b),
+        (own, a_2, b_2, qa_a, qa_b, qb_a, qb_b),
+        (pa_a, pa_b, pb_a, pb_b),
         (pa_2, pb_2, f_a, f_b),
     )
     total = None
@@ -492,16 +520,16 @@
         pair, high, low = pair_part(left, cols)
         other = on_aux(pair, CORE)
         inputs = (pair, other, row_term, col_terms[k], high, low)
-        if k < 2:
+        if k < 3:
             total = density_part(inputs, total)
-    near_0, near_1, far_0, far_1, kept_0, kept_1 = density_last(places, inputs, total)
+    near_0, near_1, far_0, far_1, kept_0, kept_1 = density_last(inputs, total)
     far_0, far_1 = on_aux(far_0, YA), on_aux(far_1, YB)
     near_0, near_1 = on_aux(near_0, YA), on_aux(near_1, YB)
     (last_0,) = small_call(final_relay_kernel, ((480, 128),), (kept_0, far_0))
     last_0 = on_aux(last_0, YB)
     (last_1,) = small_call(final_relay_kernel, ((480, 128),), (kept_1, far_1))
     last_1 = on_aux(last_1, YA)
-    result = unpack(places, kept_0, near_0, last_0, kept_1, near_1, last_1)
+    result = unpack(kept_0, near_0, last_0, kept_1, near_1, last_1)
     return result.transpose(1, 0, 2)
 
 

time: 131 us -> 132 us (level)
  waiting for transfers between devices: 53.7 us -> 60.1 us
  Pallas kernels: 26.6 us -> 23.2 us
  starting transfers between devices: 50.1 us -> 47.8 us
    ppermute x18, waiting for transfers between devices: 26.4 us -> 33.2 us  [on_virt(): return lax.ppermute(value, 'virt', pairs)]
    pallas_call x3, Pallas kernels: 10.5 us -> 6.11 us  [the longest x1 3.69 us: fitted_parts(): pl.pallas_call(partner_kernel, out_shape=(piece, piece, near_memory((OCC,...]
    ppermute x18, starting transfers between devices: 31.8 us -> 28.7 us  [on_virt(): return lax.ppermute(value, 'virt', pairs)]
    pallas_call x3 -> x4, Pallas kernels: 6.19 us -> 7.4 us  [pair_part(): pl.pallas_call(pair_kernel, out_shape=(near_memory((OCC * VL, width)), pa...]
    pallas_call x2 -> x3, Pallas kernels: 4.61 us -> 5.56 us  [density_part(): pl.pallas_call(density_first_kernel if before is None else density_next_k...]
    ppermute x20 -> x21, starting transfers between devices: 18.3 us -> 19.1 us  [on_aux(): return lax.ppermute(value, 'aux', pairs)]
    ppermute x20 -> x21, waiting for transfers between devices: 27.3 us -> 26.9 us  [on_aux(): return lax.ppermute(value, 'aux', pairs)]
  transfers between devices with their start and end apart: 38 -> 39, of which waited for: 18 -> 16; matrix products, arithmetic and copies ran while one was open for 0% -> 0% of each run, Pallas kernels for 13% -> 12%
where the time goes in v2:
time: 132 us; the launch traced here: 131 us
  waiting for transfers between devices  60.1 us (46%)
  starting transfers between devices  47.8 us (36%)
  Pallas kernels  23.2 us (18%)
    ppermute x18, waiting for transfers between devices, on_virt(): return lax.ppermute(value, 'virt', pairs)  33.2 us
    ppermute x18, starting transfers between devices, on_virt(): return lax.ppermute(value, 'virt', pairs)  28.7 us
    ppermute x21, waiting for transfers between devices, on_aux(): return lax.ppermute(value, 'aux', pairs)  26.9 us
    ppermute x21, starting transfers between devices, on_aux(): return lax.ppermute(value, 'aux', pairs)  19.1 us
    pallas_call x4, Pallas kernels, pair_part(): pl.pallas_call(pair_kernel, out_shape=(near_memory((OCC * VL, width)), pa...  7.4 us
    pallas_call x3, Pallas kernels, density_part(): pl.pallas_call(density_first_kernel if before is None else density_next_k...  5.56 us
    pallas_call x1, Pallas kernels, fitted_parts(): pl.pallas_call(partner_kernel, out_shape=(piece, piece, near_memory((OCC,...  3.69 us
  transfers between devices with their start and end apart: 39, of which 16 were waited for; matrix products, arithmetic and copies ran while one was open for 0% of the time, Pallas kernels for 12%

profile of v2, /device:TPU:0, one launch (start us, length us, event | category | flops | bytes accessed | tf_op | source)
XLA Modules:
  0.0 131.4 jit_solution(9959836975367433532)
XLA Ops:
  0.0 3.7 %fitted_for_partner.1 = (f32[2,2,6,10,8,128]{5,4,3,2,1,0:T(8,128)S(1)}, f32[2,2,6,10,8,128]{5,4,3,2,1,0:T(8,128)S(1)}, f32[6,64,320]{2,1,0:T(8,128)S(1)}, f32[4,320,384]{2,1,0:T(8,128)S(1)}) custom-call(f32[6,64,320]{2,1,0:T(8,128)} %bitcast.8, f32[320,2560]{1,0:T(8,128)} %bitcast.7), custom_call_target="tpu_custom_call" | custom-call | flops 377487360 | bytes 4194304 | tf_op jit(solution)/shard_map/fitted_for_partner/pallas_call | solution.py:157
  4.3 1.3 %fitted_for_self.1 = (f32[2,2,6,10,8,128]{5,4,3,2,1,0:T(8,128)S(1)}, f32[2,2,6,10,8,128]{5,4,3,2,1,0:T(8,128)S(1)}) custom-call(f32[6,64,320]{2,1,0:T(8,128)S(1)} %get-tuple-element.46.left, f32[4,320,384]{2,1,0:T(8,128)S(1)} %get-tuple-element.47.right), custom_call_target="tpu_custom_call" | custom-call | flops 377487360 | bytes 4194304 | tf_op jit(solution)/shard_map/fitted_for_self/pallas_call | solution.py:171
  5.6 0.7 collective-permute-done.1.other
  6.4 3.2 %collective-permute-start.6 = (f32[6,10,8,128]{3,2,1,0:T(8,128)S(1)}, f32[6,10,8,128]{3,2,1,0:T(8,128)S(1)}, u32[]{:S(2)}, u32[]{:S(2)}) collective-permute-start(f32[6,10,8,128]{3,2,1,0:T(8,128)S(1)} %get-tuple-element.55), channel_id=1, source_target_pairs={{0,96},{16,112},{32,64},{48,80},{64,32},{80,48},{96,0},{112,16},{1... | collective-permute-start | bytes 737288 | tf_op jit(solution)/shard_map/ppermute | solution.py:412
  9.8 1.9 %collective-permute-start.2 = (f32[6,10,8,128]{3,2,1,0:T(8,128)S(1)}, f32[6,10,8,128]{3,2,1,0:T(8,128)S(1)}, u32[]{:S(2)}, u32[]{:S(2)}) collective-permute-start(f32[6,10,8,128]{3,2,1,0:T(8,128)S(1)} %get-tuple-element.52), channel_id=1, source_target_pairs={{0,32},{16,48},{32,0},{48,16},{64,96},{80,112},{96,64},{112,80},{1... | collective-permute-start | bytes 737288 | tf_op jit(solution)/shard_map/ppermute | solution.py:412
  11.8 4.8 %collective-permute-done.6.far = f32[6,10,8,128]{3,2,1,0:T(8,128)S(1)} collective-permute-done((f32[6,10,8,128]{3,2,1,0:T(8,128)S(1)}, f32[6,10,8,128]{3,2,1,0:T(8,128)S(1)}, u32[]{:S(2)}, u32[]{:S(2)}) %collective-permute-start.6) | collective-permute-done | bytes 245792 | tf_op jit(solution)/shard_map/ppermute | solution.py:412
  17.2 1.3 collective-permute-done.4.far
  18.5 1.5 %collective-permute-start.5 = (f32[6,10,8,128]{3,2,1,0:T(8,128)S(1)}, f32[6,10,8,128]{3,2,1,0:T(8,128)S(1)}, u32[]{:S(2)}, u32[]{:S(2)}) collective-permute-start(f32[6,10,8,128]{3,2,1,0:T(8,128)S(1)} %shard_map.65), channel_id=1, source_target_pairs={{0,96},{16,112},{32,64},{48,80},{64,32},{80,48},{96,0},{112,16},{1... | collective-permute-start | bytes 737288 | tf_op jit(solution)/shard_map/ppermute | solution.py:412
  20.0 1.1 terms.1
  21.1 6.8 %collective-permute-done.7.last_1 = f32[6,10,8,128]{3,2,1,0:T(8,128)S(1)} collective-permute-done((f32[6,10,8,128]{3,2,1,0:T(8,128)S(1)}, f32[6,10,8,128]{3,2,1,0:T(8,128)S(1)}, u32[]{:S(2)}, u32[]{:S(2)}) %collective-permute-start.7) | collective-permute-done | bytes 245792 | tf_op jit(solution)/shard_map/ppermute | solution.py:412
  28.0 1.6 %collective-permute-start.11 = (f32[2,6,10,8,128]{4,3,2,1,0:T(8,128)S(1)}, f32[2,6,10,8,128]{4,3,2,1,0:T(8,128)S(1)}, u32[]{:S(2)}, u32[]{:S(2)}) collective-permute-start(f32[2,6,10,8,128]{4,3,2,1,0:T(8,128)S(1)} %shard_map.67.own.refs_0_), channel_id=1, source_target_pairs={{0,1},{1,0},{2,3},{3,2},{4,5},{5,4},{6,7},{7,6},{8,9},{9,8},{10,11... | collective-permute-start | bytes 1474568 | tf_op jit(solution)/shard_map/ppermute | solution.py:408
  29.6 2.1 %collective-permute-start.12 = (f32[2,6,10,8,128]{4,3,2,1,0:T(8,128)S(1)}, f32[2,6,10,8,128]{4,3,2,1,0:T(8,128)S(1)}, u32[]{:S(2)}, u32[]{:S(2)}) collective-permute-start(f32[2,6,10,8,128]{4,3,2,1,0:T(8,128)S(1)} %shard_map.67.own.refs_0_), channel_id=1, source_target_pairs={{0,3},{1,2},{2,1},{3,0},{4,7},{5,6},{6,5},{7,4},{8,11},{9,10},{10,... | collective-permute-start | bytes 1474568 | tf_op jit(solution)/shard_map/ppermute | solution.py:408
  31.7 1.9 %collective-permute-start.15 = (f32[2,6,10,8,128]{4,3,2,1,0:T(8,128)S(1)}, f32[2,6,10,8,128]{4,3,2,1,0:T(8,128)S(1)}, u32[]{:S(2)}, u32[]{:S(2)}) collective-permute-start(f32[2,6,10,8,128]{4,3,2,1,0:T(8,128)S(1)} %shard_map.67.own.refs_0_), channel_id=1, source_target_pairs={{0,4},{1,5},{2,6},{3,7},{4,0},{5,1},{6,2},{7,3},{8,12},{9,13},{10,... | collective-permute-start | bytes 1474568 | tf_op jit(solution)/shard_map/ppermute | solution.py:408
  33.6 2.5 %collective-permute-start.16 = (f32[2,6,10,8,128]{4,3,2,1,0:T(8,128)S(1)}, f32[2,6,10,8,128]{4,3,2,1,0:T(8,128)S(1)}, u32[]{:S(2)}, u32[]{:S(2)}) collective-permute-start(f32[2,6,10,8,128]{4,3,2,1,0:T(8,128)S(1)} %shard_map.67.own.refs_0_), channel_id=1, source_target_pairs={{0,12},{1,13},{2,14},{3,15},{4,8},{5,9},{6,10},{7,11},{8,4},{9,5},... | collective-permute-start | bytes 1474568 | tf_op jit(solution)/shard_map/ppermute | solution.py:408
  36.8 3.5 %collective-permute-done.11.first.value.refs_0_ = f32[2,6,10,8,128]{4,3,2,1,0:T(8,128)S(1)} collective-permute-done((f32[2,6,10,8,128]{4,3,2,1,0:T(8,128)S(1)}, f32[2,6,10,8,128]{4,3,2,1,0:T(8,128)S(1)}, u32[]{:S(2)}, u32[]{:S(2)}) %collective-permute-start.11) | collective-permute-done | bytes 491552 | tf_op jit(solution)/shard_map/ppermute | solution.py:408
  40.7 2.0 %collective-permute-done.12.second.near.refs_1_ = f32[2,6,10,8,128]{4,3,2,1,0:T(8,128)S(1)} collective-permute-done((f32[2,6,10,8,128]{4,3,2,1,0:T(8,128)S(1)}, f32[2,6,10,8,128]{4,3,2,1,0:T(8,128)S(1)}, u32[]{:S(2)}, u32[]{:S(2)}) %collective-permute-start.12) | collective-permute-done | bytes 491552 | tf_op jit(solution)/shard_map/ppermute | solution.py:408
  42.7 1.8 %collective-permute-start.9 = (f32[2,6,10,8,128]{4,3,2,1,0:T(8,128)S(1)}, f32[2,6,10,8,128]{4,3,2,1,0:T(8,128)S(1)}, u32[]{:S(2)}, u32[]{:S(2)}) collective-permute-start(f32[2,6,10,8,128]{4,3,2,1,0:T(8,128)S(1)} %shard_map.67.own.refs_0_), channel_id=1, source_target_pairs={{0,96},{16,112},{32,64},{48,80},{64,32},{80,48},{96,0},{112,16},{1... | collective-permute-start | bytes 1474568 | tf_op jit(solution)/shard_map/ppermute | solution.py:412
  44.4 2.2 %collective-permute-start.19 = (f32[6,10,8,128]{3,2,1,0:T(8,128)S(1)}, f32[6,10,8,128]{3,2,1,0:T(8,128)S(1)}, u32[]{:S(2)}, u32[]{:S(2)}) collective-permute-start(f32[6,10,8,128]{3,2,1,0:T(8,128)S(1)} %shard_map.70), channel_id=1, source_target_pairs={{0,3},{1,2},{2,1},{3,0},{4,7},{5,6},{6,5},{7,4},{8,11},{9,10},{10,... | collective-permute-start | bytes 737288 | tf_op jit(solution)/shard_map/ppermute | solution.py:408
  46.6 4.1 %collective-permute-start.22 = (f32[6,10,8,128]{3,2,1,0:T(8,128)S(1)}, f32[6,10,8,128]{3,2,1,0:T(8,128)S(1)}, u32[]{:S(2)}, u32[]{:S(2)}) collective-permute-start(f32[6,10,8,128]{3,2,1,0:T(8,128)S(1)} %shard_map.72), channel_id=1, source_target_pairs={{0,12},{1,13},{2,14},{3,15},{4,8},{5,9},{6,10},{7,11},{8,4},{9,5},... | collective-permute-start | bytes 737288 | tf_op jit(solution)/shard_map/ppermute | solution.py:408
  50.8 1.2 collective-permute-done.19.refs_1_
  51.9 4.0 %collective-permute-start.20 = (f32[6,10,8,128]{3,2,1,0:T(8,128)S(1)}, f32[6,10,8,128]{3,2,1,0:T(8,128)S(1)}, u32[]{:S(2)}, u32[]{:S(2)}) collective-permute-start(f32[6,10,8,128]{3,2,1,0:T(8,128)S(1)} %collective-permute-done.19.refs_1_), channel_id=1, source_target_pairs={{0,12},{1,13},{2,14},{3,15},{4,8},{5,9},{6,10},{7,11},{8,4},{9,5},... | collective-permute-start | bytes 737288 | tf_op jit(solution)/shard_map/ppermute | solution.py:408
  56.1 2.0 %collective-permute-start.23 = (f32[6,10,8,128]{3,2,1,0:T(8,128)S(1)}, f32[6,10,8,128]{3,2,1,0:T(8,128)S(1)}, u32[]{:S(2)}, u32[]{:S(2)}) collective-permute-start(f32[6,10,8,128]{3,2,1,0:T(8,128)S(1)} %collective-permute-done.22.refs_2_), channel_id=1, source_target_pairs={{0,3},{1,2},{2,1},{3,0},{4,7},{5,6},{6,5},{7,4},{8,11},{9,10},{10,... | collective-permute-start | bytes 737288 | tf_op jit(solution)/shard_map/ppermute | solution.py:408
  58.3 1.3 collective-permute-start.27
  59.6 0.9 collective-permute-start.13
  60.4 1.2 collective-permute-start.29
  61.6 4.5 %collective-permute-done.23.far.refs_6_ = f32[6,10,8,128]{3,2,1,0:T(8,128)S(1)} collective-permute-done((f32[6,10,8,128]{3,2,1,0:T(8,128)S(1)}, f32[6,10,8,128]{3,2,1,0:T(8,128)S(1)}, u32[]{:S(2)}, u32[]{:S(2)}) %collective-permute-start.23) | collective-permute-done | bytes 245792 | tf_op jit(solution)/shard_map/ppermute | solution.py:408
  66.1 10.6 %collective-permute-done.29.refs_3_ = f32[6,10,8,128]{3,2,1,0:T(8,128)S(1)} collective-permute-done((f32[6,10,8,128]{3,2,1,0:T(8,128)S(1)}, f32[6,10,8,128]{3,2,1,0:T(8,128)S(1)}, u32[]{:S(2)}, u32[]{:S(2)}) %collective-permute-start.29) | collective-permute-done | bytes 245792 | tf_op jit(solution)/shard_map/ppermute | solution.py:408
  76.7 1.0 collective-permute-start.26
  78.6 0.7 collective-permute-start.18
  79.3 2.3 %collective-permute-start.14 = (f32[2,6,10,8,128]{4,3,2,1,0:T(8,128)S(1)}, f32[2,6,10,8,128]{4,3,2,1,0:T(8,128)S(1)}, u32[]{:S(2)}, u32[]{:S(2)}) collective-permute-start(f32[2,6,10,8,128]{4,3,2,1,0:T(8,128)S(1)} %collective-permute-done.13.refs_0_), channel_id=1, source_target_pairs={{0,12},{1,13},{2,14},{3,15},{4,8},{5,9},{6,10},{7,11},{8,4},{9,5},... | collective-permute-start | bytes 1474568 | tf_op jit(solution)/shard_map/ppermute | solution.py:408
  82.0 1.8 %shard_map.77 = (f32[384,384]{1,0:T(8,128)S(1)}, bf16[384,1280]{1,0:T(8,128)(2,1)S(1)}, bf16[384,1280]{1,0:T(8,128)(2,1)S(1)}) custom-call(bf16[384,1280]{1,0:T(8,128)(2,1)S(1)} %get-tuple-element.62.left_high, bf16[384,1280]{1,0:T(8,128)(2,1)S(1)} %get-tuple-element.63.left_low, f32[2,6,10,8,128]{4,3,2,1,0:T(8,128)S(1)} %collective-permute-done.11.first.value.refs_0_, ...), custom_call_target="tpu_custom_call" | custom-call | flops 1132462080 | bytes 4194304 | tf_op jit(solution)/shard_map/pallas_call | solution.py:282
  83.8 8.2 %collective-permute-done.26.refs_1_ = f32[2,6,10,8,128]{4,3,2,1,0:T(8,128)S(1)} collective-permute-done((f32[2,6,10,8,128]{4,3,2,1,0:T(8,128)S(1)}, f32[2,6,10,8,128]{4,3,2,1,0:T(8,128)S(1)}, u32[]{:S(2)}, u32[]{:S(2)}) %collective-permute-start.26) | collective-permute-done | bytes 491552 | tf_op jit(solution)/shard_map/ppermute | solution.py:408
  92.1 1.9 %shard_map.76 = (f32[384,384]{1,0:T(8,128)S(1)}, bf16[384,1280]{1,0:T(8,128)(2,1)S(1)}, bf16[384,1280]{1,0:T(8,128)(2,1)S(1)}) custom-call(bf16[384,1280]{1,0:T(8,128)(2,1)S(1)} %get-tuple-element.62.left_high, bf16[384,1280]{1,0:T(8,128)(2,1)S(1)} %get-tuple-element.63.left_low, f32[2,6,10,8,128]{4,3,2,1,0:T(8,128)S(1)} %shard_map.67.own.refs_0_, ...), custom_call_target="tpu_custom_call" | custom-call | flops 1132462080 | bytes 4194304 | tf_op jit(solution)/shard_map/pallas_call | solution.py:282
  94.5 1.9 %shard_map.75 = (f32[384,384]{1,0:T(8,128)S(1)}, bf16[384,1280]{1,0:T(8,128)(2,1)S(1)}, bf16[384,1280]{1,0:T(8,128)(2,1)S(1)}) custom-call(bf16[384,1280]{1,0:T(8,128)(2,1)S(1)} %get-tuple-element.62.left_high, bf16[384,1280]{1,0:T(8,128)(2,1)S(1)} %get-tuple-element.63.left_low, f32[2,6,10,8,128]{4,3,2,1,0:T(8,128)S(1)} %collective-permute-done.13.refs_0_, ...), custom_call_target="tpu_custom_call" | custom-call | flops 1132462080 | bytes 4194304 | tf_op jit(solution)/shard_map/pallas_call | solution.py:282
  96.5 3.1 %collective-permute-done.14.refs_0_ = f32[2,6,10,8,128]{4,3,2,1,0:T(8,128)S(1)} collective-permute-done((f32[2,6,10,8,128]{4,3,2,1,0:T(8,128)S(1)}, f32[2,6,10,8,128]{4,3,2,1,0:T(8,128)S(1)}, u32[]{:S(2)}, u32[]{:S(2)}) %collective-permute-start.14) | collective-permute-done | bytes 491552 | tf_op jit(solution)/shard_map/ppermute | solution.py:408
  99.5 1.9 %shard_map.74 = (f32[384,384]{1,0:T(8,128)S(1)}, bf16[384,1280]{1,0:T(8,128)(2,1)S(1)}, bf16[384,1280]{1,0:T(8,128)(2,1)S(1)}) custom-call(bf16[384,1280]{1,0:T(8,128)(2,1)S(1)} %get-tuple-element.62.left_high, bf16[384,1280]{1,0:T(8,128)(2,1)S(1)} %get-tuple-element.63.left_low, f32[2,6,10,8,128]{4,3,2,1,0:T(8,128)S(1)} %collective-permute-done.14.refs_0_, ...), custom_call_target="tpu_custom_call" | custom-call | flops 1132462080 | bytes 4194304 | tf_op jit(solution)/shard_map/pallas_call | solution.py:282
  101.7 1.8 %shard_map.78.refs_6_ = f32[384,1280]{1,0:T(8,128)S(1)} custom-call(f32[384,384]{1,0:T(8,128)S(1)} %get-tuple-element.77.refs_0_, f32[384,384]{1,0:T(8,128)S(1)} %collective-permute-done.32.refs_1_, f32[384,1]{1,0:T(8,128)S(1)} %get-tuple-element.65.refs_2_, f32[1,384]{1,0:T(1,128)S(1)} %get-tuple-element.78.refs_3_, ...), custom_call_target="tpu_custom_call" | custom-call | flops 1132462080 | bytes 4194304 | tf_op jit(solution)/shard_map/pallas_call | solution.py:329
  103.6 1.9 %shard_map.79.refs_6_ = f32[384,1280]{1,0:T(8,128)S(1)} custom-call(f32[384,384]{1,0:T(8,128)S(1)} %get-tuple-element.73.refs_0_, f32[384,384]{1,0:T(8,128)S(1)} %collective-permute-done.31.refs_1_, f32[384,1]{1,0:T(8,128)S(1)} %get-tuple-element.65.refs_2_, f32[1,384]{1,0:T(1,128)S(1)} %get-tuple-element.74.refs_3_, ...), custom_call_target="tpu_custom_call" | custom-call | flops 1132462080 | bytes 4194304 | tf_op jit(solution)/shard_map/pallas_call | solution.py:329
  105.5 1.9 %shard_map.80.refs_6_ = f32[384,1280]{1,0:T(8,128)S(1)} custom-call(f32[384,384]{1,0:T(8,128)S(1)} %get-tuple-element.69.refs_0_, f32[384,384]{1,0:T(8,128)S(1)} %collective-permute-done.28.refs_1_, f32[384,1]{1,0:T(8,128)S(1)} %get-tuple-element.65.refs_2_, f32[1,384]{1,0:T(1,128)S(1)} %get-tuple-element.70.refs_3_, ...), custom_call_target="tpu_custom_call" | custom-call | flops 1132462080 | bytes 4194304 | tf_op jit(solution)/shard_map/pallas_call | solution.py:329
  107.3 2.3 %shard_map.81 = (f32[480,128]{1,0:T(8,128)S(1)}, f32[480,128]{1,0:T(8,128)S(1)}, f32[480,128]{1,0:T(8,128)S(1)}, f32[480,128]{1,0:T(8,128)S(1)}, f32[2,480,128]{2,1,0:T(8,128)S(1)}, /*index=5*/f32[2,480,128]{2,1,0:T(8,128)S(1)}) custom-call(f32[384,384]{1,0:T(8,128)S(1)} %get-tuple-element.64.refs_0_, f32[384,384]{1,0:T(8,128)S(1)} %collective-permute-done.25.refs_1_, ...), custom_call_target="tpu_custom_call" | custom-call | flops 1132462080 | bytes 4194304 | tf_op jit(solution)/shard_map/pallas_call | solution.py:367
  109.7 2.1 %collective-permute-start.37 = (f32[480,128]{1,0:T(8,128)S(1)}, f32[480,128]{1,0:T(8,128)S(1)}, u32[]{:S(2)}, u32[]{:S(2)}) collective-permute-start(f32[480,128]{1,0:T(8,128)S(1)} %get-tuple-element.86), channel_id=1, source_target_pairs={{0,96},{16,112},{32,64},{48,80},{64,32},{80,48},{96,0},{112,16},{1... | collective-permute-start | bytes 737288 | tf_op jit(solution)/shard_map/ppermute | solution.py:412
  111.8 2.0 %collective-permute-start.33 = (f32[480,128]{1,0:T(8,128)S(1)}, f32[480,128]{1,0:T(8,128)S(1)}, u32[]{:S(2)}, u32[]{:S(2)}) collective-permute-start(f32[480,128]{1,0:T(8,128)S(1)} %get-tuple-element.82), channel_id=1, source_target_pairs={{0,32},{16,48},{32,0},{48,16},{64,96},{80,112},{96,64},{112,80},{1... | collective-permute-start | bytes 737288 | tf_op jit(solution)/shard_map/ppermute | solution.py:412
  113.8 1.2 collective-permute-start.36
  115.0 4.8 %collective-permute-done.37.far = f32[480,128]{1,0:T(8,128)S(1)} collective-permute-done((f32[480,128]{1,0:T(8,128)S(1)}, f32[480,128]{1,0:T(8,128)S(1)}, u32[]{:S(2)}, u32[]{:S(2)}) %collective-permute-start.37) | collective-permute-done | bytes 245792 | tf_op jit(solution)/shard_map/ppermute | solution.py:412
  120.6 1.4 %collective-permute-start.35 = (f32[480,128]{1,0:T(8,128)S(1)}, f32[480,128]{1,0:T(8,128)S(1)}, u32[]{:S(2)}, u32[]{:S(2)}) collective-permute-start(f32[480,128]{1,0:T(8,128)S(1)} %shard_map.82), channel_id=1, source_target_pairs={{0,96},{16,112},{32,64},{48,80},{64,32},{80,48},{96,0},{112,16},{1... | collective-permute-start | bytes 737288 | tf_op jit(solution)/shard_map/ppermute | solution.py:412
  122.1 3.8 %collective-permute-done.33.near_0 = f32[480,128]{1,0:T(8,128)S(1)} collective-permute-done((f32[480,128]{1,0:T(8,128)S(1)}, f32[480,128]{1,0:T(8,128)S(1)}, u32[]{:S(2)}, u32[]{:S(2)}) %collective-permute-start.33) | collective-permute-done | bytes 245792 | tf_op jit(solution)/shard_map/ppermute | solution.py:412
  125.9 4.5 %collective-permute-done.38.last_1 = f32[480,128]{1,0:T(8,128)S(1)} collective-permute-done((f32[480,128]{1,0:T(8,128)S(1)}, f32[480,128]{1,0:T(8,128)S(1)}, u32[]{:S(2)}, u32[]{:S(2)}) %collective-permute-start.38) | collective-permute-done | bytes 245792 | tf_op jit(solution)/shard_map/ppermute | solution.py:412
  130.4 1.0 unpack.1
  (63 shorter events, 6.0 us)
Async XLA Ops:
  3.7 2.6 %collective-permute-start.1 = (f32[2,2,6,10,8,128]{5,4,3,2,1,0:T(8,128)S(1)}, f32[2,2,6,10,8,128]{5,4,3,2,1,0:T(8,128)S(1)}, u32[]{:S(2)}, u32[]{:S(2)}) collective-permute-start(f32[2,2,6,10,8,128]{5,4,3,2,1,0:T(8,128)S(1)} %get-tuple-element.51), channel_id=1, source_target_pairs={{0,16},{16,0},{32,48},{48,32},{64,80},{80,64},{96,112},{112,96},{1... | collective-permute-start | bytes 2949128 | tf_op jit(solution)/shard_map/ppermute | solution.py:412
  3.8 8.0 %collective-permute-start = (f32[2,2,6,10,8,128]{5,4,3,2,1,0:T(8,128)S(1)}, f32[2,2,6,10,8,128]{5,4,3,2,1,0:T(8,128)S(1)}, u32[]{:S(2)}, u32[]{:S(2)}) collective-permute-start(f32[2,2,6,10,8,128]{5,4,3,2,1,0:T(8,128)S(1)} %get-tuple-element.49), channel_id=1, source_target_pairs={{0,16},{16,0},{32,48},{48,32},{64,80},{80,64},{96,112},{112,96},{1... | collective-permute-start | bytes 2949128 | tf_op jit(solution)/shard_map/ppermute | solution.py:412
  6.4 10.1 %collective-permute-start.6 = (f32[6,10,8,128]{3,2,1,0:T(8,128)S(1)}, f32[6,10,8,128]{3,2,1,0:T(8,128)S(1)}, u32[]{:S(2)}, u32[]{:S(2)}) collective-permute-start(f32[6,10,8,128]{3,2,1,0:T(8,128)S(1)} %get-tuple-element.55), channel_id=1, source_target_pairs={{0,96},{16,112},{32,64},{48,80},{64,32},{80,48},{96,0},{112,16},{1... | collective-permute-start | bytes 737288 | tf_op jit(solution)/shard_map/ppermute | solution.py:412
  9.7 8.8 %collective-permute-start.4 = (f32[6,10,8,128]{3,2,1,0:T(8,128)S(1)}, f32[6,10,8,128]{3,2,1,0:T(8,128)S(1)}, u32[]{:S(2)}, u32[]{:S(2)}) collective-permute-start(f32[6,10,8,128]{3,2,1,0:T(8,128)S(1)} %get-tuple-element.54), channel_id=1, source_target_pairs={{0,32},{16,48},{32,0},{48,16},{64,96},{80,112},{96,64},{112,80},{1... | collective-permute-start | bytes 737288 | tf_op jit(solution)/shard_map/ppermute | solution.py:412
  9.8 18.1 %collective-permute-start.2 = (f32[6,10,8,128]{3,2,1,0:T(8,128)S(1)}, f32[6,10,8,128]{3,2,1,0:T(8,128)S(1)}, u32[]{:S(2)}, u32[]{:S(2)}) collective-permute-start(f32[6,10,8,128]{3,2,1,0:T(8,128)S(1)} %get-tuple-element.52), channel_id=1, source_target_pairs={{0,32},{16,48},{32,0},{48,16},{64,96},{80,112},{96,64},{112,80},{1... | collective-permute-start | bytes 737288 | tf_op jit(solution)/shard_map/ppermute | solution.py:412
  11.7 16.2 %collective-permute-start.3 = (f32[6,10,8,128]{3,2,1,0:T(8,128)S(1)}, f32[6,10,8,128]{3,2,1,0:T(8,128)S(1)}, u32[]{:S(2)}, u32[]{:S(2)}) collective-permute-start(f32[6,10,8,128]{3,2,1,0:T(8,128)S(1)} %get-tuple-element.53), channel_id=1, source_target_pairs={{0,96},{16,112},{32,64},{48,80},{64,32},{80,48},{96,0},{112,16},{1... | collective-permute-start | bytes 737288 | tf_op jit(solution)/shard_map/ppermute | solution.py:412
  16.6 3.4 %copy-start = (f32[1024]{0:T(1024)S(1)}, f32[1024]{0:T(1024)}, u32[]{:S(2)}) copy-start(f32[1024]{0:T(1024)} %param.9) | copy-start | bytes 12292
  16.6 3.4 %copy-start.1 = (s32[1024]{0:T(1024)S(1)}, s32[1024]{0:T(1024)}, u32[]{:S(2)}) copy-start(s32[1024]{0:T(1024)} %param.11) | copy-start | bytes 12292
  16.6 3.4 %copy-start.2 = (f32[256]{0:T(256)S(1)}, f32[256]{0:T(256)}, u32[]{:S(2)}) copy-start(f32[256]{0:T(256)} %occ_energy.1) | copy-start | bytes 3076
  16.6 3.4 %copy-start.3 = (s32[6]{0:T(128)S(1)}, s32[6]{0:T(128)}, u32[]{:S(2)}) copy-start(s32[6]{0:T(128)} %batch_index.1) | copy-start | bytes 76
  16.6 11.3 %collective-permute-start.7 = (f32[6,10,8,128]{3,2,1,0:T(8,128)S(1)}, f32[6,10,8,128]{3,2,1,0:T(8,128)S(1)}, u32[]{:S(2)}, u32[]{:S(2)}) collective-permute-start(f32[6,10,8,128]{3,2,1,0:T(8,128)S(1)} %shard_map.66), channel_id=1, source_target_pairs={{0,32},{16,48},{32,0},{48,16},{64,96},{80,112},{96,64},{112,80},{1... | collective-permute-start | bytes 737288 | tf_op jit(solution)/shard_map/ppermute | solution.py:412
  18.5 9.4 %collective-permute-start.5 = (f32[6,10,8,128]{3,2,1,0:T(8,128)S(1)}, f32[6,10,8,128]{3,2,1,0:T(8,128)S(1)}, u32[]{:S(2)}, u32[]{:S(2)}) collective-permute-start(f32[6,10,8,128]{3,2,1,0:T(8,128)S(1)} %shard_map.65), channel_id=1, source_target_pairs={{0,96},{16,112},{32,64},{48,80},{64,32},{80,48},{96,0},{112,16},{1... | collective-permute-start | bytes 737288 | tf_op jit(solution)/shard_map/ppermute | solution.py:412
  28.0 12.2 %collective-permute-start.11 = (f32[2,6,10,8,128]{4,3,2,1,0:T(8,128)S(1)}, f32[2,6,10,8,128]{4,3,2,1,0:T(8,128)S(1)}, u32[]{:S(2)}, u32[]{:S(2)}) collective-permute-start(f32[2,6,10,8,128]{4,3,2,1,0:T(8,128)S(1)} %shard_map.67.own.refs_0_), channel_id=1, source_target_pairs={{0,1},{1,0},{2,3},{3,2},{4,5},{5,4},{6,7},{7,6},{8,9},{9,8},{10,11... | collective-permute-start | bytes 1474568 | tf_op jit(solution)/shard_map/ppermute | solution.py:408
  29.6 13.1 %collective-permute-start.12 = (f32[2,6,10,8,128]{4,3,2,1,0:T(8,128)S(1)}, f32[2,6,10,8,128]{4,3,2,1,0:T(8,128)S(1)}, u32[]{:S(2)}, u32[]{:S(2)}) collective-permute-start(f32[2,6,10,8,128]{4,3,2,1,0:T(8,128)S(1)} %shard_map.67.own.refs_0_), channel_id=1, source_target_pairs={{0,3},{1,2},{2,1},{3,0},{4,7},{5,6},{6,5},{7,4},{8,11},{9,10},{10,... | collective-permute-start | bytes 1474568 | tf_op jit(solution)/shard_map/ppermute | solution.py:408
  31.7 12.7 %collective-permute-start.15 = (f32[2,6,10,8,128]{4,3,2,1,0:T(8,128)S(1)}, f32[2,6,10,8,128]{4,3,2,1,0:T(8,128)S(1)}, u32[]{:S(2)}, u32[]{:S(2)}) collective-permute-start(f32[2,6,10,8,128]{4,3,2,1,0:T(8,128)S(1)} %shard_map.67.own.refs_0_), channel_id=1, source_target_pairs={{0,4},{1,5},{2,6},{3,7},{4,0},{5,1},{6,2},{7,3},{8,12},{9,13},{10,... | collective-permute-start | bytes 1474568 | tf_op jit(solution)/shard_map/ppermute | solution.py:408
  33.6 13.0 %collective-permute-start.16 = (f32[2,6,10,8,128]{4,3,2,1,0:T(8,128)S(1)}, f32[2,6,10,8,128]{4,3,2,1,0:T(8,128)S(1)}, u32[]{:S(2)}, u32[]{:S(2)}) collective-permute-start(f32[2,6,10,8,128]{4,3,2,1,0:T(8,128)S(1)} %shard_map.67.own.refs_0_), channel_id=1, source_target_pairs={{0,12},{1,13},{2,14},{3,15},{4,8},{5,9},{6,10},{7,11},{8,4},{9,5},... | collective-permute-start | bytes 1474568 | tf_op jit(solution)/shard_map/ppermute | solution.py:408
  36.1 22.0 %collective-permute-start.10 = (f32[2,6,10,8,128]{4,3,2,1,0:T(8,128)S(1)}, f32[2,6,10,8,128]{4,3,2,1,0:T(8,128)S(1)}, u32[]{:S(2)}, u32[]{:S(2)}) collective-permute-start(f32[2,6,10,8,128]{4,3,2,1,0:T(8,128)S(1)} %shard_map.67.own.refs_0_), channel_id=1, source_target_pairs={{0,64},{16,80},{32,96},{48,112},{64,0},{80,16},{96,32},{112,48},{1... | collective-permute-start | bytes 1474568 | tf_op jit(solution)/shard_map/ppermute | solution.py:412
  40.2 18.0 %collective-permute-start.8 = (f32[2,6,10,8,128]{4,3,2,1,0:T(8,128)S(1)}, f32[2,6,10,8,128]{4,3,2,1,0:T(8,128)S(1)}, u32[]{:S(2)}, u32[]{:S(2)}) collective-permute-start(f32[2,6,10,8,128]{4,3,2,1,0:T(8,128)S(1)} %shard_map.67.own.refs_0_), channel_id=1, source_target_pairs={{0,32},{16,48},{32,0},{48,16},{64,96},{80,112},{96,64},{112,80},{1... | collective-permute-start | bytes 1474568 | tf_op jit(solution)/shard_map/ppermute | solution.py:412
  42.7 16.9 %collective-permute-start.9 = (f32[2,6,10,8,128]{4,3,2,1,0:T(8,128)S(1)}, f32[2,6,10,8,128]{4,3,2,1,0:T(8,128)S(1)}, u32[]{:S(2)}, u32[]{:S(2)}) collective-permute-start(f32[2,6,10,8,128]{4,3,2,1,0:T(8,128)S(1)} %shard_map.67.own.refs_0_), channel_id=1, source_target_pairs={{0,96},{16,112},{32,64},{48,80},{64,32},{80,48},{96,0},{112,16},{1... | collective-permute-start | bytes 1474568 | tf_op jit(solution)/shard_map/ppermute | solution.py:412
  44.4 7.5 %collective-permute-start.19 = (f32[6,10,8,128]{3,2,1,0:T(8,128)S(1)}, f32[6,10,8,128]{3,2,1,0:T(8,128)S(1)}, u32[]{:S(2)}, u32[]{:S(2)}) collective-permute-start(f32[6,10,8,128]{3,2,1,0:T(8,128)S(1)} %shard_map.70), channel_id=1, source_target_pairs={{0,3},{1,2},{2,1},{3,0},{4,7},{5,6},{6,5},{7,4},{8,11},{9,10},{10,... | collective-permute-start | bytes 737288 | tf_op jit(solution)/shard_map/ppermute | solution.py:408
  46.6 9.4 %collective-permute-start.22 = (f32[6,10,8,128]{3,2,1,0:T(8,128)S(1)}, f32[6,10,8,128]{3,2,1,0:T(8,128)S(1)}, u32[]{:S(2)}, u32[]{:S(2)}) collective-permute-start(f32[6,10,8,128]{3,2,1,0:T(8,128)S(1)} %shard_map.72), channel_id=1, source_target_pairs={{0,12},{1,13},{2,14},{3,15},{4,8},{5,9},{6,10},{7,11},{8,4},{9,5},... | collective-permute-start | bytes 737288 | tf_op jit(solution)/shard_map/ppermute | solution.py:408
  51.9 8.5 %collective-permute-start.20 = (f32[6,10,8,128]{3,2,1,0:T(8,128)S(1)}, f32[6,10,8,128]{3,2,1,0:T(8,128)S(1)}, u32[]{:S(2)}, u32[]{:S(2)}) collective-permute-start(f32[6,10,8,128]{3,2,1,0:T(8,128)S(1)} %collective-permute-done.19.refs_1_), channel_id=1, source_target_pairs={{0,12},{1,13},{2,14},{3,15},{4,8},{5,9},{6,10},{7,11},{8,4},{9,5},... | collective-permute-start | bytes 737288 | tf_op jit(solution)/shard_map/ppermute | solution.py:408
  56.1 10.0 %collective-permute-start.23 = (f32[6,10,8,128]{3,2,1,0:T(8,128)S(1)}, f32[6,10,8,128]{3,2,1,0:T(8,128)S(1)}, u32[]{:S(2)}, u32[]{:S(2)}) collective-permute-start(f32[6,10,8,128]{3,2,1,0:T(8,128)S(1)} %collective-permute-done.22.refs_2_), channel_id=1, source_target_pairs={{0,3},{1,2},{2,1},{3,0},{4,7},{5,6},{6,5},{7,4},{8,11},{9,10},{10,... | collective-permute-start | bytes 737288 | tf_op jit(solution)/shard_map/ppermute | solution.py:408
  58.2 19.8 %collective-permute-start.17 = (f32[2,6,10,8,128]{4,3,2,1,0:T(8,128)S(1)}, f32[2,6,10,8,128]{4,3,2,1,0:T(8,128)S(1)}, u32[]{:S(2)}, u32[]{:S(2)}) collective-permute-start(f32[2,6,10,8,128]{4,3,2,1,0:T(8,128)S(1)} %shard_map.69), channel_id=1, source_target_pairs={{0,1},{1,0},{2,3},{3,2},{4,5},{5,4},{6,7},{7,6},{8,9},{9,8},{10,11... | collective-permute-start | bytes 1474568 | tf_op jit(solution)/shard_map/ppermute | solution.py:408
  58.3 20.4 %collective-permute-start.27 = (f32[2,6,10,8,128]{4,3,2,1,0:T(8,128)S(1)}, f32[2,6,10,8,128]{4,3,2,1,0:T(8,128)S(1)}, u32[]{:S(2)}, u32[]{:S(2)}) collective-permute-start(f32[2,6,10,8,128]{4,3,2,1,0:T(8,128)S(1)} %shard_map.69), channel_id=1, source_target_pairs={{0,3},{1,2},{2,1},{3,0},{4,7},{5,6},{6,5},{7,4},{8,11},{9,10},{10,... | collective-permute-start | bytes 1474568 | tf_op jit(solution)/shard_map/ppermute | solution.py:408
  59.6 19.8 %collective-permute-start.13 = (f32[2,6,10,8,128]{4,3,2,1,0:T(8,128)S(1)}, f32[2,6,10,8,128]{4,3,2,1,0:T(8,128)S(1)}, u32[]{:S(2)}, u32[]{:S(2)}) collective-permute-start(f32[2,6,10,8,128]{4,3,2,1,0:T(8,128)S(1)} %shard_map.68), channel_id=1, source_target_pairs={{0,4},{1,5},{2,6},{3,7},{4,0},{5,1},{6,2},{7,3},{8,12},{9,13},{10,... | collective-permute-start | bytes 1474568 | tf_op jit(solution)/shard_map/ppermute | solution.py:408
  60.4 16.3 %collective-permute-start.29 = (f32[6,10,8,128]{3,2,1,0:T(8,128)S(1)}, f32[6,10,8,128]{3,2,1,0:T(8,128)S(1)}, u32[]{:S(2)}, u32[]{:S(2)}) collective-permute-start(f32[6,10,8,128]{3,2,1,0:T(8,128)S(1)} %collective-permute-done.19.refs_1_), channel_id=1, source_target_pairs={{0,4},{1,5},{2,6},{3,7},{4,0},{5,1},{6,2},{7,3},{8,12},{9,13},{10,... | collective-permute-start | bytes 737288 | tf_op jit(solution)/shard_map/ppermute | solution.py:408
  66.1 11.7 %collective-permute-start.30 = (f32[6,10,8,128]{3,2,1,0:T(8,128)S(1)}, f32[6,10,8,128]{3,2,1,0:T(8,128)S(1)}, u32[]{:S(2)}, u32[]{:S(2)}) collective-permute-start(f32[6,10,8,128]{3,2,1,0:T(8,128)S(1)} %collective-permute-done.22.refs_2_), channel_id=1, source_target_pairs={{0,1},{1,0},{2,3},{3,2},{4,5},{5,4},{6,7},{7,6},{8,9},{9,8},{10,11... | collective-permute-start | bytes 737288 | tf_op jit(solution)/shard_map/ppermute | solution.py:408
  76.7 15.3 %collective-permute-start.26 = (f32[2,6,10,8,128]{4,3,2,1,0:T(8,128)S(1)}, f32[2,6,10,8,128]{4,3,2,1,0:T(8,128)S(1)}, u32[]{:S(2)}, u32[]{:S(2)}) collective-permute-start(f32[2,6,10,8,128]{4,3,2,1,0:T(8,128)S(1)} %shard_map.68), channel_id=1, source_target_pairs={{0,12},{1,13},{2,14},{3,15},{4,8},{5,9},{6,10},{7,11},{8,4},{9,5},... | collective-permute-start | bytes 1474568 | tf_op jit(solution)/shard_map/ppermute | solution.py:408
  77.8 16.1 %collective-permute-start.24 = (f32[2,6,10,8,128]{4,3,2,1,0:T(8,128)S(1)}, f32[2,6,10,8,128]{4,3,2,1,0:T(8,128)S(1)}, u32[]{:S(2)}, u32[]{:S(2)}) collective-permute-start(f32[2,6,10,8,128]{4,3,2,1,0:T(8,128)S(1)} %shard_map.73), channel_id=1, source_target_pairs={{0,1},{1,0},{2,3},{3,2},{4,5},{5,4},{6,7},{7,6},{8,9},{9,8},{10,11... | collective-permute-start | bytes 1474568 | tf_op jit(solution)/shard_map/ppermute | solution.py:408
  78.0 18.4 %collective-permute-start.21 = (f32[2,6,10,8,128]{4,3,2,1,0:T(8,128)S(1)}, f32[2,6,10,8,128]{4,3,2,1,0:T(8,128)S(1)}, u32[]{:S(2)}, u32[]{:S(2)}) collective-permute-start(f32[2,6,10,8,128]{4,3,2,1,0:T(8,128)S(1)} %shard_map.71), channel_id=1, source_target_pairs={{0,4},{1,5},{2,6},{3,7},{4,0},{5,1},{6,2},{7,3},{8,12},{9,13},{10,... | collective-permute-start | bytes 1474568 | tf_op jit(solution)/shard_map/ppermute | solution.py:408
  78.6 17.9 %collective-permute-start.18 = (f32[2,6,10,8,128]{4,3,2,1,0:T(8,128)S(1)}, f32[2,6,10,8,128]{4,3,2,1,0:T(8,128)S(1)}, u32[]{:S(2)}, u32[]{:S(2)}) collective-permute-start(f32[2,6,10,8,128]{4,3,2,1,0:T(8,128)S(1)} %collective-permute-done.17.refs_2_), channel_id=1, source_target_pairs={{0,3},{1,2},{2,1},{3,0},{4,7},{5,6},{6,5},{7,4},{8,11},{9,10},{10,... | collective-permute-start | bytes 1474568 | tf_op jit(solution)/shard_map/ppermute | solution.py:408
  79.3 20.2 %collective-permute-start.14 = (f32[2,6,10,8,128]{4,3,2,1,0:T(8,128)S(1)}, f32[2,6,10,8,128]{4,3,2,1,0:T(8,128)S(1)}, u32[]{:S(2)}, u32[]{:S(2)}) collective-permute-start(f32[2,6,10,8,128]{4,3,2,1,0:T(8,128)S(1)} %collective-permute-done.13.refs_0_), channel_id=1, source_target_pairs={{0,12},{1,13},{2,14},{3,15},{4,8},{5,9},{6,10},{7,11},{8,4},{9,5},... | collective-permute-start | bytes 1474568 | tf_op jit(solution)/shard_map/ppermute | solution.py:408
  92.0 9.7 %collective-permute-start.32 = (f32[384,384]{1,0:T(8,128)S(1)}, f32[384,384]{1,0:T(8,128)S(1)}, u32[]{:S(2)}, u32[]{:S(2)}) collective-permute-start(f32[384,384]{1,0:T(8,128)S(1)} %get-tuple-element.77.refs_0_), channel_id=1, source_target_pairs={{0,16},{16,0},{32,48},{48,32},{64,80},{80,64},{96,112},{112,96},{1... | collective-permute-start | bytes 1769480 | tf_op jit(solution)/shard_map/ppermute | solution.py:412
  93.9 9.7 %collective-permute-start.31 = (f32[384,384]{1,0:T(8,128)S(1)}, f32[384,384]{1,0:T(8,128)S(1)}, u32[]{:S(2)}, u32[]{:S(2)}) collective-permute-start(f32[384,384]{1,0:T(8,128)S(1)} %get-tuple-element.73.refs_0_), channel_id=1, source_target_pairs={{0,16},{16,0},{32,48},{48,32},{64,80},{80,64},{96,112},{112,96},{1... | collective-permute-start | bytes 1769480 | tf_op jit(solution)/shard_map/ppermute | solution.py:412
  96.4 9.1 %collective-permute-start.28 = (f32[384,384]{1,0:T(8,128)S(1)}, f32[384,384]{1,0:T(8,128)S(1)}, u32[]{:S(2)}, u32[]{:S(2)}) collective-permute-start(f32[384,384]{1,0:T(8,128)S(1)} %get-tuple-element.69.refs_0_), channel_id=1, source_target_pairs={{0,16},{16,0},{32,48},{48,32},{64,80},{80,64},{96,112},{112,96},{1... | collective-permute-start | bytes 1769480 | tf_op jit(solution)/shard_map/ppermute | solution.py:412
  101.4 5.9 %collective-permute-start.25 = (f32[384,384]{1,0:T(8,128)S(1)}, f32[384,384]{1,0:T(8,128)S(1)}, u32[]{:S(2)}, u32[]{:S(2)}) collective-permute-start(f32[384,384]{1,0:T(8,128)S(1)} %get-tuple-element.64.refs_0_), channel_id=1, source_target_pairs={{0,16},{16,0},{32,48},{48,32},{64,80},{80,64},{96,112},{112,96},{1... | collective-permute-start | bytes 1769480 | tf_op jit(solution)/shard_map/ppermute | solution.py:412
  109.7 10.1 %collective-permute-start.37 = (f32[480,128]{1,0:T(8,128)S(1)}, f32[480,128]{1,0:T(8,128)S(1)}, u32[]{:S(2)}, u32[]{:S(2)}) collective-permute-start(f32[480,128]{1,0:T(8,128)S(1)} %get-tuple-element.86), channel_id=1, source_target_pairs={{0,96},{16,112},{32,64},{48,80},{64,32},{80,48},{96,0},{112,16},{1... | collective-permute-start | bytes 737288 | tf_op jit(solution)/shard_map/ppermute | solution.py:412
  111.8 8.8 %collective-permute-start.34 = (f32[480,128]{1,0:T(8,128)S(1)}, f32[480,128]{1,0:T(8,128)S(1)}, u32[]{:S(2)}, u32[]{:S(2)}) collective-permute-start(f32[480,128]{1,0:T(8,128)S(1)} %get-tuple-element.83), channel_id=1, source_target_pairs={{0,32},{16,48},{32,0},{48,16},{64,96},{80,112},{96,64},{112,80},{1... | collective-permute-start | bytes 737288 | tf_op jit(solution)/shard_map/ppermute | solution.py:412
  111.8 14.1 %collective-permute-start.33 = (f32[480,128]{1,0:T(8,128)S(1)}, f32[480,128]{1,0:T(8,128)S(1)}, u32[]{:S(2)}, u32[]{:S(2)}) collective-permute-start(f32[480,128]{1,0:T(8,128)S(1)} %get-tuple-element.82), channel_id=1, source_target_pairs={{0,32},{16,48},{32,0},{48,16},{64,96},{80,112},{96,64},{112,80},{1... | collective-permute-start | bytes 737288 | tf_op jit(solution)/shard_map/ppermute | solution.py:412
  113.8 12.1 %collective-permute-start.36 = (f32[480,128]{1,0:T(8,128)S(1)}, f32[480,128]{1,0:T(8,128)S(1)}, u32[]{:S(2)}, u32[]{:S(2)}) collective-permute-start(f32[480,128]{1,0:T(8,128)S(1)} %get-tuple-element.85), channel_id=1, source_target_pairs={{0,96},{16,112},{32,64},{48,80},{64,32},{80,48},{96,0},{112,16},{1... | collective-permute-start | bytes 737288 | tf_op jit(solution)/shard_map/ppermute | solution.py:412
  119.8 10.6 %collective-permute-start.38 = (f32[480,128]{1,0:T(8,128)S(1)}, f32[480,128]{1,0:T(8,128)S(1)}, u32[]{:S(2)}, u32[]{:S(2)}) collective-permute-start(f32[480,128]{1,0:T(8,128)S(1)} %shard_map.83), channel_id=1, source_target_pairs={{0,32},{16,48},{32,0},{48,16},{64,96},{80,112},{96,64},{112,80},{1... | collective-permute-start | bytes 737288 | tf_op jit(solution)/shard_map/ppermute | solution.py:412
  120.6 9.7 %collective-permute-start.35 = (f32[480,128]{1,0:T(8,128)S(1)}, f32[480,128]{1,0:T(8,128)S(1)}, u32[]{:S(2)}, u32[]{:S(2)}) collective-permute-start(f32[480,128]{1,0:T(8,128)S(1)} %shard_map.82), channel_id=1, source_target_pairs={{0,96},{16,112},{32,64},{48,80},{64,32},{80,48},{96,0},{112,16},{1... | collective-permute-start | bytes 737288 | tf_op jit(solution)/shard_map/ppermute | solution.py:412

commit v3 on v2

--- a/solution.py
+++ b/solution.py
@@ -336,43 +336,83 @@
     )(*held(*args))
 
 
-def density_last_kernel(*refs):
-    before, near_0, near_1, far_0, far_1, kept_0, kept_1, whole = refs[6:]
-    term = before[...] + density_term(*refs[:6])
-    _, (y_a, y_b, y_far, y_own) = chip_column()
-    order = (y_own, y_a, y_b, y_far)
-    for q in range(QT):
+def block_columns(y):
+    return pl.multiple_of(256 * y, 128), pl.multiple_of(1024 + 128 * (y >> 1), 128)
+
+
+def in_row_order(value, target, order):
+    for q in range(value.shape[1] // 128):
         for i in range(OCC):
             for k in range(4):
                 row = (i * 4 + k) * 16
-                whole[q, i, order[k]] = term[row : row + 16, 128 * q : 128 * q + 128]
+                target[q, i, order[k]] = value[row : row + 16, 128 * q : 128 * q + 128]
+
+
+def put_block(target, whole, first, last, start, odd):
     low = lanes(32)
-    for target, start, k in (
-        (far_0, 0, 3), (far_1, 3, 3), (near_0, 0, 1), (near_1, 3, 2),
-        (kept_0.at[0], 0, 0), (kept_0.at[1], 0, 2), (kept_1.at[0], 3, 0), (kept_1.at[1], 3, 1),
+    for i in range(3):
+        for q in range(2):
+            row = (q * 3 + i) * VL
+            target[row : row + VL, :] = whole[first + q, start + i].reshape(VL, 128)
+        rest = whole[last, start + i].reshape(VL, 128)
+        rest = jnp.where(odd == 1, half_turn(rest), rest)
+        row = 6 * VL + 32 * i
+        target[row : row + 32, :] = jnp.where(low, rest[:32], half_turn(rest[32:]))
+
+
+def density_far_kernel(own, other, row_term, col_term, high, low, before, upper, lower, far_0, far_1, whole):
+    _, (y_a, y_b, y_far, y_own) = chip_column()
+    amplitude = split(amplitudes(own[...] + other[...], row_term[...], col_term[...]))
+    upper[...], lower[...] = amplitude
+    main, rest = block_columns(y_far)
+    right = [jnp.concatenate([ref[:, pl.ds(main, 256)], ref[:, pl.ds(rest, 128)]], axis=1) for ref in (high, low, before)]
+    in_row_order(right[2] + product(amplitude, right[:2], ((1,), (0,))), whole, (y_own, y_a, y_b, y_far))
+    for target, start in ((far_0, 0), (far_1, 3)):
+        put_block(target, whole, 0, 2, start, y_far & 1)
+
+
+def density_rest_kernel(upper, lower, high, low, before, near_0, near_1, kept_0, kept_1, whole):
+    _, (y_a, y_b, y_far, y_own) = chip_column()
+    order = (y_own, y_a, y_b, y_far)
+    amplitude = upper[...], lower[...]
+
+    def columns(at):
+        right = high[:, pl.ds(at, 256)], low[:, pl.ds(at, 256)]
+        return before[:, pl.ds(at, 256)] + product(amplitude, right, ((1,), (0,)))
+
+    in_row_order(columns(1024), whole.at[6:8], order)
+    for k, y in enumerate((y_own, y_a, y_b)):
+        in_row_order(columns(block_columns(y)[0]), whole.at[2 * k : 2 * k + 2], order)
+    for target, k, y, start in (
+        (near_0, 1, y_a, 0), (near_1, 2, y_b, 3),
+        (kept_0.at[0], 0, y_own, 0), (kept_0.at[1], 2, y_b, 0), (kept_1.at[0], 0, y_own, 3), (kept_1.at[1], 1, y_a, 3),
     ):
-        y = order[k]
-        for i in range(3):
-            for q in range(2):
-                row = (q * 3 + i) * VL
-                target[row : row + VL, :] = whole[2 * y + q, start + i].reshape(VL, 128)
-            rest = whole[8 + (y >> 1), start + i].reshape(VL, 128)
-            rest = jnp.where((y & 1) == 1, half_turn(rest), rest)
-            row = 6 * VL + 32 * i
-            target[row : row + 32, :] = jnp.where(low, rest[:32], half_turn(rest[32:]))
+        put_block(target, whole, 2 * k, 6 + (y >> 1), start, y & 1)
 
 
 def density_last(inputs, before):
     piece, two = near_memory((480, 128)), near_memory((2, 480, 128))
-    return pl.pallas_call(
-        density_last_kernel,
-        out_shape=(piece,) * 4 + (two,) * 2,
+    common = dict(compiler_params=settings(10), cost_estimate=cost(FLOPS // 2))
+    square = near_memory((OCC * VL, OCC * VL), BF16)
+    upper, lower, far_0, far_1 = pl.pallas_call(
+        density_far_kernel,
+        out_shape=(square, square, piece, piece),
         in_specs=[VMEM_SPEC] * 7,
-        out_specs=(VMEM_SPEC,) * 6,
-        scratch_shapes=[pltpu.VMEM((QT, OCC, 4, 16, 128), F32)],
-        compiler_params=settings(12),
-        cost_estimate=cost(FLOPS),
+        out_specs=(VMEM_SPEC,) * 4,
+        scratch_shapes=[pltpu.VMEM((3, OCC, 4, 16, 128), F32)],
+        name="density_far",
+        **common,
     )(*held(*inputs, before))
+    rest = pl.pallas_call(
+        density_rest_kernel,
+        out_shape=(piece, piece, two, two),
+        in_specs=[VMEM_SPEC] * 5,
+        out_specs=(VMEM_SPEC,) * 4,
+        scratch_shapes=[pltpu.VMEM((8, OCC, 4, 16, 128), F32)],
+        name="density_rest",
+        **common,
+    )(*held(upper, lower, *inputs[4:], before))
+    return (far_0, far_1, *rest)
 
 
 def unpack_kernel(kept_0, near_0, last_0, kept_1, near_1, last_1, result):
@@ -522,7 +562,7 @@
         inputs = (pair, other, row_term, col_terms[k], high, low)
         if k < 3:
             total = density_part(inputs, total)
-    near_0, near_1, far_0, far_1, kept_0, kept_1 = density_last(inputs, total)
+    far_0, far_1, near_0, near_1, kept_0, kept_1 = density_last(inputs, total)
     far_0, far_1 = on_aux(far_0, YA), on_aux(far_1, YB)
     near_0, near_1 = on_aux(near_0, YA), on_aux(near_1, YB)
     (last_0,) = small_call(final_relay_kernel, ((480, 128),), (kept_0, far_0))

time: 132 us -> 124 us (0.939)
  waiting for transfers between devices: 60.1 us -> 49.1 us
  starting transfers between devices: 47.8 us -> 49.8 us
    ppermute x18, waiting for transfers between devices: 33.2 us -> 19.7 us  [on_virt(): return lax.ppermute(value, 'virt', pairs)]
    ppermute x21, waiting for transfers between devices: 26.9 us -> 29.5 us  [on_aux(): return lax.ppermute(value, 'aux', pairs)]
    ppermute x18, starting transfers between devices: 28.7 us -> 31 us  [on_virt(): return lax.ppermute(value, 'virt', pairs)]
    pallas_call x1 -> x2, Pallas kernels: 2.31 us -> 2.82 us  [the longest x1 1.75 us: density_last(): pl.pallas_call(density_rest_kernel, out_shape=(piece, piece, two, two), i...]
  transfers between devices with their start and end apart: 39 -> 39, of which waited for: 16 -> 17; matrix products, arithmetic and copies ran while one was open for 0% -> 0% of each run, Pallas kernels for 12% -> 14%
where the time goes in v3:
time: 124 us; the launch traced here: 123 us
  starting transfers between devices  49.8 us (40%)
  waiting for transfers between devices  49.1 us (40%)
  Pallas kernels  23.7 us (19%)
    ppermute x18, starting transfers between devices, on_virt(): return lax.ppermute(value, 'virt', pairs)  31 us
    ppermute x21, waiting for transfers between devices, on_aux(): return lax.ppermute(value, 'aux', pairs)  29.5 us
    ppermute x18, waiting for transfers between devices, on_virt(): return lax.ppermute(value, 'virt', pairs)  19.7 us
    ppermute x21, starting transfers between devices, on_aux(): return lax.ppermute(value, 'aux', pairs)  18.9 us
    pallas_call x4, Pallas kernels, pair_part(): pl.pallas_call(pair_kernel, out_shape=(near_memory((OCC * VL, width)), pa...  7.35 us
    pallas_call x3, Pallas kernels, density_part(): pl.pallas_call(density_first_kernel if before is None else density_next_k...  5.59 us
    pallas_call x1, Pallas kernels, fitted_parts(): pl.pallas_call(partner_kernel, out_shape=(piece, piece, near_memory((OCC,...  3.69 us
  transfers between devices with their start and end apart: 39, of which 17 were waited for; matrix products, arithmetic and copies ran while one was open for 0% of the time, Pallas kernels for 14%

profile of v3, /device:TPU:0, one launch (start us, length us, event | category | flops | bytes accessed | tf_op | source)
XLA Modules:
  0.0 123.0 jit_solution(13584439332849081529)
XLA Ops:
  0.0 3.7 %fitted_for_partner.1 = (f32[2,2,6,10,8,128]{5,4,3,2,1,0:T(8,128)S(1)}, f32[2,2,6,10,8,128]{5,4,3,2,1,0:T(8,128)S(1)}, f32[6,64,320]{2,1,0:T(8,128)S(1)}, f32[4,320,384]{2,1,0:T(8,128)S(1)}) custom-call(f32[6,64,320]{2,1,0:T(8,128)} %bitcast.8, f32[320,2560]{1,0:T(8,128)} %bitcast.7), custom_call_target="tpu_custom_call" | custom-call | flops 377487360 | bytes 4194304 | tf_op jit(solution)/shard_map/fitted_for_partner/pallas_call | solution.py:157
  4.3 1.3 %fitted_for_self.1 = (f32[2,2,6,10,8,128]{5,4,3,2,1,0:T(8,128)S(1)}, f32[2,2,6,10,8,128]{5,4,3,2,1,0:T(8,128)S(1)}) custom-call(f32[6,64,320]{2,1,0:T(8,128)S(1)} %get-tuple-element.48.left, f32[4,320,384]{2,1,0:T(8,128)S(1)} %get-tuple-element.49.right), custom_call_target="tpu_custom_call" | custom-call | flops 377487360 | bytes 4194304 | tf_op jit(solution)/shard_map/fitted_for_self/pallas_call | solution.py:171
  6.4 3.2 %collective-permute-start.6 = (f32[6,10,8,128]{3,2,1,0:T(8,128)S(1)}, f32[6,10,8,128]{3,2,1,0:T(8,128)S(1)}, u32[]{:S(2)}, u32[]{:S(2)}) collective-permute-start(f32[6,10,8,128]{3,2,1,0:T(8,128)S(1)} %get-tuple-element.57), channel_id=1, source_target_pairs={{0,96},{16,112},{32,64},{48,80},{64,32},{80,48},{96,0},{112,16},{1... | collective-permute-start | bytes 737288 | tf_op jit(solution)/shard_map/ppermute | solution.py:452
  9.8 1.9 %collective-permute-start.2 = (f32[6,10,8,128]{3,2,1,0:T(8,128)S(1)}, f32[6,10,8,128]{3,2,1,0:T(8,128)S(1)}, u32[]{:S(2)}, u32[]{:S(2)}) collective-permute-start(f32[6,10,8,128]{3,2,1,0:T(8,128)S(1)} %get-tuple-element.54), channel_id=1, source_target_pairs={{0,32},{16,48},{32,0},{48,16},{64,96},{80,112},{96,64},{112,80},{1... | collective-permute-start | bytes 737288 | tf_op jit(solution)/shard_map/ppermute | solution.py:452
  11.8 4.8 %collective-permute-done.6.far = f32[6,10,8,128]{3,2,1,0:T(8,128)S(1)} collective-permute-done((f32[6,10,8,128]{3,2,1,0:T(8,128)S(1)}, f32[6,10,8,128]{3,2,1,0:T(8,128)S(1)}, u32[]{:S(2)}, u32[]{:S(2)}) %collective-permute-start.6) | collective-permute-done | bytes 245792 | tf_op jit(solution)/shard_map/ppermute | solution.py:452
  17.2 1.3 %collective-permute-done.4.far = f32[6,10,8,128]{3,2,1,0:T(8,128)S(1)} collective-permute-done((f32[6,10,8,128]{3,2,1,0:T(8,128)S(1)}, f32[6,10,8,128]{3,2,1,0:T(8,128)S(1)}, u32[]{:S(2)}, u32[]{:S(2)}) %collective-permute-start.4) | collective-permute-done | bytes 245792 | tf_op jit(solution)/shard_map/ppermute | solution.py:452
  18.5 1.5 %collective-permute-start.5 = (f32[6,10,8,128]{3,2,1,0:T(8,128)S(1)}, f32[6,10,8,128]{3,2,1,0:T(8,128)S(1)}, u32[]{:S(2)}, u32[]{:S(2)}) collective-permute-start(f32[6,10,8,128]{3,2,1,0:T(8,128)S(1)} %shard_map.65), channel_id=1, source_target_pairs={{0,96},{16,112},{32,64},{48,80},{64,32},{80,48},{96,0},{112,16},{1... | collective-permute-start | bytes 737288 | tf_op jit(solution)/shard_map/ppermute | solution.py:452
  20.0 1.1 terms.1
  21.1 6.8 %collective-permute-done.7.last_1 = f32[6,10,8,128]{3,2,1,0:T(8,128)S(1)} collective-permute-done((f32[6,10,8,128]{3,2,1,0:T(8,128)S(1)}, f32[6,10,8,128]{3,2,1,0:T(8,128)S(1)}, u32[]{:S(2)}, u32[]{:S(2)}) %collective-permute-start.7) | collective-permute-done | bytes 245792 | tf_op jit(solution)/shard_map/ppermute | solution.py:452
  28.7 1.5 %collective-permute-start.11 = (f32[2,6,10,8,128]{4,3,2,1,0:T(8,128)S(1)}, f32[2,6,10,8,128]{4,3,2,1,0:T(8,128)S(1)}, u32[]{:S(2)}, u32[]{:S(2)}) collective-permute-start(f32[2,6,10,8,128]{4,3,2,1,0:T(8,128)S(1)} %shard_map.67.own.refs_0_), channel_id=1, source_target_pairs={{0,1},{1,0},{2,3},{3,2},{4,5},{5,4},{6,7},{7,6},{8,9},{9,8},{10,11... | collective-permute-start | bytes 1474568 | tf_op jit(solution)/shard_map/ppermute | solution.py:448
  30.2 1.9 %collective-permute-start.15 = (f32[2,6,10,8,128]{4,3,2,1,0:T(8,128)S(1)}, f32[2,6,10,8,128]{4,3,2,1,0:T(8,128)S(1)}, u32[]{:S(2)}, u32[]{:S(2)}) collective-permute-start(f32[2,6,10,8,128]{4,3,2,1,0:T(8,128)S(1)} %shard_map.67.own.refs_0_), channel_id=1, source_target_pairs={{0,4},{1,5},{2,6},{3,7},{4,0},{5,1},{6,2},{7,3},{8,12},{9,13},{10,... | collective-permute-start | bytes 1474568 | tf_op jit(solution)/shard_map/ppermute | solution.py:448
  32.1 2.5 %collective-permute-start.16 = (f32[2,6,10,8,128]{4,3,2,1,0:T(8,128)S(1)}, f32[2,6,10,8,128]{4,3,2,1,0:T(8,128)S(1)}, u32[]{:S(2)}, u32[]{:S(2)}) collective-permute-start(f32[2,6,10,8,128]{4,3,2,1,0:T(8,128)S(1)} %shard_map.67.own.refs_0_), channel_id=1, source_target_pairs={{0,12},{1,13},{2,14},{3,15},{4,8},{5,9},{6,10},{7,11},{8,4},{9,5},... | collective-permute-start | bytes 1474568 | tf_op jit(solution)/shard_map/ppermute | solution.py:448
  34.7 2.1 %collective-permute-start.12 = (f32[2,6,10,8,128]{4,3,2,1,0:T(8,128)S(1)}, f32[2,6,10,8,128]{4,3,2,1,0:T(8,128)S(1)}, u32[]{:S(2)}, u32[]{:S(2)}) collective-permute-start(f32[2,6,10,8,128]{4,3,2,1,0:T(8,128)S(1)} %shard_map.67.own.refs_0_), channel_id=1, source_target_pairs={{0,3},{1,2},{2,1},{3,0},{4,7},{5,6},{6,5},{7,4},{8,11},{9,10},{10,... | collective-permute-start | bytes 1474568 | tf_op jit(solution)/shard_map/ppermute | solution.py:448
  36.8 5.0 %collective-permute-done.10.far = f32[2,6,10,8,128]{4,3,2,1,0:T(8,128)S(1)} collective-permute-done((f32[2,6,10,8,128]{4,3,2,1,0:T(8,128)S(1)}, f32[2,6,10,8,128]{4,3,2,1,0:T(8,128)S(1)}, u32[]{:S(2)}, u32[]{:S(2)}) %collective-permute-start.10) | collective-permute-done | bytes 491552 | tf_op jit(solution)/shard_map/ppermute | solution.py:452
  42.2 1.3 %collective-permute-start.9 = (f32[2,6,10,8,128]{4,3,2,1,0:T(8,128)S(1)}, f32[2,6,10,8,128]{4,3,2,1,0:T(8,128)S(1)}, u32[]{:S(2)}, u32[]{:S(2)}) collective-permute-start(f32[2,6,10,8,128]{4,3,2,1,0:T(8,128)S(1)} %shard_map.67.own.refs_0_), channel_id=1, source_target_pairs={{0,96},{16,112},{32,64},{48,80},{64,32},{80,48},{96,0},{112,16},{1... | collective-permute-start | bytes 1474568 | tf_op jit(solution)/shard_map/ppermute | solution.py:452
  43.5 2.8 %collective-permute-start.19 = (f32[6,10,8,128]{3,2,1,0:T(8,128)S(1)}, f32[6,10,8,128]{3,2,1,0:T(8,128)S(1)}, u32[]{:S(2)}, u32[]{:S(2)}) collective-permute-start(f32[6,10,8,128]{3,2,1,0:T(8,128)S(1)} %shard_map.70), channel_id=1, source_target_pairs={{0,3},{1,2},{2,1},{3,0},{4,7},{5,6},{6,5},{7,4},{8,11},{9,10},{10,... | collective-permute-start | bytes 737288 | tf_op jit(solution)/shard_map/ppermute | solution.py:448
  46.4 4.1 %collective-permute-start.22 = (f32[6,10,8,128]{3,2,1,0:T(8,128)S(1)}, f32[6,10,8,128]{3,2,1,0:T(8,128)S(1)}, u32[]{:S(2)}, u32[]{:S(2)}) collective-permute-start(f32[6,10,8,128]{3,2,1,0:T(8,128)S(1)} %shard_map.72), channel_id=1, source_target_pairs={{0,12},{1,13},{2,14},{3,15},{4,8},{5,9},{6,10},{7,11},{8,4},{9,5},... | collective-permute-start | bytes 737288 | tf_op jit(solution)/shard_map/ppermute | solution.py:448
  50.5 1.6 %collective-permute-done.19.refs_1_ = f32[6,10,8,128]{3,2,1,0:T(8,128)S(1)} collective-permute-done((f32[6,10,8,128]{3,2,1,0:T(8,128)S(1)}, f32[6,10,8,128]{3,2,1,0:T(8,128)S(1)}, u32[]{:S(2)}, u32[]{:S(2)}) %collective-permute-start.19) | collective-permute-done | bytes 245792 | tf_op jit(solution)/shard_map/ppermute | solution.py:448
  52.1 2.9 %collective-permute-start.20 = (f32[6,10,8,128]{3,2,1,0:T(8,128)S(1)}, f32[6,10,8,128]{3,2,1,0:T(8,128)S(1)}, u32[]{:S(2)}, u32[]{:S(2)}) collective-permute-start(f32[6,10,8,128]{3,2,1,0:T(8,128)S(1)} %collective-permute-done.19.refs_1_), channel_id=1, source_target_pairs={{0,12},{1,13},{2,14},{3,15},{4,8},{5,9},{6,10},{7,11},{8,4},{9,5},... | collective-permute-start | bytes 737288 | tf_op jit(solution)/shard_map/ppermute | solution.py:448
  55.1 0.9 collective-permute-done.22.refs_2_
  56.0 1.8 %collective-permute-start.23 = (f32[6,10,8,128]{3,2,1,0:T(8,128)S(1)}, f32[6,10,8,128]{3,2,1,0:T(8,128)S(1)}, u32[]{:S(2)}, u32[]{:S(2)}) collective-permute-start(f32[6,10,8,128]{3,2,1,0:T(8,128)S(1)} %collective-permute-done.22.refs_2_), channel_id=1, source_target_pairs={{0,3},{1,2},{2,1},{3,0},{4,7},{5,6},{6,5},{7,4},{8,11},{9,10},{10,... | collective-permute-start | bytes 737288 | tf_op jit(solution)/shard_map/ppermute | solution.py:448
  58.0 1.5 %collective-permute-start.27 = (f32[2,6,10,8,128]{4,3,2,1,0:T(8,128)S(1)}, f32[2,6,10,8,128]{4,3,2,1,0:T(8,128)S(1)}, u32[]{:S(2)}, u32[]{:S(2)}) collective-permute-start(f32[2,6,10,8,128]{4,3,2,1,0:T(8,128)S(1)} %shard_map.69), channel_id=1, source_target_pairs={{0,3},{1,2},{2,1},{3,0},{4,7},{5,6},{6,5},{7,4},{8,11},{9,10},{10,... | collective-permute-start | bytes 1474568 | tf_op jit(solution)/shard_map/ppermute | solution.py:448
  60.0 1.6 %collective-permute-start.29 = (f32[6,10,8,128]{3,2,1,0:T(8,128)S(1)}, f32[6,10,8,128]{3,2,1,0:T(8,128)S(1)}, u32[]{:S(2)}, u32[]{:S(2)}) collective-permute-start(f32[6,10,8,128]{3,2,1,0:T(8,128)S(1)} %collective-permute-done.19.refs_1_), channel_id=1, source_target_pairs={{0,4},{1,5},{2,6},{3,7},{4,0},{5,1},{6,2},{7,3},{8,12},{9,13},{10,... | collective-permute-start | bytes 737288 | tf_op jit(solution)/shard_map/ppermute | solution.py:448
  61.5 4.5 %collective-permute-done.23.far.refs_6_ = f32[6,10,8,128]{3,2,1,0:T(8,128)S(1)} collective-permute-done((f32[6,10,8,128]{3,2,1,0:T(8,128)S(1)}, f32[6,10,8,128]{3,2,1,0:T(8,128)S(1)}, u32[]{:S(2)}, u32[]{:S(2)}) %collective-permute-start.23) | collective-permute-done | bytes 245792 | tf_op jit(solution)/shard_map/ppermute | solution.py:448
  66.0 7.6 %collective-permute-done.29.refs_3_ = f32[6,10,8,128]{3,2,1,0:T(8,128)S(1)} collective-permute-done((f32[6,10,8,128]{3,2,1,0:T(8,128)S(1)}, f32[6,10,8,128]{3,2,1,0:T(8,128)S(1)}, u32[]{:S(2)}, u32[]{:S(2)}) %collective-permute-start.29) | collective-permute-done | bytes 245792 | tf_op jit(solution)/shard_map/ppermute | solution.py:448
  73.6 3.5 %collective-permute-start.26 = (f32[2,6,10,8,128]{4,3,2,1,0:T(8,128)S(1)}, f32[2,6,10,8,128]{4,3,2,1,0:T(8,128)S(1)}, u32[]{:S(2)}, u32[]{:S(2)}) collective-permute-start(f32[2,6,10,8,128]{4,3,2,1,0:T(8,128)S(1)} %shard_map.68), channel_id=1, source_target_pairs={{0,12},{1,13},{2,14},{3,15},{4,8},{5,9},{6,10},{7,11},{8,4},{9,5},... | collective-permute-start | bytes 1474568 | tf_op jit(solution)/shard_map/ppermute | solution.py:448
  77.1 2.0 %collective-permute-start.24 = (f32[2,6,10,8,128]{4,3,2,1,0:T(8,128)S(1)}, f32[2,6,10,8,128]{4,3,2,1,0:T(8,128)S(1)}, u32[]{:S(2)}, u32[]{:S(2)}) collective-permute-start(f32[2,6,10,8,128]{4,3,2,1,0:T(8,128)S(1)} %shard_map.73), channel_id=1, source_target_pairs={{0,1},{1,0},{2,3},{3,2},{4,5},{5,4},{6,7},{7,6},{8,9},{9,8},{10,11... | collective-permute-start | bytes 1474568 | tf_op jit(solution)/shard_map/ppermute | solution.py:448
  79.4 2.4 %collective-permute-start.14 = (f32[2,6,10,8,128]{4,3,2,1,0:T(8,128)S(1)}, f32[2,6,10,8,128]{4,3,2,1,0:T(8,128)S(1)}, u32[]{:S(2)}, u32[]{:S(2)}) collective-permute-start(f32[2,6,10,8,128]{4,3,2,1,0:T(8,128)S(1)} %collective-permute-done.13.refs_0_), channel_id=1, source_target_pairs={{0,12},{1,13},{2,14},{3,15},{4,8},{5,9},{6,10},{7,11},{8,4},{9,5},... | collective-permute-start | bytes 1474568 | tf_op jit(solution)/shard_map/ppermute | solution.py:448
  82.1 1.8 %shard_map.77 = (f32[384,384]{1,0:T(8,128)S(1)}, bf16[384,1280]{1,0:T(8,128)(2,1)S(1)}, bf16[384,1280]{1,0:T(8,128)(2,1)S(1)}) custom-call(bf16[384,1280]{1,0:T(8,128)(2,1)S(1)} %get-tuple-element.64.left_high, bf16[384,1280]{1,0:T(8,128)(2,1)S(1)} %get-tuple-element.65.left_low, f32[2,6,10,8,128]{4,3,2,1,0:T(8,128)S(1)} %collective-permute-done.11.first.value.refs_0_, ...), custom_call_target="tpu_custom_call" | custom-call | flops 1132462080 | bytes 4194304 | tf_op jit(solution)/shard_map/pallas_call | solution.py:282
  84.0 3.7 %collective-permute-done.26.refs_1_ = f32[2,6,10,8,128]{4,3,2,1,0:T(8,128)S(1)} collective-permute-done((f32[2,6,10,8,128]{4,3,2,1,0:T(8,128)S(1)}, f32[2,6,10,8,128]{4,3,2,1,0:T(8,128)S(1)}, u32[]{:S(2)}, u32[]{:S(2)}) %collective-permute-start.26) | collective-permute-done | bytes 491552 | tf_op jit(solution)/shard_map/ppermute | solution.py:448
  87.7 1.8 %shard_map.76 = (f32[384,384]{1,0:T(8,128)S(1)}, bf16[384,1280]{1,0:T(8,128)(2,1)S(1)}, bf16[384,1280]{1,0:T(8,128)(2,1)S(1)}) custom-call(bf16[384,1280]{1,0:T(8,128)(2,1)S(1)} %get-tuple-element.64.left_high, bf16[384,1280]{1,0:T(8,128)(2,1)S(1)} %get-tuple-element.65.left_low, f32[2,6,10,8,128]{4,3,2,1,0:T(8,128)S(1)} %shard_map.67.own.refs_0_, ...), custom_call_target="tpu_custom_call" | custom-call | flops 1132462080 | bytes 4194304 | tf_op jit(solution)/shard_map/pallas_call | solution.py:282
  90.1 1.8 %shard_map.75 = (f32[384,384]{1,0:T(8,128)S(1)}, bf16[384,1280]{1,0:T(8,128)(2,1)S(1)}, bf16[384,1280]{1,0:T(8,128)(2,1)S(1)}) custom-call(bf16[384,1280]{1,0:T(8,128)(2,1)S(1)} %get-tuple-element.64.left_high, bf16[384,1280]{1,0:T(8,128)(2,1)S(1)} %get-tuple-element.65.left_low, f32[2,6,10,8,128]{4,3,2,1,0:T(8,128)S(1)} %collective-permute-done.13.refs_0_, ...), custom_call_target="tpu_custom_call" | custom-call | flops 1132462080 | bytes 4194304 | tf_op jit(solution)/shard_map/pallas_call | solution.py:282
  92.1 0.8 collective-permute-done.14.refs_0_
  92.9 1.8 %shard_map.74 = (f32[384,384]{1,0:T(8,128)S(1)}, bf16[384,1280]{1,0:T(8,128)(2,1)S(1)}, bf16[384,1280]{1,0:T(8,128)(2,1)S(1)}) custom-call(bf16[384,1280]{1,0:T(8,128)(2,1)S(1)} %get-tuple-element.64.left_high, bf16[384,1280]{1,0:T(8,128)(2,1)S(1)} %get-tuple-element.65.left_low, f32[2,6,10,8,128]{4,3,2,1,0:T(8,128)S(1)} %collective-permute-done.14.refs_0_, ...), custom_call_target="tpu_custom_call" | custom-call | flops 1132462080 | bytes 4194304 | tf_op jit(solution)/shard_map/pallas_call | solution.py:282
  94.9 1.8 %shard_map.78.refs_6_ = f32[384,1280]{1,0:T(8,128)S(1)} custom-call(f32[384,384]{1,0:T(8,128)S(1)} %get-tuple-element.79.refs_0_, f32[384,384]{1,0:T(8,128)S(1)} %collective-permute-done.32.refs_1_, f32[384,1]{1,0:T(8,128)S(1)} %get-tuple-element.67.refs_2_.row_term, f32[1,384]{1,0:T(1,128)S(1)} %get-tuple-element.80.refs_3_, ...), custom_call_target="tpu_custom_call" | custom-call | flops 1132462080 | bytes 4194304 | tf_op jit(solution)/shard_map/pallas_call | solution.py:329
  96.7 1.9 %shard_map.79.refs_6_ = f32[384,1280]{1,0:T(8,128)S(1)} custom-call(f32[384,384]{1,0:T(8,128)S(1)} %get-tuple-element.75.refs_0_, f32[384,384]{1,0:T(8,128)S(1)} %collective-permute-done.31.refs_1_, f32[384,1]{1,0:T(8,128)S(1)} %get-tuple-element.67.refs_2_.row_term, f32[1,384]{1,0:T(1,128)S(1)} %get-tuple-element.76.refs_3_, ...), custom_call_target="tpu_custom_call" | custom-call | flops 1132462080 | bytes 4194304 | tf_op jit(solution)/shard_map/pallas_call | solution.py:329
  98.6 1.9 %shard_map.80.before = f32[384,1280]{1,0:T(8,128)S(1)} custom-call(f32[384,384]{1,0:T(8,128)S(1)} %get-tuple-element.71.refs_0_, f32[384,384]{1,0:T(8,128)S(1)} %collective-permute-done.28.refs_1_, f32[384,1]{1,0:T(8,128)S(1)} %get-tuple-element.67.refs_2_.row_term, f32[1,384]{1,0:T(1,128)S(1)} %get-tuple-element.72.refs_3_, ...), custom_call_target="tpu_custom_call" | custom-call | flops 1132462080 | bytes 4194304 | tf_op jit(solution)/shard_map/pallas_call | solution.py:329
  100.5 1.1 density_far.1
  101.6 1.0 collective-permute-start.37
  102.6 1.8 %density_rest.1 = (f32[480,128]{1,0:T(8,128)S(1)}, f32[480,128]{1,0:T(8,128)S(1)}, f32[2,480,128]{2,1,0:T(8,128)S(1)}, f32[2,480,128]{2,1,0:T(8,128)S(1)}) custom-call(bf16[384,384]{1,0:T(8,128)(2,1)S(1)} %get-tuple-element.83.upper, bf16[384,384]{1,0:T(8,128)(2,1)S(1)} %get-tuple-element.84.lower, bf16[384,1280]{1,0:T(8,128)(2,1)S(1)} %get-tuple-element.69.high, ...), custom_call_target="tpu_custom_call" | custom-call | flops 566231040 | bytes 4194304 | tf_op jit(solution)/shard_map/density_rest/pallas_call | solution.py:406
  104.3 2.1 %collective-permute-start.33 = (f32[480,128]{1,0:T(8,128)S(1)}, f32[480,128]{1,0:T(8,128)S(1)}, u32[]{:S(2)}, u32[]{:S(2)}) collective-permute-start(f32[480,128]{1,0:T(8,128)S(1)} %get-tuple-element.86), channel_id=1, source_target_pairs={{0,32},{16,48},{32,0},{48,16},{64,96},{80,112},{96,64},{112,80},{1... | collective-permute-start | bytes 737288 | tf_op jit(solution)/shard_map/ppermute | solution.py:452
  106.4 2.6 %collective-permute-start.36 = (f32[480,128]{1,0:T(8,128)S(1)}, f32[480,128]{1,0:T(8,128)S(1)}, u32[]{:S(2)}, u32[]{:S(2)}) collective-permute-start(f32[480,128]{1,0:T(8,128)S(1)} %get-tuple-element.89), channel_id=1, source_target_pairs={{0,96},{16,112},{32,64},{48,80},{64,32},{80,48},{96,0},{112,16},{1... | collective-permute-start | bytes 737288 | tf_op jit(solution)/shard_map/ppermute | solution.py:452
  109.0 2.9 %collective-permute-done.37.far = f32[480,128]{1,0:T(8,128)S(1)} collective-permute-done((f32[480,128]{1,0:T(8,128)S(1)}, f32[480,128]{1,0:T(8,128)S(1)}, u32[]{:S(2)}, u32[]{:S(2)}) %collective-permute-start.37) | collective-permute-done | bytes 245792 | tf_op jit(solution)/shard_map/ppermute | solution.py:452
  112.1 2.0 %collective-permute-start.35 = (f32[480,128]{1,0:T(8,128)S(1)}, f32[480,128]{1,0:T(8,128)S(1)}, u32[]{:S(2)}, u32[]{:S(2)}) collective-permute-start(f32[480,128]{1,0:T(8,128)S(1)} %shard_map.81), channel_id=1, source_target_pairs={{0,96},{16,112},{32,64},{48,80},{64,32},{80,48},{96,0},{112,16},{1... | collective-permute-start | bytes 737288 | tf_op jit(solution)/shard_map/ppermute | solution.py:452
  114.1 2.6 %collective-permute-done.33.near_0 = f32[480,128]{1,0:T(8,128)S(1)} collective-permute-done((f32[480,128]{1,0:T(8,128)S(1)}, f32[480,128]{1,0:T(8,128)S(1)}, u32[]{:S(2)}, u32[]{:S(2)}) %collective-permute-start.33) | collective-permute-done | bytes 245792 | tf_op jit(solution)/shard_map/ppermute | solution.py:452
  117.2 4.0 %collective-permute-done.38.last_1 = f32[480,128]{1,0:T(8,128)S(1)} collective-permute-done((f32[480,128]{1,0:T(8,128)S(1)}, f32[480,128]{1,0:T(8,128)S(1)}, u32[]{:S(2)}, u32[]{:S(2)}) %collective-permute-start.38) | collective-permute-done | bytes 245792 | tf_op jit(solution)/shard_map/ppermute | solution.py:452
  121.2 0.8 collective-permute-done.35.last_0
  122.0 1.0 unpack.1
  (64 shorter events, 6.2 us)
Async XLA Ops:
  3.7 2.6 %collective-permute-start.1 = (f32[2,2,6,10,8,128]{5,4,3,2,1,0:T(8,128)S(1)}, f32[2,2,6,10,8,128]{5,4,3,2,1,0:T(8,128)S(1)}, u32[]{:S(2)}, u32[]{:S(2)}) collective-permute-start(f32[2,2,6,10,8,128]{5,4,3,2,1,0:T(8,128)S(1)} %get-tuple-element.53), channel_id=1, source_target_pairs={{0,16},{16,0},{32,48},{48,32},{64,80},{80,64},{96,112},{112,96},{1... | collective-permute-start | bytes 2949128 | tf_op jit(solution)/shard_map/ppermute | solution.py:452
  3.8 8.0 %collective-permute-start = (f32[2,2,6,10,8,128]{5,4,3,2,1,0:T(8,128)S(1)}, f32[2,2,6,10,8,128]{5,4,3,2,1,0:T(8,128)S(1)}, u32[]{:S(2)}, u32[]{:S(2)}) collective-permute-start(f32[2,2,6,10,8,128]{5,4,3,2,1,0:T(8,128)S(1)} %get-tuple-element.51), channel_id=1, source_target_pairs={{0,16},{16,0},{32,48},{48,32},{64,80},{80,64},{96,112},{112,96},{1... | collective-permute-start | bytes 2949128 | tf_op jit(solution)/shard_map/ppermute | solution.py:452
  6.4 10.1 %collective-permute-start.6 = (f32[6,10,8,128]{3,2,1,0:T(8,128)S(1)}, f32[6,10,8,128]{3,2,1,0:T(8,128)S(1)}, u32[]{:S(2)}, u32[]{:S(2)}) collective-permute-start(f32[6,10,8,128]{3,2,1,0:T(8,128)S(1)} %get-tuple-element.57), channel_id=1, source_target_pairs={{0,96},{16,112},{32,64},{48,80},{64,32},{80,48},{96,0},{112,16},{1... | collective-permute-start | bytes 737288 | tf_op jit(solution)/shard_map/ppermute | solution.py:452
  9.7 8.8 %collective-permute-start.4 = (f32[6,10,8,128]{3,2,1,0:T(8,128)S(1)}, f32[6,10,8,128]{3,2,1,0:T(8,128)S(1)}, u32[]{:S(2)}, u32[]{:S(2)}) collective-permute-start(f32[6,10,8,128]{3,2,1,0:T(8,128)S(1)} %get-tuple-element.56), channel_id=1, source_target_pairs={{0,32},{16,48},{32,0},{48,16},{64,96},{80,112},{96,64},{112,80},{1... | collective-permute-start | bytes 737288 | tf_op jit(solution)/shard_map/ppermute | solution.py:452
  9.8 18.1 %collective-permute-start.2 = (f32[6,10,8,128]{3,2,1,0:T(8,128)S(1)}, f32[6,10,8,128]{3,2,1,0:T(8,128)S(1)}, u32[]{:S(2)}, u32[]{:S(2)}) collective-permute-start(f32[6,10,8,128]{3,2,1,0:T(8,128)S(1)} %get-tuple-element.54), channel_id=1, source_target_pairs={{0,32},{16,48},{32,0},{48,16},{64,96},{80,112},{96,64},{112,80},{1... | collective-permute-start | bytes 737288 | tf_op jit(solution)/shard_map/ppermute | solution.py:452
  11.7 16.2 %collective-permute-start.3 = (f32[6,10,8,128]{3,2,1,0:T(8,128)S(1)}, f32[6,10,8,128]{3,2,1,0:T(8,128)S(1)}, u32[]{:S(2)}, u32[]{:S(2)}) collective-permute-start(f32[6,10,8,128]{3,2,1,0:T(8,128)S(1)} %get-tuple-element.55), channel_id=1, source_target_pairs={{0,96},{16,112},{32,64},{48,80},{64,32},{80,48},{96,0},{112,16},{1... | collective-permute-start | bytes 737288 | tf_op jit(solution)/shard_map/ppermute | solution.py:452
  16.6 3.4 %copy-start = (f32[1024]{0:T(1024)S(1)}, f32[1024]{0:T(1024)}, u32[]{:S(2)}) copy-start(f32[1024]{0:T(1024)} %param.9) | copy-start | bytes 12292
  16.6 3.4 %copy-start.1 = (s32[1024]{0:T(1024)S(1)}, s32[1024]{0:T(1024)}, u32[]{:S(2)}) copy-start(s32[1024]{0:T(1024)} %param.11) | copy-start | bytes 12292
  16.6 3.4 %copy-start.2 = (f32[256]{0:T(256)S(1)}, f32[256]{0:T(256)}, u32[]{:S(2)}) copy-start(f32[256]{0:T(256)} %occ_energy.1) | copy-start | bytes 3076
  16.6 3.4 %copy-start.3 = (s32[6]{0:T(128)S(1)}, s32[6]{0:T(128)}, u32[]{:S(2)}) copy-start(s32[6]{0:T(128)} %batch_index.1) | copy-start | bytes 76
  16.6 11.3 %collective-permute-start.7 = (f32[6,10,8,128]{3,2,1,0:T(8,128)S(1)}, f32[6,10,8,128]{3,2,1,0:T(8,128)S(1)}, u32[]{:S(2)}, u32[]{:S(2)}) collective-permute-start(f32[6,10,8,128]{3,2,1,0:T(8,128)S(1)} %shard_map.66), channel_id=1, source_target_pairs={{0,32},{16,48},{32,0},{48,16},{64,96},{80,112},{96,64},{112,80},{1... | collective-permute-start | bytes 737288 | tf_op jit(solution)/shard_map/ppermute | solution.py:452
  18.5 9.4 %collective-permute-start.5 = (f32[6,10,8,128]{3,2,1,0:T(8,128)S(1)}, f32[6,10,8,128]{3,2,1,0:T(8,128)S(1)}, u32[]{:S(2)}, u32[]{:S(2)}) collective-permute-start(f32[6,10,8,128]{3,2,1,0:T(8,128)S(1)} %shard_map.65), channel_id=1, source_target_pairs={{0,96},{16,112},{32,64},{48,80},{64,32},{80,48},{96,0},{112,16},{1... | collective-permute-start | bytes 737288 | tf_op jit(solution)/shard_map/ppermute | solution.py:452
  28.0 13.7 %collective-permute-start.10 = (f32[2,6,10,8,128]{4,3,2,1,0:T(8,128)S(1)}, f32[2,6,10,8,128]{4,3,2,1,0:T(8,128)S(1)}, u32[]{:S(2)}, u32[]{:S(2)}) collective-permute-start(f32[2,6,10,8,128]{4,3,2,1,0:T(8,128)S(1)} %shard_map.67.own.refs_0_), channel_id=1, source_target_pairs={{0,64},{16,80},{32,96},{48,112},{64,0},{80,16},{96,32},{112,48},{1... | collective-permute-start | bytes 1474568 | tf_op jit(solution)/shard_map/ppermute | solution.py:452
  28.7 13.4 %collective-permute-start.11 = (f32[2,6,10,8,128]{4,3,2,1,0:T(8,128)S(1)}, f32[2,6,10,8,128]{4,3,2,1,0:T(8,128)S(1)}, u32[]{:S(2)}, u32[]{:S(2)}) collective-permute-start(f32[2,6,10,8,128]{4,3,2,1,0:T(8,128)S(1)} %shard_map.67.own.refs_0_), channel_id=1, source_target_pairs={{0,1},{1,0},{2,3},{3,2},{4,5},{5,4},{6,7},{7,6},{8,9},{9,8},{10,11... | collective-permute-start | bytes 1474568 | tf_op jit(solution)/shard_map/ppermute | solution.py:448
  30.2 13.3 %collective-permute-start.15 = (f32[2,6,10,8,128]{4,3,2,1,0:T(8,128)S(1)}, f32[2,6,10,8,128]{4,3,2,1,0:T(8,128)S(1)}, u32[]{:S(2)}, u32[]{:S(2)}) collective-permute-start(f32[2,6,10,8,128]{4,3,2,1,0:T(8,128)S(1)} %shard_map.67.own.refs_0_), channel_id=1, source_target_pairs={{0,4},{1,5},{2,6},{3,7},{4,0},{5,1},{6,2},{7,3},{8,12},{9,13},{10,... | collective-permute-start | bytes 1474568 | tf_op jit(solution)/shard_map/ppermute | solution.py:448
  32.1 14.2 %collective-permute-start.16 = (f32[2,6,10,8,128]{4,3,2,1,0:T(8,128)S(1)}, f32[2,6,10,8,128]{4,3,2,1,0:T(8,128)S(1)}, u32[]{:S(2)}, u32[]{:S(2)}) collective-permute-start(f32[2,6,10,8,128]{4,3,2,1,0:T(8,128)S(1)} %shard_map.67.own.refs_0_), channel_id=1, source_target_pairs={{0,12},{1,13},{2,14},{3,15},{4,8},{5,9},{6,10},{7,11},{8,4},{9,5},... | collective-permute-start | bytes 1474568 | tf_op jit(solution)/shard_map/ppermute | solution.py:448
  34.7 23.2 %collective-permute-start.12 = (f32[2,6,10,8,128]{4,3,2,1,0:T(8,128)S(1)}, f32[2,6,10,8,128]{4,3,2,1,0:T(8,128)S(1)}, u32[]{:S(2)}, u32[]{:S(2)}) collective-permute-start(f32[2,6,10,8,128]{4,3,2,1,0:T(8,128)S(1)} %shard_map.67.own.refs_0_), channel_id=1, source_target_pairs={{0,3},{1,2},{2,1},{3,0},{4,7},{5,6},{6,5},{7,4},{8,11},{9,10},{10,... | collective-permute-start | bytes 1474568 | tf_op jit(solution)/shard_map/ppermute | solution.py:448
  41.7 16.3 %collective-permute-start.8 = (f32[2,6,10,8,128]{4,3,2,1,0:T(8,128)S(1)}, f32[2,6,10,8,128]{4,3,2,1,0:T(8,128)S(1)}, u32[]{:S(2)}, u32[]{:S(2)}) collective-permute-start(f32[2,6,10,8,128]{4,3,2,1,0:T(8,128)S(1)} %shard_map.67.own.refs_0_), channel_id=1, source_target_pairs={{0,32},{16,48},{32,0},{48,16},{64,96},{80,112},{96,64},{112,80},{1... | collective-permute-start | bytes 1474568 | tf_op jit(solution)/shard_map/ppermute | solution.py:452
  42.2 17.3 %collective-permute-start.9 = (f32[2,6,10,8,128]{4,3,2,1,0:T(8,128)S(1)}, f32[2,6,10,8,128]{4,3,2,1,0:T(8,128)S(1)}, u32[]{:S(2)}, u32[]{:S(2)}) collective-permute-start(f32[2,6,10,8,128]{4,3,2,1,0:T(8,128)S(1)} %shard_map.67.own.refs_0_), channel_id=1, source_target_pairs={{0,96},{16,112},{32,64},{48,80},{64,32},{80,48},{96,0},{112,16},{1... | collective-permute-start | bytes 1474568 | tf_op jit(solution)/shard_map/ppermute | solution.py:452
  43.5 8.6 %collective-permute-start.19 = (f32[6,10,8,128]{3,2,1,0:T(8,128)S(1)}, f32[6,10,8,128]{3,2,1,0:T(8,128)S(1)}, u32[]{:S(2)}, u32[]{:S(2)}) collective-permute-start(f32[6,10,8,128]{3,2,1,0:T(8,128)S(1)} %shard_map.70), channel_id=1, source_target_pairs={{0,3},{1,2},{2,1},{3,0},{4,7},{5,6},{6,5},{7,4},{8,11},{9,10},{10,... | collective-permute-start | bytes 737288 | tf_op jit(solution)/shard_map/ppermute | solution.py:448
  46.4 9.6 %collective-permute-start.22 = (f32[6,10,8,128]{3,2,1,0:T(8,128)S(1)}, f32[6,10,8,128]{3,2,1,0:T(8,128)S(1)}, u32[]{:S(2)}, u32[]{:S(2)}) collective-permute-start(f32[6,10,8,128]{3,2,1,0:T(8,128)S(1)} %shard_map.72), channel_id=1, source_target_pairs={{0,12},{1,13},{2,14},{3,15},{4,8},{5,9},{6,10},{7,11},{8,4},{9,5},... | collective-permute-start | bytes 737288 | tf_op jit(solution)/shard_map/ppermute | solution.py:448
  52.1 7.8 %collective-permute-start.20 = (f32[6,10,8,128]{3,2,1,0:T(8,128)S(1)}, f32[6,10,8,128]{3,2,1,0:T(8,128)S(1)}, u32[]{:S(2)}, u32[]{:S(2)}) collective-permute-start(f32[6,10,8,128]{3,2,1,0:T(8,128)S(1)} %collective-permute-done.19.refs_1_), channel_id=1, source_target_pairs={{0,12},{1,13},{2,14},{3,15},{4,8},{5,9},{6,10},{7,11},{8,4},{9,5},... | collective-permute-start | bytes 737288 | tf_op jit(solution)/shard_map/ppermute | solution.py:448
  56.0 10.0 %collective-permute-start.23 = (f32[6,10,8,128]{3,2,1,0:T(8,128)S(1)}, f32[6,10,8,128]{3,2,1,0:T(8,128)S(1)}, u32[]{:S(2)}, u32[]{:S(2)}) collective-permute-start(f32[6,10,8,128]{3,2,1,0:T(8,128)S(1)} %collective-permute-done.22.refs_2_), channel_id=1, source_target_pairs={{0,3},{1,2},{2,1},{3,0},{4,7},{5,6},{6,5},{7,4},{8,11},{9,10},{10,... | collective-permute-start | bytes 737288 | tf_op jit(solution)/shard_map/ppermute | solution.py:448
  57.9 21.4 %collective-permute-start.17 = (f32[2,6,10,8,128]{4,3,2,1,0:T(8,128)S(1)}, f32[2,6,10,8,128]{4,3,2,1,0:T(8,128)S(1)}, u32[]{:S(2)}, u32[]{:S(2)}) collective-permute-start(f32[2,6,10,8,128]{4,3,2,1,0:T(8,128)S(1)} %shard_map.69), channel_id=1, source_target_pairs={{0,1},{1,0},{2,3},{3,2},{4,5},{5,4},{6,7},{7,6},{8,9},{9,8},{10,11... | collective-permute-start | bytes 1474568 | tf_op jit(solution)/shard_map/ppermute | solution.py:448
  58.0 21.3 %collective-permute-start.27 = (f32[2,6,10,8,128]{4,3,2,1,0:T(8,128)S(1)}, f32[2,6,10,8,128]{4,3,2,1,0:T(8,128)S(1)}, u32[]{:S(2)}, u32[]{:S(2)}) collective-permute-start(f32[2,6,10,8,128]{4,3,2,1,0:T(8,128)S(1)} %shard_map.69), channel_id=1, source_target_pairs={{0,3},{1,2},{2,1},{3,0},{4,7},{5,6},{6,5},{7,4},{8,11},{9,10},{10,... | collective-permute-start | bytes 1474568 | tf_op jit(solution)/shard_map/ppermute | solution.py:448
  59.5 19.9 %collective-permute-start.13 = (f32[2,6,10,8,128]{4,3,2,1,0:T(8,128)S(1)}, f32[2,6,10,8,128]{4,3,2,1,0:T(8,128)S(1)}, u32[]{:S(2)}, u32[]{:S(2)}) collective-permute-start(f32[2,6,10,8,128]{4,3,2,1,0:T(8,128)S(1)} %shard_map.68), channel_id=1, source_target_pairs={{0,4},{1,5},{2,6},{3,7},{4,0},{5,1},{6,2},{7,3},{8,12},{9,13},{10,... | collective-permute-start | bytes 1474568 | tf_op jit(solution)/shard_map/ppermute | solution.py:448
  60.0 13.6 %collective-permute-start.29 = (f32[6,10,8,128]{3,2,1,0:T(8,128)S(1)}, f32[6,10,8,128]{3,2,1,0:T(8,128)S(1)}, u32[]{:S(2)}, u32[]{:S(2)}) collective-permute-start(f32[6,10,8,128]{3,2,1,0:T(8,128)S(1)} %collective-permute-done.19.refs_1_), channel_id=1, source_target_pairs={{0,4},{1,5},{2,6},{3,7},{4,0},{5,1},{6,2},{7,3},{8,12},{9,13},{10,... | collective-permute-start | bytes 737288 | tf_op jit(solution)/shard_map/ppermute | solution.py:448
  66.0 11.1 %collective-permute-start.30 = (f32[6,10,8,128]{3,2,1,0:T(8,128)S(1)}, f32[6,10,8,128]{3,2,1,0:T(8,128)S(1)}, u32[]{:S(2)}, u32[]{:S(2)}) collective-permute-start(f32[6,10,8,128]{3,2,1,0:T(8,128)S(1)} %collective-permute-done.22.refs_2_), channel_id=1, source_target_pairs={{0,1},{1,0},{2,3},{3,2},{4,5},{5,4},{6,7},{7,6},{8,9},{9,8},{10,11... | collective-permute-start | bytes 737288 | tf_op jit(solution)/shard_map/ppermute | solution.py:448
  73.6 14.1 %collective-permute-start.26 = (f32[2,6,10,8,128]{4,3,2,1,0:T(8,128)S(1)}, f32[2,6,10,8,128]{4,3,2,1,0:T(8,128)S(1)}, u32[]{:S(2)}, u32[]{:S(2)}) collective-permute-start(f32[2,6,10,8,128]{4,3,2,1,0:T(8,128)S(1)} %shard_map.68), channel_id=1, source_target_pairs={{0,12},{1,13},{2,14},{3,15},{4,8},{5,9},{6,10},{7,11},{8,4},{9,5},... | collective-permute-start | bytes 1474568 | tf_op jit(solution)/shard_map/ppermute | solution.py:448
  77.1 12.4 %collective-permute-start.24 = (f32[2,6,10,8,128]{4,3,2,1,0:T(8,128)S(1)}, f32[2,6,10,8,128]{4,3,2,1,0:T(8,128)S(1)}, u32[]{:S(2)}, u32[]{:S(2)}) collective-permute-start(f32[2,6,10,8,128]{4,3,2,1,0:T(8,128)S(1)} %shard_map.73), channel_id=1, source_target_pairs={{0,1},{1,0},{2,3},{3,2},{4,5},{5,4},{6,7},{7,6},{8,9},{9,8},{10,11... | collective-permute-start | bytes 1474568 | tf_op jit(solution)/shard_map/ppermute | solution.py:448
  79.2 12.8 %collective-permute-start.21 = (f32[2,6,10,8,128]{4,3,2,1,0:T(8,128)S(1)}, f32[2,6,10,8,128]{4,3,2,1,0:T(8,128)S(1)}, u32[]{:S(2)}, u32[]{:S(2)}) collective-permute-start(f32[2,6,10,8,128]{4,3,2,1,0:T(8,128)S(1)} %shard_map.71), channel_id=1, source_target_pairs={{0,4},{1,5},{2,6},{3,7},{4,0},{5,1},{6,2},{7,3},{8,12},{9,13},{10,... | collective-permute-start | bytes 1474568 | tf_op jit(solution)/shard_map/ppermute | solution.py:448
  79.3 12.8 %collective-permute-start.18 = (f32[2,6,10,8,128]{4,3,2,1,0:T(8,128)S(1)}, f32[2,6,10,8,128]{4,3,2,1,0:T(8,128)S(1)}, u32[]{:S(2)}, u32[]{:S(2)}) collective-permute-start(f32[2,6,10,8,128]{4,3,2,1,0:T(8,128)S(1)} %collective-permute-done.17.refs_2_), channel_id=1, source_target_pairs={{0,3},{1,2},{2,1},{3,0},{4,7},{5,6},{6,5},{7,4},{8,11},{9,10},{10,... | collective-permute-start | bytes 1474568 | tf_op jit(solution)/shard_map/ppermute | solution.py:448
  79.4 13.5 %collective-permute-start.14 = (f32[2,6,10,8,128]{4,3,2,1,0:T(8,128)S(1)}, f32[2,6,10,8,128]{4,3,2,1,0:T(8,128)S(1)}, u32[]{:S(2)}, u32[]{:S(2)}) collective-permute-start(f32[2,6,10,8,128]{4,3,2,1,0:T(8,128)S(1)} %collective-permute-done.13.refs_0_), channel_id=1, source_target_pairs={{0,12},{1,13},{2,14},{3,15},{4,8},{5,9},{6,10},{7,11},{8,4},{9,5},... | collective-permute-start | bytes 1474568 | tf_op jit(solution)/shard_map/ppermute | solution.py:448
  87.7 7.2 %collective-permute-start.32 = (f32[384,384]{1,0:T(8,128)S(1)}, f32[384,384]{1,0:T(8,128)S(1)}, u32[]{:S(2)}, u32[]{:S(2)}) collective-permute-start(f32[384,384]{1,0:T(8,128)S(1)} %get-tuple-element.79.refs_0_), channel_id=1, source_target_pairs={{0,16},{16,0},{32,48},{48,32},{64,80},{80,64},{96,112},{112,96},{1... | collective-permute-start | bytes 1769480 | tf_op jit(solution)/shard_map/ppermute | solution.py:452
  89.5 7.2 %collective-permute-start.31 = (f32[384,384]{1,0:T(8,128)S(1)}, f32[384,384]{1,0:T(8,128)S(1)}, u32[]{:S(2)}, u32[]{:S(2)}) collective-permute-start(f32[384,384]{1,0:T(8,128)S(1)} %get-tuple-element.75.refs_0_), channel_id=1, source_target_pairs={{0,16},{16,0},{32,48},{48,32},{64,80},{80,64},{96,112},{112,96},{1... | collective-permute-start | bytes 1769480 | tf_op jit(solution)/shard_map/ppermute | solution.py:452
  92.0 6.6 %collective-permute-start.28 = (f32[384,384]{1,0:T(8,128)S(1)}, f32[384,384]{1,0:T(8,128)S(1)}, u32[]{:S(2)}, u32[]{:S(2)}) collective-permute-start(f32[384,384]{1,0:T(8,128)S(1)} %get-tuple-element.71.refs_0_), channel_id=1, source_target_pairs={{0,16},{16,0},{32,48},{48,32},{64,80},{80,64},{96,112},{112,96},{1... | collective-permute-start | bytes 1769480 | tf_op jit(solution)/shard_map/ppermute | solution.py:452
  94.8 5.7 %collective-permute-start.25 = (f32[384,384]{1,0:T(8,128)S(1)}, f32[384,384]{1,0:T(8,128)S(1)}, u32[]{:S(2)}, u32[]{:S(2)}) collective-permute-start(f32[384,384]{1,0:T(8,128)S(1)} %get-tuple-element.66.own), channel_id=1, source_target_pairs={{0,16},{16,0},{32,48},{48,32},{64,80},{80,64},{96,112},{112,96},{1... | collective-permute-start | bytes 1769480 | tf_op jit(solution)/shard_map/ppermute | solution.py:452
  101.6 10.3 %collective-permute-start.37 = (f32[480,128]{1,0:T(8,128)S(1)}, f32[480,128]{1,0:T(8,128)S(1)}, u32[]{:S(2)}, u32[]{:S(2)}) collective-permute-start(f32[480,128]{1,0:T(8,128)S(1)} %get-tuple-element.90), channel_id=1, source_target_pairs={{0,96},{16,112},{32,64},{48,80},{64,32},{80,48},{96,0},{112,16},{1... | collective-permute-start | bytes 737288 | tf_op jit(solution)/shard_map/ppermute | solution.py:452
  102.6 9.5 %collective-permute-start.34 = (f32[480,128]{1,0:T(8,128)S(1)}, f32[480,128]{1,0:T(8,128)S(1)}, u32[]{:S(2)}, u32[]{:S(2)}) collective-permute-start(f32[480,128]{1,0:T(8,128)S(1)} %get-tuple-element.87), channel_id=1, source_target_pairs={{0,32},{16,48},{32,0},{48,16},{64,96},{80,112},{96,64},{112,80},{1... | collective-permute-start | bytes 737288 | tf_op jit(solution)/shard_map/ppermute | solution.py:452
  104.3 12.3 %collective-permute-start.33 = (f32[480,128]{1,0:T(8,128)S(1)}, f32[480,128]{1,0:T(8,128)S(1)}, u32[]{:S(2)}, u32[]{:S(2)}) collective-permute-start(f32[480,128]{1,0:T(8,128)S(1)} %get-tuple-element.86), channel_id=1, source_target_pairs={{0,32},{16,48},{32,0},{48,16},{64,96},{80,112},{96,64},{112,80},{1... | collective-permute-start | bytes 737288 | tf_op jit(solution)/shard_map/ppermute | solution.py:452
  106.4 10.8 %collective-permute-start.36 = (f32[480,128]{1,0:T(8,128)S(1)}, f32[480,128]{1,0:T(8,128)S(1)}, u32[]{:S(2)}, u32[]{:S(2)}) collective-permute-start(f32[480,128]{1,0:T(8,128)S(1)} %get-tuple-element.89), channel_id=1, source_target_pairs={{0,96},{16,112},{32,64},{48,80},{64,32},{80,48},{96,0},{112,16},{1... | collective-permute-start | bytes 737288 | tf_op jit(solution)/shard_map/ppermute | solution.py:452
  112.0 9.2 %collective-permute-start.38 = (f32[480,128]{1,0:T(8,128)S(1)}, f32[480,128]{1,0:T(8,128)S(1)}, u32[]{:S(2)}, u32[]{:S(2)}) collective-permute-start(f32[480,128]{1,0:T(8,128)S(1)} %shard_map.82), channel_id=1, source_target_pairs={{0,32},{16,48},{32,0},{48,16},{64,96},{80,112},{96,64},{112,80},{1... | collective-permute-start | bytes 737288 | tf_op jit(solution)/shard_map/ppermute | solution.py:452
  112.1 9.9 %collective-permute-start.35 = (f32[480,128]{1,0:T(8,128)S(1)}, f32[480,128]{1,0:T(8,128)S(1)}, u32[]{:S(2)}, u32[]{:S(2)}) collective-permute-start(f32[480,128]{1,0:T(8,128)S(1)} %shard_map.81), channel_id=1, source_target_pairs={{0,96},{16,112},{32,64},{48,80},{64,32},{80,48},{96,0},{112,16},{1... | collective-permute-start | bytes 737288 | tf_op jit(solution)/shard_map/ppermute | solution.py:452
